TPU v7x, 32 devices: a whole 2x2x4 slice. The times are simulated.
32 devices in a mesh: dp: 32 (over z, y, x, core).
Axes of the slice: x: 2, y: 2, z: 4, core: 2. Of those that a mesh axis runs over, the one named last changes fastest.
Arguments:
- tokens: bfloat16 [16384, 384], P('dp'), may hold values from -6 to 6
- gain_attn: bfloat16 [384], P('dp'), may hold values from 0.5 to 1.5
- w_qkv: bfloat16 [384, 1152], P('dp'), may hold values from -0.3125 to 0.3125
- w_proj: bfloat16 [384, 384], P('dp'), may hold values from -0.875 to 0.875
- gain_moe: bfloat16 [384], P('dp'), may hold values from 0.5 to 1.5
- w_router: bfloat16 [384, 8], P('dp'), may hold values from -0.3125 to 0.3125
- w_in: bfloat16 [32, 384, 384], P('dp'), may hold values from -0.3125 to 0.3125
- w_out: bfloat16 [32, 384, 384], P('dp'), may hold values from -1.25 to 1.25
- cotangent: bfloat16 [16384, 384], P('dp'), may hold values from -6 to 6
- image_ids: int32 [16384], P('dp'), may hold values from 0 to 109, never falling along the last dimension, each value on 1 to 197 neighbouring positions
- expert_ids: int32 [16384, 2], P('dp'), may hold values from 0 to 7, as said below
- slots: int32 [16384, 2], P('dp'), may hold values from -1 to 159, as said below
Outputs:
- mixed: bfloat16 [16384, 384], P('dp')
- grad_tokens: bfloat16 [16384, 384], P('dp')
- grad_gain_attn: float32 [384], P('dp')
- grad_w_qkv: float32 [384, 1152], P('dp')
- grad_w_proj: float32 [384, 384], P('dp')
- grad_gain_moe: float32 [384], P('dp')
- grad_w_router: float32 [384, 8], P('dp')
- grad_w_in: float32 [32, 384, 384], P('dp')
- grad_w_out: float32 [32, 384, 384], P('dp')
Inputs may be any that keep to these rules, and one draw needn't show every extreme that they name: `image_ids`: image numbers never fall along the rows; an image has 1 to 197 rows, and some image has exactly 197. `expert_ids`: the two experts of a row differ. Within one device's 512 rows, the choices naming an expert take slots 0, 1, 2, ... in the order of all first choices by row, then all second choices by row; choices beyond 160 get -1; in every draw some expert gets all 160 slots from every device.
All inputs are finite; a program needn't handle non-finite values.
Results may differ from a plain program's by a relative error of at most 0.017.
Values may be sent and summed in bfloat16 or wider, within the bound.
No kernel may reach another device: no remote copies, remote signals or barrier semaphores. Data moves between devices by JAX's collectives and lax.ppermute only.
A program may use at most 128 MiB of HBM per device.

v0:
```python
import jax
import jax.numpy as jnp
from jax import lax
from jax.sharding import PartitionSpec as P

HEAD_DIM = 64
LEN = 197


EPSILON = 1e-06
MASKED = -1e30


def extended_2(block, sides, width):
    for axis, dim in sides:
        count = lax.axis_size(axis)
        forward = [(i, i + 1) for i in range(count - 1)]
        backward = [(target, source) for source, target in forward]
        low = lax.ppermute(
            lax.slice_in_dim(block, block.shape[dim] - width, None, axis=dim), axis, forward
        )
        high = lax.ppermute(lax.slice_in_dim(block, 0, width, axis=dim), axis, backward)
        block = jnp.concatenate([low, block, high], axis=dim)
    return block


def layer_norm(values, gain):
    centered = values - jnp.mean(values, axis=-1, keepdims=True)
    variance = jnp.mean(centered * centered, axis=-1, keepdims=True)
    return centered * lax.rsqrt(variance + EPSILON) * gain


def product(left, right):
    return jnp.dot(left, right, preferred_element_type=jnp.float32)


def left_transposed(left, right):
    return lax.dot_general(
        left, right, (((0,), (0,)), ((), ())), preferred_element_type=jnp.float32
    )


def right_transposed(left, right):
    return lax.dot_general(
        left, right, (((1,), (1,)), ((), ())), preferred_element_type=jnp.float32
    )


def pair_scores(query_part, key_part, same_image):
    scale = HEAD_DIM ** (-0.5)
    scores = (
        jnp.einsum("qhd,khd->hqk", query_part, key_part, preferred_element_type=jnp.float32) * scale
    )
    return jnp.where(same_image[None], scores, MASKED)


def per_device(
    tokens,
    gain_attn,
    w_qkv,
    w_proj,
    gain_moe,
    w_router,
    w_in,
    w_out,
    cotangent,
    image_ids,
    expert_ids,
    slots,
):
    devices = lax.axis_size("dp")
    experts_all = devices // 4
    row_count = tokens.shape[0]
    model_width = tokens.shape[1]
    capacity = max(2, 5 * row_count // (2 * experts_all))
    rim_width = LEN - 1
    pair_width = 2 * HEAD_DIM
    head_pairs = model_width // pair_width
    scale = HEAD_DIM ** (-0.5)
    weight_in = w_in[0]
    weight_out = w_out[0]
    gain_one, qkv_weight, proj_weight, gain_two, router_weight = (
        lax.all_gather(gain_attn, "dp", axis=0, tiled=True),
        lax.all_gather(w_qkv, "dp", axis=0, tiled=True),
        lax.all_gather(w_proj, "dp", axis=0, tiled=True),
        lax.all_gather(gain_moe, "dp", axis=0, tiled=True),
        lax.all_gather(w_router, "dp", axis=0, tiled=True),
    )
    gain_first = gain_one.astype(jnp.float32)
    gain_second = gain_two.astype(jnp.float32)
    inputs = tokens.astype(jnp.float32)
    normed_one = layer_norm(inputs, gain_first).astype(jnp.bfloat16)
    qkv = product(normed_one, qkv_weight).astype(jnp.bfloat16)
    queries = qkv[:, :model_width]
    extended = extended_2(qkv[:, model_width:], (("dp", 0),), rim_width)
    marks = extended_2(image_ids + 1, (("dp", 0),), rim_width)
    same_image = (image_ids + 1)[:, None] == marks[None, :]
    key_count = extended.shape[0]

    def head_parts(head_pair):
        start = head_pair * pair_width
        query_part = queries[:, start : start + pair_width].reshape(row_count, 2, HEAD_DIM)
        key_part = extended[:, start : start + pair_width].reshape(key_count, 2, HEAD_DIM)
        value_part = extended[:, model_width + start : model_width + start + pair_width].reshape(
            key_count, 2, HEAD_DIM
        )
        return (start, query_part, key_part, value_part)

    attended_parts = []
    totals = []
    for head_pair in range(head_pairs):
        start, query_part, key_part, value_part = head_parts(head_pair)
        masked = pair_scores(query_part, key_part, same_image)
        total = jax.nn.logsumexp(masked, axis=-1, keepdims=True)
        weights = jnp.exp(masked - total).astype(jnp.bfloat16)
        result = jnp.einsum("hqk,khd->qhd", weights, value_part, preferred_element_type=jnp.float32)
        attended_parts.append(result.reshape(row_count, pair_width))
        totals.append(total)
    attended = jnp.concatenate(attended_parts, axis=1).astype(jnp.bfloat16)
    middle = inputs + product(attended, proj_weight)
    normed_two = layer_norm(middle, gain_second).astype(jnp.bfloat16)
    logits = product(normed_two, router_weight)
    router_probs = jax.nn.softmax(logits, axis=-1)
    choice_table = (
        expert_ids[:, :, None] == jnp.arange(experts_all, dtype=jnp.int32)[None, None, :]
    ).astype(jnp.float32)
    gates = jnp.sum(router_probs[:, None, :] * choice_table, axis=-1)
    kept = slots >= 0
    buffer_rows = experts_all * capacity
    place = jnp.where(kept, expert_ids * capacity + slots, buffer_rows)
    safe_place = jnp.minimum(place, buffer_rows - 1)
    flat_place = place.reshape(-1)

    def spread(values):
        filled = (
            jnp.zeros((buffer_rows, model_width), jnp.bfloat16)
            .at[flat_place]
            .set(values.reshape(-1, model_width), mode="drop")
        )
        copies = jnp.broadcast_to(
            filled.reshape(experts_all, 1, capacity, model_width),
            (experts_all, 4, capacity, model_width),
        )
        return copies.reshape(devices, capacity, model_width)

    outgoing = spread(jnp.broadcast_to(normed_two[:, None, :], (row_count, 2, model_width)))
    arrived_rows = lax.all_to_all(outgoing, "dp", split_axis=0, concat_axis=0, tiled=True)
    pre_values = jnp.einsum(
        "scd,df->scf", arrived_rows, weight_in, preferred_element_type=jnp.float32
    )
    hidden = jax.nn.gelu(pre_values).astype(jnp.bfloat16)
    partial_out = jnp.einsum(
        "scf,fd->scd", hidden, weight_out, preferred_element_type=jnp.float32
    ).astype(jnp.bfloat16)
    returned_part = lax.all_to_all(partial_out, "dp", split_axis=0, concat_axis=0, tiled=True)
    expert_out = jnp.sum(
        returned_part.astype(jnp.float32).reshape(experts_all, 4, capacity, model_width), axis=1
    ).reshape(buffer_rows, model_width)
    picked = expert_out[safe_place]
    pair_gates = jnp.where(kept, gates, 0.0)
    mixed = middle + jnp.sum(picked * pair_gates[:, :, None], axis=1)
    gain_one, qkv_weight, proj_weight, gain_two, router_weight = (
        lax.all_gather(gain_attn, "dp", axis=0, tiled=True),
        lax.all_gather(w_qkv, "dp", axis=0, tiled=True),
        lax.all_gather(w_proj, "dp", axis=0, tiled=True),
        lax.all_gather(gain_moe, "dp", axis=0, tiled=True),
        lax.all_gather(w_router, "dp", axis=0, tiled=True),
    )
    gain_first = gain_one.astype(jnp.float32)
    gain_second = gain_two.astype(jnp.float32)
    upstream = cotangent.astype(jnp.float32)
    gate_grad = jnp.where(kept, jnp.sum(picked * upstream[:, None, :], axis=-1), 0.0)
    out_grad = spread((pair_gates[:, :, None] * upstream[:, None, :]).astype(jnp.bfloat16))
    grad_arrived, rows_arrived = (
        lax.all_to_all(out_grad, "dp", split_axis=0, concat_axis=0, tiled=True),
        lax.all_to_all(outgoing, "dp", split_axis=0, concat_axis=0, tiled=True),
    )
    pre_values = jnp.einsum(
        "scd,df->scf", rows_arrived, weight_in, preferred_element_type=jnp.float32
    )
    hidden_values, gelu_back = jax.vjp(jax.nn.gelu, pre_values)
    hidden_low = hidden_values.astype(jnp.bfloat16)
    grad_weight_out = jnp.einsum(
        "scf,scd->fd", hidden_low, grad_arrived, preferred_element_type=jnp.float32
    )
    hidden_grad = jnp.einsum(
        "scd,fd->scf", grad_arrived, weight_out, preferred_element_type=jnp.float32
    )
    pre_grad = gelu_back(hidden_grad)[0].astype(jnp.bfloat16)
    grad_weight_in = jnp.einsum(
        "scd,scf->df", rows_arrived, pre_grad, preferred_element_type=jnp.float32
    )
    row_grad = jnp.einsum("scf,df->scd", pre_grad, weight_in, preferred_element_type=jnp.float32)
    row_back = lax.all_to_all(
        row_grad.astype(jnp.bfloat16), "dp", split_axis=0, concat_axis=0, tiled=True
    ).astype(row_grad.dtype)
    expert_grad = jnp.sum(row_back.reshape(experts_all, 4, capacity, model_width), axis=1).reshape(
        buffer_rows, model_width
    )
    normed_grad = jnp.sum(expert_grad[safe_place] * kept[:, :, None].astype(jnp.float32), axis=1)
    probs_grad = jnp.sum(gate_grad[:, :, None] * choice_table, axis=1)
    logits_grad = (
        router_probs * (probs_grad - jnp.sum(router_probs * probs_grad, axis=-1, keepdims=True))
    ).astype(jnp.bfloat16)
    grad_router = left_transposed(normed_two, logits_grad)
    normed_grad = normed_grad + right_transposed(logits_grad, router_weight)
    renormed_two, second_back = jax.vjp(layer_norm, middle, gain_second)
    middle_part, gain_two_grad = second_back(normed_grad)
    middle_grad = upstream + middle_part
    branch_grad = middle_grad.astype(jnp.bfloat16)
    grad_proj = left_transposed(attended, branch_grad)
    attended_grad = right_transposed(branch_grad, proj_weight).astype(jnp.bfloat16)
    query_grads = []
    key_grads = []
    value_grads = []
    for head_pair in range(head_pairs):
        start, query_part, key_part, value_part = head_parts(head_pair)
        masked = pair_scores(query_part, key_part, same_image)
        probs = jnp.exp(masked - totals[head_pair])
        weights = probs.astype(jnp.bfloat16)
        grad_part = attended_grad[:, start : start + pair_width].reshape(row_count, 2, HEAD_DIM)
        value_grads.append(
            jnp.einsum(
                "hqk,qhd->khd", weights, grad_part, preferred_element_type=jnp.float32
            ).reshape(key_count, pair_width)
        )
        weight_grad = jnp.einsum(
            "qhd,khd->hqk", grad_part, value_part, preferred_element_type=jnp.float32
        )
        score_grad = (
            probs * (weight_grad - jnp.sum(probs * weight_grad, axis=-1, keepdims=True))
        ).astype(jnp.bfloat16)
        query_grads.append(
            (
                jnp.einsum("hqk,khd->qhd", score_grad, key_part, preferred_element_type=jnp.float32)
                * scale
            ).reshape(row_count, pair_width)
        )
        key_grads.append(
            (
                jnp.einsum(
                    "hqk,qhd->khd", score_grad, query_part, preferred_element_type=jnp.float32
                )
                * scale
            ).reshape(key_count, pair_width)
        )
    pair_grad = jnp.concatenate(key_grads + value_grads, axis=1)
    outer_rims = jnp.concatenate(
        [pair_grad[:rim_width], pair_grad[key_count - rim_width :]], axis=0
    )
    incoming = extended_2(outer_rims.astype(jnp.bfloat16), (("dp", 0),), rim_width).astype(
        outer_rims.dtype
    )
    inner = pair_grad[rim_width : rim_width + row_count]
    inner = inner.at[:rim_width].add(incoming[:rim_width])
    inner = inner.at[row_count - rim_width :].add(incoming[3 * rim_width :])
    qkv_grad = jnp.concatenate([jnp.concatenate(query_grads, axis=1), inner], axis=1).astype(
        jnp.bfloat16
    )
    grad_qkv = left_transposed(normed_one, qkv_grad)
    normed_one_grad = right_transposed(qkv_grad, qkv_weight)
    renormed_one, first_back = jax.vjp(layer_norm, inputs, gain_first)
    input_part, gain_one_grad = first_back(normed_one_grad)
    grad_tokens = (middle_grad + input_part).astype(jnp.bfloat16)
    owned = (
        lax.psum_scatter(gain_one_grad, "dp", scatter_dimension=0, tiled=True),
        lax.psum_scatter(grad_qkv, "dp", scatter_dimension=0, tiled=True),
        lax.psum_scatter(grad_proj, "dp", scatter_dimension=0, tiled=True),
        lax.psum_scatter(gain_two_grad, "dp", scatter_dimension=0, tiled=True),
        lax.psum_scatter(grad_router, "dp", scatter_dimension=0, tiled=True),
    )
    return (
        mixed.astype(jnp.bfloat16),
        grad_tokens,
        owned[0],
        owned[1],
        owned[2],
        owned[3],
        owned[4],
        grad_weight_in[None],
        grad_weight_out[None],
    )


def solution(mesh):
    in_specs = (
        P("dp", None),
        P("dp"),
        P("dp", None),
        P("dp", None),
        P("dp"),
        P("dp", None),
        P("dp", None, None),
        P("dp", None, None),
        P("dp", None),
        P("dp"),
        P("dp", None),
        P("dp", None),
    )
    out_specs = (
        P("dp", None),
        P("dp", None),
        P("dp"),
        P("dp", None),
        P("dp", None),
        P("dp"),
        P("dp", None),
        P("dp", None, None),
        P("dp", None, None),
    )
    return jax.shard_map(
        per_device, mesh=mesh, in_specs=in_specs, out_specs=out_specs, check_vma=False
    )
```

profile of v0, /device:TPU:0, one launch (start us, length us, event | category | flops | bytes accessed | tf_op | source)
XLA Modules:
  0.0 853.8 jit_solution(8464754447912741535)
XLA Ops:
  1.5 2.3 collective-permute-start.2
  6.8 44.7 %all-reduce.10 = (bf16[384]{0:T(512)(128)(2,1)S(1)}, bf16[384]{0:T(512)(128)(2,1)S(1)}) all-reduce(bf16[384]{0:T(512)(128)(2,1)S(1)} %dynamic-update-slice.6, bf16[384]{0:T(512)(128)(2,1)S(1)} %dynamic-update-slice.7), channel_id=1, replica_groups=mesh['dp'=32] {'dp'}, use_global_device_ids=true, to_apply=%add | all-reduce | flops 768 | bytes 3072
  52.9 43.9 %all-gather = bf16[32,12,1152]{2,1,0:T(8,128)(2,1)S(1)} all-gather(bf16[1,12,1152]{2,1,0:T(8,128)(2,1)} %bitcast.178), channel_id=1, replica_groups=mesh['dp'=32] {'dp'}, dimensions={0}, use_global_device_ids=true | all-gather | bytes 912384 | tf_op jit(solution)/shard_map/all_gather | solution.py:84
  98.9 3.0 collective-permute-start
  104.3 39.0 %all-gather.1 = bf16[32,12,384]{2,1,0:T(8,128)(2,1)S(1)} all-gather(bf16[1,12,384]{2,1,0:T(8,128)(2,1)S(1)} %bitcast.179), channel_id=1, replica_groups=mesh['dp'=32] {'dp'}, dimensions={0}, use_global_device_ids=true | all-gather | bytes 304128 | tf_op jit(solution)/shard_map/all_gather | solution.py:85
  158.2 2.4 exponential_reduce_fusion.2
  167.7 6.0 scatter_custom_fusion
  173.7 3.4 broadcast_in_dim.70
  177.1 3.7 all-to-all-start
  180.8 99.8 %all-gather.2 = bf16[32,12,8]{1,2,0:T(8,128)(2,1)S(1)} all-gather(bf16[1,12,8]{1,2,0:T(8,128)(2,1)S(1)} %bitcast.182), channel_id=1, replica_groups=mesh['dp'=32] {'dp'}, dimensions={0}, use_global_device_ids=true | all-gather | bytes 6336 | tf_op jit(solution)/shard_map/all_gather | solution.py:87
  282.9 3.2 mul.324
  287.4 6.3 scatter_custom_fusion.1
  293.7 2.3 broadcast_in_dim.135
  296.0 16.7 %all-to-all-start.2 = ((bf16[32,160,384]{2,1,0:T(8,128)(2,1)}), bf16[32,160,384]{2,1,0:T(8,128)(2,1)}, u32[]{:S(2)}, u32[]{:S(2)}) async-start(bf16[32,160,384]{2,1,0:T(8,128)(2,1)} %bitcast.139), calls=%async_computation.2 | async-start | bytes 7864320 | tf_op jit(solution)/shard_map/all_to_all | solution.py:175
  312.8 7.8 fusion.37
  320.5 80.5 %all-to-all-done.2 = bf16[32,160,384]{2,1,0:T(8,128)(2,1)} async-done(((bf16[32,160,384]{2,1,0:T(8,128)(2,1)}), bf16[32,160,384]{2,1,0:T(8,128)(2,1)}, u32[]{:S(2)}, u32[]{:S(2)}) %all-to-all-start.2) | async-done | bytes 3932192 | tf_op jit(solution)/shard_map/all_to_all | solution.py:175
  401.0 10.2 %fusion.8 = bf16[32,160,384]{2,1,0:T(8,128)(2,1)S(1)} fusion(f32[32,160,384]{2,1,0:T(8,128)} %fusion.37, bf16[32,160,384]{2,1,0:T(8,128)(2,1)} %all-to-all-done.2, bf16[1,384,384]{2,1,0:T(8,128)(2,1)S(1)} %copy-done.55), kind=kOutput, calls=%fused_computation.12 | convolution fusion | flops 1549271040 | bytes 16023552 | tf_op jit(solution)/shard_map/scd,fd->scf/dot_general | solution.py:186
  413.2 4.1 convolution_convert_fusion.1
  417.2 4.1 all-to-all-start.3
  421.3 8.3 convolution_convert_fusion.2
  429.6 79.9 %all-to-all-done.3 = bf16[32,160,384]{2,1,0:T(8,128)(2,1)} async-done(((bf16[32,160,384]{2,1,0:T(8,128)(2,1)}), bf16[32,160,384]{2,1,0:T(8,128)(2,1)}, u32[]{:S(2)}, u32[]{:S(2)}) %all-to-all-start.3) | async-done | bytes 3932192 | tf_op jit(solution)/shard_map/all_to_all | solution.py:194
  509.6 4.3 all-to-all-start.1
  514.4 6.3 convolution_bitcast_fusion.1
  520.7 8.1 convolution_bitcast_fusion
  528.8 2.9 convert_reduce_fusion
  531.7 4.8 gather_fusion.1
  538.7 4.0 multiply_reduce_fusion.4
  542.8 2.3 copy.119
  545.0 57.1 %all-to-all-done.1 = bf16[32,160,384]{2,1,0:T(8,128)(2,1)} async-done(((bf16[32,160,384]{2,1,0:T(8,128)(2,1)}), bf16[32,160,384]{2,1,0:T(8,128)(2,1)}, u32[]{:S(2)}, u32[]{:S(2)}) %all-to-all-start.1) | async-done | bytes 3932192 | tf_op jit(solution)/shard_map/all_to_all | solution.py:155
  602.1 2.9 convert_reduce_fusion.1
  605.0 4.8 gather_fusion
  612.0 6.1 multiply_reduce_fusion.3
  618.4 2.5 multiply_reduce_fusion.6
  620.8 2.4 copy.113
  623.2 2.5 fusion.64
  634.9 4.5 multiply_reduce_fusion
  639.4 5.1 multiply_convert_fusion.1
  661.7 4.7 scatter-add.6
  668.1 4.5 scatter-add.9
  678.0 82.9 %fusion.63 = (f32[16,1152]{1,0:T(8,128)S(1)}, f32[16,384]{1,0:T(8,128)S(1)}) fusion(f32[384,1152]{1,0:T(8,128)} %fusion.39, f32[384,384]{1,0:T(8,128)} %fusion.41), kind=kCustom, calls=%all-reduce-scatter.2 | all-reduce-scatter fusion | flops 786433 | bytes 2457600
  766.1 2.6 collective-permute-start.21
  771.9 45.5 %all-reduce.9 = (f32[384]{0:T(512)S(1)}, f32[384]{0:T(512)S(1)}, f32[384,8]{0,1:T(8,128)S(1)}) all-reduce(f32[384]{0:T(512)S(1)} %get-tuple-element.73, f32[384]{0:T(512)S(1)} %get-tuple-element.69, f32[384,8]{0,1:T(8,128)S(1)} %fusion.76), channel_id=2, replica_groups=mesh['dp'=32] {'dp'}, use_global_device_ids=true, to_apply=%region_30.31.clone | all-reduce | flops 3840 | bytes 30720
  817.4 4.2 collective-permute-start.15
  822.9 6.3 collective-permute-start.12
  831.1 2.7 collective-permute-start.13
  838.2 3.3 collective-permute-start.9
  842.6 3.4 collective-permute-start.8
  846.0 3.4 collective-permute-start.7
  (286 shorter events, 95.6 us)
Async XLA Ops:
  0.6 312.1 %copy-start = (bf16[1,384,384]{2,1,0:T(8,128)(2,1)S(1)}, bf16[1,384,384]{2,1,0:T(8,128)(2,1)}, u32[]{:S(2)}) copy-start(bf16[1,384,384]{2,1,0:T(8,128)(2,1)} %param.22) | copy-start | bytes 884740
  1.5 146.8 %collective-permute-start.2 = (s32[196]{0:T(256)S(1)}, s32[196]{0:T(256)S(1)}, u32[]{:S(2)}, u32[]{:S(2)}) collective-permute-start(s32[196]{0:T(256)S(1)} %get-tuple-element.116), channel_id=1, source_target_pairs={{0,1},{1,2},{2,3},{3,4},{4,5},{5,6},{6,7},{7,8},{8,9},{9,10},{10,1... | collective-permute-start | bytes 2360 | tf_op jit(solution)/shard_map/ppermute | solution.py:19
  3.8 144.5 %collective-permute-start.3 = (s32[196]{0:T(256)S(1)}, s32[196]{0:T(256)S(1)}, u32[]{:S(2)}, u32[]{:S(2)}) collective-permute-start(s32[196]{0:T(256)S(1)} %get-tuple-element.117), channel_id=1, source_target_pairs={{1,0},{2,1},{3,2},{4,3},{5,4},{6,5},{7,6},{8,7},{9,8},{10,9},{11,1... | collective-permute-start | bytes 2360 | tf_op jit(solution)/shard_map/ppermute | solution.py:22
  96.8 7.1 copy-start.51
  96.8 7.1 copy-start.52
  96.8 7.5 copy-start.53
  98.9 49.8 %collective-permute-start = (bf16[196,768]{1,0:T(8,128)(2,1)}, bf16[196,768]{1,0:T(8,128)(2,1)}, u32[]{:S(2)}, u32[]{:S(2)}) collective-permute-start(bf16[196,768]{1,0:T(8,128)(2,1)} %get-tuple-element.107), channel_id=1, source_target_pairs={{0,1},{1,2},{2,3},{3,4},{4,5},{5,6},{6,7},{7,8},{8,9},{9,10},{10,1... | collective-permute-start | bytes 903176 | tf_op jit(solution)/shard_map/ppermute | solution.py:19
  101.8 46.9 %collective-permute-start.1 = (bf16[196,768]{1,0:T(8,128)(2,1)}, bf16[196,768]{1,0:T(8,128)(2,1)}, u32[]{:S(2)}, u32[]{:S(2)}) collective-permute-start(bf16[196,768]{1,0:T(8,128)(2,1)} %get-tuple-element.108), channel_id=1, source_target_pairs={{1,0},{2,1},{3,2},{4,3},{5,4},{6,5},{7,6},{8,7},{9,8},{10,9},{11,1... | collective-permute-start | bytes 903176 | tf_op jit(solution)/shard_map/ppermute | solution.py:22
  103.9 43.6 %copy-start.45 = (bf16[512,128]{1,0:T(8,128)(2,1)S(1)}, bf16[512,128]{1,0:T(8,128)(2,1)}, u32[]{:S(2)}) copy-start(bf16[512,128]{1,0:T(8,128)(2,1)} %get-tuple-element.106) | copy-start | bytes 393220
  148.7 16.0 %copy-start.10 = (pred[512,904]{0,1:T(8,128)(4,1)}, pred[512,904]{0,1:T(8,128)(4,1)S(1)}, u32[]{:S(2)}) copy-start(pred[512,904]{0,1:T(8,128)(4,1)S(1)} %broadcast_compare_fusion) | copy-start | bytes 1388548
  152.3 12.4 %copy-start.35 = (bf16[904,128]{0,1:T(8,128)(2,1)}, bf16[904,128]{0,1:T(8,128)(2,1)S(1)}, u32[]{:S(2)}) copy-start(bf16[904,128]{0,1:T(8,128)(2,1)S(1)} %copy.99) | copy-start | bytes 694276
  154.8 7.5 copy-start.29
  155.2 8.3 copy-start.37
  157.4 7.3 copy-start.7
  166.7 119.3 %copy-start.16 = (bf16[512,384]{0,1:T(8,128)(2,1)}, bf16[512,384]{0,1:T(8,128)(2,1)S(1)}, u32[]{:S(2)}) copy-start(bf16[512,384]{0,1:T(8,128)(2,1)S(1)} %multiply_convert_fusion.6) | copy-start | bytes 1179652
  177.1 103.6 %copy-start.46 = (bf16[512,384]{1,0:T(8,128)(2,1)S(1)}, bf16[512,384]{1,0:T(8,128)(2,1)}, u32[]{:S(2)}) copy-start(bf16[512,384]{1,0:T(8,128)(2,1)} %param.24) | copy-start | bytes 1179652
  177.1 116.6 %all-to-all-start = ((bf16[32,160,384]{2,1,0:T(8,128)(2,1)}), bf16[32,160,384]{2,1,0:T(8,128)(2,1)}, u32[]{:S(2)}, u32[]{:S(2)}) async-start(bf16[32,160,384]{2,1,0:T(8,128)(2,1)} %bitcast.138), calls=%async_computation | async-start | bytes 7864320 | tf_op jit(solution)/shard_map/all_to_all | solution.py:147
  281.2 12.5 %copy-start.13 = (f32[512,384]{1,0:T(8,128)}, f32[512,384]{1,0:T(8,128)S(1)}, u32[]{:S(2)}) copy-start(f32[512,384]{1,0:T(8,128)S(1)} %copy.116) | copy-start | bytes 2359300
  296.0 105.0 %all-to-all-start.2 = ((bf16[32,160,384]{2,1,0:T(8,128)(2,1)}), bf16[32,160,384]{2,1,0:T(8,128)(2,1)}, u32[]{:S(2)}, u32[]{:S(2)}) async-start(bf16[32,160,384]{2,1,0:T(8,128)(2,1)} %bitcast.139), calls=%async_computation.2 | async-start | bytes 7864320 | tf_op jit(solution)/shard_map/all_to_all | solution.py:175
  312.8 88.3 %copy-start.55 = (bf16[1,384,384]{2,1,0:T(8,128)(2,1)S(1)}, bf16[1,384,384]{2,1,0:T(8,128)(2,1)}, u32[]{:S(2)}) copy-start(bf16[1,384,384]{2,1,0:T(8,128)(2,1)} %param.23) | copy-start | bytes 884740
  417.2 92.3 %all-to-all-start.3 = ((bf16[32,160,384]{2,1,0:T(8,128)(2,1)}), bf16[32,160,384]{2,1,0:T(8,128)(2,1)}, u32[]{:S(2)}, u32[]{:S(2)}) async-start(bf16[32,160,384]{2,1,0:T(8,128)(2,1)} %convolution_convert_fusion.1), calls=%async_computation.3 | async-start | bytes 7864320 | tf_op jit(solution)/shard_map/all_to_all | solution.py:194
  509.6 92.5 %all-to-all-start.1 = ((bf16[32,160,384]{2,1,0:T(8,128)(2,1)}), bf16[32,160,384]{2,1,0:T(8,128)(2,1)}, u32[]{:S(2)}, u32[]{:S(2)}) async-start(bf16[32,160,384]{2,1,0:T(8,128)(2,1)} %convolution_convert_fusion.2), calls=%async_computation.1 | async-start | bytes 7864320 | tf_op jit(solution)/shard_map/all_to_all | solution.py:155
  618.3 7.4 copy-start.19
  650.5 8.3 copy-start.24
  651.5 8.5 collective-permute-start.4
  653.8 6.2 collective-permute-start.5
  666.5 7.7 copy-start.47
  666.5 7.7 copy-start.48
  666.5 7.7 copy-start.49
  676.1 95.5 %copy-start.15 = (f32[512,384]{0,1:T(8,128)S(1)}, f32[512,384]{0,1:T(8,128)}, u32[]{:S(2)}) copy-start(f32[512,384]{0,1:T(8,128)} %copy-done.14) | copy-start | bytes 2359300
  676.1 95.5 %copy-start.20 = (bf16[512,384]{0,1:T(8,128)(2,1)S(1)}, bf16[512,384]{0,1:T(8,128)(2,1)}, u32[]{:S(2)}) copy-start(bf16[512,384]{0,1:T(8,128)(2,1)} %copy-done.18) | copy-start | bytes 1179652
  678.0 175.3 %copy-start.1 = (bf16[1,384,384]{2,1,0:T(8,128)(2,1)S(1)}, bf16[1,384,384]{2,1,0:T(8,128)(2,1)}, u32[]{:S(2)}) copy-start(bf16[1,384,384]{2,1,0:T(8,128)(2,1)} %param.22) | copy-start | bytes 884740
  760.9 56.5 %collective-permute-start.20 = (f32[16,384]{1,0:T(8,128)S(1)}, f32[16,384]{1,0:T(8,128)S(1)}, u32[]{:S(2)}, u32[]{:S(2)}) collective-permute-start(f32[16,384]{1,0:T(8,128)S(1)} %get-tuple-element.91), channel_id=1, source_target_pairs={{0,7},{1,8},{2,9},{3,10},{4,11},{5,12},{6,13},{7,14},{8,15},{9,16}... | collective-permute-start | bytes 73736
  762.2 59.4 %collective-permute-start.19 = (f32[16,384]{1,0:T(8,128)S(1)}, f32[16,384]{1,0:T(8,128)S(1)}, u32[]{:S(2)}, u32[]{:S(2)}) collective-permute-start(f32[16,384]{1,0:T(8,128)S(1)} %get-tuple-element.91), channel_id=1, source_target_pairs={{0,6},{1,7},{2,8},{3,9},{4,10},{5,11},{6,12},{7,13},{8,14},{9,15},... | collective-permute-start | bytes 73736
  763.5 59.4 %collective-permute-start.18 = (f32[16,384]{1,0:T(8,128)S(1)}, f32[16,384]{1,0:T(8,128)S(1)}, u32[]{:S(2)}, u32[]{:S(2)}) collective-permute-start(f32[16,384]{1,0:T(8,128)S(1)} %get-tuple-element.91), channel_id=1, source_target_pairs={{0,5},{1,6},{2,7},{3,8},{4,9},{5,10},{6,11},{7,12},{8,13},{9,14},{... | collective-permute-start | bytes 73736
  764.8 64.5 %collective-permute-start.17 = (f32[16,384]{1,0:T(8,128)S(1)}, f32[16,384]{1,0:T(8,128)S(1)}, u32[]{:S(2)}, u32[]{:S(2)}) collective-permute-start(f32[16,384]{1,0:T(8,128)S(1)} %get-tuple-element.91), channel_id=1, source_target_pairs={{0,4},{1,5},{2,6},{3,7},{4,8},{5,9},{6,10},{7,11},{8,12},{9,13},{1... | collective-permute-start | bytes 73736
  766.1 4.1 collective-permute-start.21
  770.2 60.8 %collective-permute-start.16 = (f32[16,384]{1,0:T(8,128)S(1)}, f32[16,384]{1,0:T(8,128)S(1)}, u32[]{:S(2)}, u32[]{:S(2)}) collective-permute-start(f32[16,384]{1,0:T(8,128)S(1)} %get-tuple-element.91), channel_id=1, source_target_pairs={{0,3},{1,4},{2,5},{3,6},{4,7},{5,8},{6,9},{7,10},{8,11},{9,12},{10... | collective-permute-start | bytes 73736
  817.4 19.1 %collective-permute-start.15 = (f32[16,384]{1,0:T(8,128)S(1)}, f32[16,384]{1,0:T(8,128)S(1)}, u32[]{:S(2)}, u32[]{:S(2)}) collective-permute-start(f32[16,384]{1,0:T(8,128)S(1)} %get-tuple-element.91), channel_id=1, source_target_pairs={{0,2},{1,3},{2,4},{3,5},{4,6},{5,7},{6,8},{7,9},{8,10},{9,11},{10,... | collective-permute-start | bytes 73736
  821.6 16.6 %collective-permute-start.14 = (f32[16,384]{1,0:T(8,128)S(1)}, f32[16,384]{1,0:T(8,128)S(1)}, u32[]{:S(2)}, u32[]{:S(2)}) collective-permute-start(f32[16,384]{1,0:T(8,128)S(1)} %get-tuple-element.91), channel_id=1, source_target_pairs={{0,1},{1,2},{2,3},{3,4},{4,5},{5,6},{6,7},{7,8},{8,9},{9,10},{10,1... | collective-permute-start | bytes 73736
  822.9 23.1 %collective-permute-start.12 = (f32[16,1152]{1,0:T(8,128)S(1)}, f32[16,1152]{1,0:T(8,128)S(1)}, u32[]{:S(2)}, u32[]{:S(2)}) collective-permute-start(f32[16,1152]{1,0:T(8,128)S(1)} %get-tuple-element.90), channel_id=1, source_target_pairs={{0,7},{1,8},{2,9},{3,10},{4,11},{5,12},{6,13},{7,14},{8,15},{9,16}... | collective-permute-start | bytes 221192
  829.3 20.1 %collective-permute-start.11 = (f32[16,1152]{1,0:T(8,128)S(1)}, f32[16,1152]{1,0:T(8,128)S(1)}, u32[]{:S(2)}, u32[]{:S(2)}) collective-permute-start(f32[16,1152]{1,0:T(8,128)S(1)} %get-tuple-element.90), channel_id=1, source_target_pairs={{0,6},{1,7},{2,8},{3,9},{4,10},{5,11},{6,12},{7,13},{8,14},{9,15},... | collective-permute-start | bytes 221192
  831.1 11.5 %collective-permute-start.13 = (f32[12,1152]{1,0:T(8,128)S(1)}, f32[12,1152]{1,0:T(8,128)S(1)}, u32[]{:S(2)}, u32[]{:S(2)}) collective-permute-start(f32[12,1152]{1,0:T(8,128)S(1)} %slice.172), channel_id=1, source_target_pairs={{0,8},{1,9},{2,10},{3,11},{4,12},{5,13},{6,14},{7,15},{8,16},{9,17... | collective-permute-start | bytes 165896
  836.6 14.8 %collective-permute-start.10 = (f32[16,1152]{1,0:T(8,128)S(1)}, f32[16,1152]{1,0:T(8,128)S(1)}, u32[]{:S(2)}, u32[]{:S(2)}) collective-permute-start(f32[16,1152]{1,0:T(8,128)S(1)} %get-tuple-element.90), channel_id=1, source_target_pairs={{0,5},{1,6},{2,7},{3,8},{4,9},{5,10},{6,11},{7,12},{8,13},{9,14},{... | collective-permute-start | bytes 221192
  838.2 13.1 %collective-permute-start.9 = (f32[16,1152]{1,0:T(8,128)S(1)}, f32[16,1152]{1,0:T(8,128)S(1)}, u32[]{:S(2)}, u32[]{:S(2)}) collective-permute-start(f32[16,1152]{1,0:T(8,128)S(1)} %get-tuple-element.90), channel_id=1, source_target_pairs={{0,4},{1,5},{2,6},{3,7},{4,8},{5,9},{6,10},{7,11},{8,12},{9,13},{1... | collective-permute-start | bytes 221192
  842.6 8.8 %collective-permute-start.8 = (f32[16,1152]{1,0:T(8,128)S(1)}, f32[16,1152]{1,0:T(8,128)S(1)}, u32[]{:S(2)}, u32[]{:S(2)}) collective-permute-start(f32[16,1152]{1,0:T(8,128)S(1)} %get-tuple-element.90), channel_id=1, source_target_pairs={{0,3},{1,4},{2,5},{3,6},{4,7},{5,8},{6,9},{7,10},{8,11},{9,12},{10... | collective-permute-start | bytes 221192
  846.0 5.3 collective-permute-start.7
  849.4 2.2 collective-permute-start.6
  (40 other events, 134.8 us)
where the time goes:
time: 863 us; the launch traced here: 854 us
  blocking collectives  356 us (41%)
  waiting for transfers between devices  219 us (25%)
  matrix products  81 us (9%)
  starting transfers between devices  78.6 us (9%)
  local copies, waits for them, and re-layouts  76.1 us (9%)
  other arithmetic  40.7 us (5%)
    unnamed x3, blocking collectives  173 us
    all_gather x1, blocking collectives, per_device(): lax.all_gather(w_router, 'dp', axis=0, tiled=True)  99.8 us
    all_to_all x1, waiting for transfers between devices, per_device(): lax.all_to_all(out_grad, 'dp', split_axis=0, concat_axis=0, tiled=True)  80.5 us
    all_to_all x1, waiting for transfers between devices, per_device(): lax.all_to_all(row_grad.astype(jnp.bfloat16), 'dp', split_axis=0, concat_...  79.9 us
    all_to_all x1, waiting for transfers between devices, per_device(): lax.all_to_all(partial_out, 'dp', split_axis=0, concat_axis=0, tiled=True)  57.1 us
    all_gather x1, blocking collectives, per_device(): lax.all_gather(w_qkv, 'dp', axis=0, tiled=True)  43.9 us
    all_gather x1, blocking collectives, per_device(): lax.all_gather(w_proj, 'dp', axis=0, tiled=True)  39 us
    unnamed x16, starting transfers between devices  38.4 us
  transfers between devices with their start and end apart: 26, of which 5 were waited for; matrix products, arithmetic and copies ran while one was open for 9% of the time, Pallas kernels for 0%

commit v1 on v0

v1 whole, which is shorter than its diff:
```python
import functools

import jax
import jax.numpy as jnp
import numpy as np
from jax import lax
from jax.experimental import pallas as pl
from jax.experimental.pallas import tpu as pltpu
from jax.sharding import PartitionSpec as P

HEAD_DIM = 64
LEN = 197
EPSILON = 1e-06
MASKED = -1e30
HALO = 256
BLOCK = 128
WINDOW = BLOCK + 2 * HALO
LANES = 128
SCALE = HEAD_DIM ** (-0.5)
BF = jnp.bfloat16
F32 = jnp.float32
GELU_C = (2.0 / np.pi) ** 0.5
GELU_A = 0.044715


def dot(left, right, left_dim=1, right_dim=0):
    return lax.dot_general(
        left,
        right,
        (((left_dim,), (right_dim,)), ((), ())),
        preferred_element_type=F32,
    )


def call(body, outs, ins, scratch=(), flops=0, name=None, vmem_mib=12, fetch=False):
    vmem = pl.BlockSpec(memory_space=pltpu.VMEM)
    spec = pl.BlockSpec(memory_space=pl.ANY) if fetch else vmem
    return pl.pallas_call(
        body,
        out_shape=tuple(outs),
        in_specs=[spec] * len(ins),
        out_specs=tuple([vmem] * len(outs)),
        scratch_shapes=list(scratch),
        compiler_params=pltpu.CompilerParams(vmem_limit_bytes=vmem_mib * 1024 * 1024),
        cost_estimate=pl.CostEstimate(flops=int(flops), bytes_accessed=1024, transcendentals=0),
        name=name,
    )(*ins)


def shape(dims, dtype):
    return jax.ShapeDtypeStruct(dims, dtype)


def lane_iota(rows, lanes=LANES):
    return lax.broadcasted_iota(jnp.int32, (rows, lanes), 1)


def fetched(refs, held, sems):
    copies = [
        pltpu.make_async_copy(ref, into, sems.at[index])
        for index, (ref, into) in enumerate(zip(refs, held))
    ]
    for copy in copies:
        copy.start()
    for copy in copies:
        copy.wait()


def pack_body(experts, *refs):
    out, held, sems = refs[5], refs[6:11], refs[11]
    fetched(refs[:5], held, sems)
    w_qkv, w_proj, router_turned, gain_attn, gain_moe = held
    share, cols = w_qkv.shape
    width = cols // 3
    out[:, :cols] = w_qkv[...]
    out[:, cols : 4 * width] = w_proj[...]
    lanes = lane_iota(share)
    diagonal = lax.broadcasted_iota(jnp.int32, (share, share), 0) == lane_iota(share, share)
    pick = lax.broadcasted_iota(jnp.int32, (experts, LANES), 0) == lane_iota(experts)
    tail = dot(router_turned[...], pick.astype(F32).astype(BF), 0, 0)
    for index, gain in enumerate((gain_attn, gain_moe)):
        column = jnp.sum(
            jnp.where(diagonal, gain[...].astype(F32), 0.0), axis=1, keepdims=True
        )
        tail = jnp.where(lanes == experts + index, column, tail)
    out[:, 4 * width :] = tail.astype(BF)


def front_body(width, tokens_ref, ids_ref, own, low, high, tokens, ids, sems):
    fetched((tokens_ref, ids_ref), (tokens, ids), sems)
    rows = tokens.shape[0]
    own[:, :width] = tokens[...]
    for index in range(rows // BLOCK):
        line = (ids[index : index + 1, :] + 1).astype(F32)
        column = jnp.broadcast_to(line, (BLOCK, BLOCK)).T
        upper = jnp.floor(column * (1.0 / 256.0))
        lower = column - 256.0 * upper
        own[index * BLOCK : (index + 1) * BLOCK, width:] = jnp.where(
            lane_iota(BLOCK) == 0, upper, lower
        ).astype(BF)
    low[...] = own[rows - HALO :, :]
    high[...] = own[:HALO, :]


def quarter_body(width, w_in, w_out, quarter, sems):
    fetched(
        (w_in.at[0], w_out.at[0]), (quarter.at[:width, :], quarter.at[width:, :]), sems
    )


def join_body(parts, *refs):
    pieces, outs = refs[:-parts], refs[-parts:]
    whole = jnp.concatenate([piece[...].astype(F32) for piece in pieces], axis=0).astype(BF)
    size = whole.shape[0] // parts
    for index, out in enumerate(outs):
        out[...] = whole[index * size : (index + 1) * size, :]


def prepare_body(
    width,
    experts,
    capacity,
    own,
    low,
    high,
    order,
    experts_row,
    slots_row,
    xhat,
    rstd_out,
    select,
    idcol,
    idrow,
    routes,
    place_row,
):
    me = lax.axis_index("dp")
    devices = 4 * experts
    share = width // devices
    target = (me ^ order[0:1, :]) * share + order[1:2, :]
    sel = (lax.broadcasted_iota(jnp.int32, (width, width), 0) == target).astype(F32).astype(BF)
    select[...] = sel
    start = 0
    for ref in (low, own, high):
        rows = ref.shape[0]
        values = dot(ref[:, :width], sel)
        mean = jnp.mean(values, axis=1, keepdims=True)
        centered = values - mean
        rstd = lax.rsqrt(jnp.mean(centered * centered, axis=1, keepdims=True) + EPSILON)
        xhat[start : start + rows, :] = centered * rstd
        rstd_out[start : start + rows, :] = jnp.broadcast_to(rstd, (rows, LANES))
        marks = ref[:, width : width + LANES].astype(F32)
        column = marks[:, 0:1] * 256.0 + marks[:, 1:2]
        idcol[start : start + rows, :] = jnp.broadcast_to(column, (rows, LANES))
        turned = marks.T
        line = turned[0:1, :] * 256.0 + turned[1:2, :]
        idrow[:, start : start + rows] = jnp.broadcast_to(line, (8, rows))
        start += rows
    rows = own.shape[0]
    group = (((me >> 2) & (experts // 2 - 1)) << 1) | (me & 1)
    half_bits = (experts // 2).bit_length() - 1
    expert = experts_row[...]
    slot = slots_row[...]
    holder = ((expert & (experts // 2 - 1)) << 1) | (expert >> half_bits)
    place = jnp.where(slot >= 0, (group ^ holder) * capacity + slot, -1).astype(F32)
    lines = jnp.concatenate(
        [place, expert.astype(F32), jnp.zeros((4, rows), F32)], axis=0
    )
    place_row[...] = lines
    routes[...] = jnp.concatenate([lines] * (LANES // 8), axis=0).T


def stacked(values, half):
    zero = jnp.zeros_like(values)
    return jnp.concatenate(
        [jnp.where(half, values, zero), jnp.where(half, zero, values)], axis=0
    )


def forward_body(
    width,
    experts,
    capacity,
    xhat,
    idcol,
    idrow,
    select,
    own,
    cotangent,
    routes,
    place_row,
    near_one,
    near_two,
    far_one,
    far_two,
    *outs,
):
    chunks = outs[:experts]
    qkv, attended, lse, middle, normed_two, probs, normed, weights, weights_tail, gain = outs[
        experts:
    ]
    rows = own.shape[0]
    span = xhat.shape[0]
    cols = 3 * width
    parts = (near_one, near_two, far_one, far_two)
    size = width // 4
    for index, part in enumerate(parts):
        weights[index * size : (index + 1) * size, :] = part[:, :cols]
    sel = select[...]
    tail = jnp.concatenate([part[:, cols:] for part in parts], axis=0)
    gain_row = tail[:, width:].astype(F32).T[experts : experts + 1, :]
    gain[...] = jnp.broadcast_to(gain_row, (8, width))
    natural = dot(sel, tail)
    weights_tail[...] = natural.astype(BF)
    gain_two = natural[:, width:].T[experts + 1 : experts + 2, :]
    normed[...] = (xhat[...] * gain_row).astype(BF)
    qkv[HALO : HALO + rows, :] = dot(normed[HALO : HALO + rows, :], weights[...]).astype(BF)
    for first in (0, HALO + rows):
        qkv[first : first + HALO, width:] = dot(
            normed[first : first + HALO, :], weights[:, width:]
        ).astype(BF)
    half = lane_iota(BLOCK) < HEAD_DIM

    def attend(block, carry):
        base = pl.multiple_of(block * BLOCK, BLOCK)
        marks = idcol[pl.ds(base + HALO, BLOCK), 0:1]
        same = marks == idrow[0:1, pl.ds(base, WINDOW)]
        same = jnp.concatenate([same, same], axis=0)
        totals = jnp.zeros((BLOCK, LANES), F32)
        for pair in range(width // LANES):
            start = pair * LANES
            queries = qkv[pl.ds(base + HALO, BLOCK), start : start + LANES]
            queries = stacked((queries.astype(F32) * SCALE).astype(BF), half)
            keys = qkv[pl.ds(base, WINDOW), width + start : width + start + LANES]
            values = qkv[pl.ds(base, WINDOW), 2 * width + start : 2 * width + start + LANES]
            scores = jnp.where(same, dot(queries, keys, 1, 1), MASKED)
            peak = jnp.max(scores, axis=1, keepdims=True)
            raised = jnp.exp(scores - peak)
            total = jnp.sum(raised, axis=1, keepdims=True)
            result = dot(raised.astype(BF), values) / total
            attended[pl.ds(base, BLOCK), start : start + LANES] = jnp.where(
                half, result[:BLOCK], result[BLOCK:]
            ).astype(BF)
            logs = peak + jnp.log(total)
            lanes = lane_iota(BLOCK)
            totals = jnp.where(lanes == 2 * pair, logs[:BLOCK], totals)
            totals = jnp.where(lanes == 2 * pair + 1, logs[BLOCK:], totals)
        lse[pl.ds(base, BLOCK), :] = totals
        return carry

    lax.fori_loop(0, rows // BLOCK, attend, 0)
    mid = own[:, :width].astype(F32) + dot(attended[...], weights_tail[:, :width])
    middle[...] = mid
    centered = mid - jnp.mean(mid, axis=1, keepdims=True)
    variance = jnp.mean(centered * centered, axis=1, keepdims=True)
    low_two = (centered * lax.rsqrt(variance + EPSILON) * gain_two).astype(BF)
    normed_two[...] = low_two
    lanes = lane_iota(rows)
    logits = jnp.where(lanes < experts, dot(low_two, weights_tail[:, width:]), MASKED)
    raised = jnp.exp(logits - jnp.max(logits, axis=1, keepdims=True))
    share = raised / jnp.sum(raised, axis=1, keepdims=True)
    probs[...] = share
    upstream = cotangent[...].astype(F32)
    scaled = []
    wide_lanes = lanes.astype(F32)
    for choice in range(2):
        gate = jnp.sum(
            jnp.where(wide_lanes == routes[:, 2 + choice : 3 + choice], share, 0.0),
            axis=1,
            keepdims=True,
        )
        scaled.append((gate * upstream).astype(BF))
    scaled = jnp.concatenate(scaled, axis=0)
    for index, chunk in enumerate(chunks):
        slot = (
            lax.broadcasted_iota(jnp.int32, (capacity, rows), 0) + index * capacity
        ).astype(F32)
        first = (slot == place_row[0:1, :]).astype(F32)
        second = (slot == place_row[1:2, :]).astype(F32)
        chunk[:, :width] = dot((first + second).astype(BF), low_two).astype(BF)
        chunk[:, width:] = dot(
            jnp.concatenate([first, second], axis=1).astype(BF), scaled
        ).astype(BF)


def joined(pieces, held):
    capacity = pieces[0].shape[0]
    for index, piece in enumerate(pieces):
        held[index * capacity : (index + 1) * capacity, :] = piece[...]


def expert_body(width, tile, count, *refs):
    pieces, (kept, sent), rest = refs[:count], refs[count : count + 2], refs[count + 2 :]
    returns, (hidden_out, grad_out, arrived, back) = rest[:count], rest[count:]
    joined(pieces, arrived)
    size = 2 * width
    weights = [pair.at[at : at + size, :] for pair in (kept, sent) for at in (0, size)]

    def step(index, carry):
        at = pl.ds(pl.multiple_of(index * tile, tile), tile)
        rows = arrived[at, :width]
        grads = arrived[at, width:]
        total = jnp.zeros((tile, width), F32)
        total_grad = jnp.zeros((tile, width), F32)
        for quarter, weight in enumerate(weights):
            first, second = weight[:width, :], weight[width:, :]
            columns = slice(quarter * width, (quarter + 1) * width)
            pre = dot(rows, first)
            square = pre * pre
            bend = jnp.tanh(GELU_C * pre * (1.0 + GELU_A * square))
            hidden = (0.5 * pre * (1.0 + bend)).astype(BF)
            slope = 0.5 * (1.0 + bend) + 0.5 * pre * (1.0 - bend * bend) * (
                GELU_C * (1.0 + 3.0 * GELU_A * square)
            )
            pre_grad = (dot(grads, second, 1, 1) * slope).astype(BF)
            total = total + dot(hidden, second)
            total_grad = total_grad + dot(pre_grad, first, 1, 1)
            hidden_out[at, columns] = hidden
            grad_out[at, columns] = pre_grad
        back[at, :width] = total.astype(BF)
        back[at, width:] = total_grad.astype(BF)
        return carry

    lax.fori_loop(0, arrived.shape[0] // tile, step, 0)
    capacity = pieces[0].shape[0]
    for index, out in enumerate(returns):
        out[...] = back[index * capacity : (index + 1) * capacity, :]


def expert_grad_body(width, count, *refs):
    hidden, pre_grad, kept, sent, arrived = refs[count:]
    joined(refs[:count], arrived)
    size = 2 * width
    outs = (kept.at[:size, :], kept.at[size:, :], sent.at[:size, :], sent.at[size:, :])
    for quarter, out in enumerate(outs):
        columns = slice(quarter * width, (quarter + 1) * width)
        out[:width, :] = dot(arrived[:, :width], pre_grad[:, columns], 0, 0).astype(out.dtype)
        out[width:, :] = dot(hidden[:, columns], arrived[:, width:], 0, 0).astype(out.dtype)


def at_home(half):
    me = lax.axis_index("dp")
    return (me >= half) == ((me & 1) == 1)


def choose_body(half, size, near_one, near_two, far_one, far_two, kept, sent):
    home = at_home(half)

    @pl.when(home)
    def _():
        kept[:size, :], kept[size:, :] = near_one[...], near_two[...]
        sent[:size, :], sent[size:, :] = far_one[...], far_two[...]

    @pl.when(jnp.logical_not(home))
    def _():
        kept[:size, :], kept[size:, :] = far_one[...], far_two[...]
        sent[:size, :], sent[size:, :] = near_one[...], near_two[...]


def split_body(half, size, mine, theirs, home_one, home_two, away_one, away_two):
    home = at_home(half)

    @pl.when(home)
    def _():
        home_one[...], home_two[...] = mine[:size, :], mine[size:, :]
        away_one[...], away_two[...] = theirs[:size, :], theirs[size:, :]

    @pl.when(jnp.logical_not(home))
    def _():
        home_one[...], home_two[...] = theirs[:size, :], theirs[size:, :]
        away_one[...], away_two[...] = mine[:size, :], mine[size:, :]


def combine_body(
    width,
    experts,
    capacity,
    middle,
    normed_two,
    probs,
    cotangent,
    routes,
    attended,
    weights_tail,
    select,
    *refs,
):
    mixed, middle_grad, attended_grad, tail_grad, held = refs[experts:]
    joined(refs[:experts], held)
    rows = middle.shape[0]
    slots = experts * capacity
    gain_two = weights_tail[:, width:].astype(F32).T[experts + 1 : experts + 2, :]
    gain_grad = jnp.zeros((1, width), F32)
    router_rows = []
    branch_rows = []
    tile = 128
    for start in range(0, rows, tile):
        at = slice(start, start + tile)
        lanes = lane_iota(tile).astype(F32)
        wide = lax.broadcasted_iota(jnp.int32, (tile, slots), 1).astype(F32)
        first = (wide == routes[at, 0:1]).astype(F32)
        second = (wide == routes[at, 1:2]).astype(F32)
        picked = dot(
            jnp.concatenate([first, second], axis=0).astype(BF), held[:, :width]
        )
        grad_two = dot((first + second).astype(BF), held[:, width:])
        upstream = cotangent[at, :].astype(F32)
        share = probs[at, :]
        mid = middle[at, :]
        total = mid
        probs_grad = jnp.zeros((tile, LANES), F32)
        for choice in range(2):
            chosen = lanes == routes[at, 2 + choice : 3 + choice]
            gate = jnp.sum(jnp.where(chosen, share, 0.0), axis=1, keepdims=True)
            one = picked[choice * tile : (choice + 1) * tile, :]
            total = total + gate * one
            gate_grad = jnp.sum(one * upstream, axis=1, keepdims=True)
            probs_grad = probs_grad + jnp.where(chosen, gate_grad, 0.0)
        mixed[at, :] = total.astype(BF)
        logits_grad = (
            share * (probs_grad - jnp.sum(share * probs_grad, axis=1, keepdims=True))
        ).astype(BF)
        router_rows.append(logits_grad)
        grad_two = grad_two + dot(logits_grad, weights_tail[:, width:], 1, 1)
        centered = mid - jnp.mean(mid, axis=1, keepdims=True)
        variance = jnp.mean(centered * centered, axis=1, keepdims=True)
        rstd = lax.rsqrt(variance + EPSILON)
        xhat = centered * rstd
        gain_grad = gain_grad + jnp.sum(grad_two * xhat, axis=0, keepdims=True)
        inner = grad_two * gain_two
        inner_grad = rstd * (
            inner
            - jnp.mean(inner, axis=1, keepdims=True)
            - xhat * jnp.mean(inner * xhat, axis=1, keepdims=True)
        )
        through = upstream + inner_grad
        middle_grad[at, :] = through
        branch = through.astype(BF)
        branch_rows.append(branch)
        attended_grad[at, :] = dot(branch, weights_tail[:, :width], 1, 1).astype(BF)
    sel = select[...]
    logits_grad = jnp.concatenate(router_rows, axis=0)
    branch = jnp.concatenate(branch_rows, axis=0)
    attended_turned = dot(attended[...], sel).astype(BF)
    normed_turned = dot(normed_two[...], sel).astype(BF)
    tail_grad[:, :width] = dot(attended_turned, branch, 0, 0).astype(BF)
    gain_line = jnp.broadcast_to(gain_grad, (8, width))
    upper = gain_line.astype(BF)
    lower = (gain_line - upper.astype(F32)).astype(BF)
    gain_turned = dot(upper, sel) + dot(lower, sel)
    gain_column = jnp.broadcast_to(gain_turned[0:1, :], (LANES, width)).T
    router_grad = dot(normed_turned, logits_grad, 0, 0)
    tail_grad[:, width:] = jnp.where(
        lane_iota(width) == experts + 1, gain_column, router_grad
    ).astype(BF)


def backward_body(
    width,
    qkv,
    lse,
    attended_grad,
    idcol,
    idrow,
    normed,
    tail_grad,
    dq,
    rims_low,
    rims_high,
    inner,
    kept,
    sent_one,
    sent_two,
    acc,
):
    rows = attended_grad.shape[0]
    half_rows = width // 2
    half = lane_iota(BLOCK) < HEAD_DIM
    acc[...] = jnp.zeros_like(acc)

    def attend(block, carry):
        base = pl.multiple_of(block * BLOCK, BLOCK)
        marks = idcol[pl.ds(base + HALO, BLOCK), 0:1]
        same = marks == idrow[0:1, pl.ds(base, WINDOW)]
        same = jnp.concatenate([same, same], axis=0)
        totals = lse[pl.ds(base, BLOCK), :]
        for pair in range(width // LANES):
            start = pair * LANES
            queries = qkv[pl.ds(base + HALO, BLOCK), start : start + LANES]
            queries = stacked((queries.astype(F32) * SCALE).astype(BF), half)
            grads = stacked(attended_grad[pl.ds(base, BLOCK), start : start + LANES], half)
            keys = qkv[pl.ds(base, WINDOW), width + start : width + start + LANES]
            values = qkv[pl.ds(base, WINDOW), 2 * width + start : 2 * width + start + LANES]
            logs = jnp.concatenate(
                [totals[:, 2 * pair : 2 * pair + 1], totals[:, 2 * pair + 1 : 2 * pair + 2]], axis=0
            )
            scores = jnp.where(same, dot(queries, keys, 1, 1), MASKED)
            weights = jnp.exp(scores - logs)
            weights_grad = dot(grads, values, 1, 1)
            product = weights * weights_grad
            delta = jnp.sum(product, axis=1, keepdims=True)
            scores_grad = (product - weights * delta).astype(BF)
            low_weights = weights.astype(BF)
            window = pl.ds(base, WINDOW)
            acc[window, start : start + LANES] += dot(scores_grad, queries, 0, 0)
            acc[window, width + start : width + start + LANES] += dot(low_weights, grads, 0, 0)
            result = dot(scores_grad, keys)
            dq[pl.ds(base, BLOCK), start : start + LANES] = (
                jnp.where(half, result[:BLOCK], result[BLOCK:]) * SCALE
            ).astype(BF)
        return carry

    lax.fori_loop(0, rows // BLOCK, attend, 0)
    rims_low[...] = acc[:HALO, :].astype(BF)
    rims_high[...] = acc[HALO + rows :, :].astype(BF)
    inner[...] = acc[HALO : HALO + rows, :]
    own = normed[HALO : HALO + rows, :]
    query_part = dot(own, dq[...], 0, 0)
    kept[:, :width] = query_part[:half_rows]
    other_part = dot(normed[...], acc[...].astype(BF), 0, 0)
    kept[:, width : 3 * width] = other_part[:half_rows]
    kept[:, 3 * width :] = tail_grad[:half_rows, :].astype(F32)
    size = half_rows // 2
    for start, sent in ((half_rows, sent_one), (half_rows + size, sent_two)):
        at = slice(start, start + size)
        sent[:, :width] = query_part[at].astype(BF)
        sent[:, width : 3 * width] = other_part[at].astype(BF)
        sent[:, 3 * width :] = tail_grad[at, :]


def finish_body(
    width, dq, inner, from_low, from_high, weights, normed_gain, xhat, rstd, select, middle_grad, out, grad
):
    rows = dq.shape[0]
    experts_lane = 0
    grad[...] = inner[...]
    grad[:HALO, :] += from_low[...].astype(F32)
    grad[rows - HALO :, :] += from_high[...].astype(F32)
    values = dot(dq[...], weights[:, :width], 1, 1) + dot(
        grad[...].astype(BF), weights[:, width:], 1, 1
    )
    hat = xhat[HALO : HALO + rows, :]
    values = values * normed_gain[0:1, :]
    part = rstd[HALO : HALO + rows, 0:1] * (
        values
        - jnp.mean(values, axis=1, keepdims=True)
        - hat * jnp.mean(values * hat, axis=1, keepdims=True)
    )
    upper = part.astype(BF)
    lower = (part - upper.astype(F32)).astype(BF)
    sel = select[...]
    out[...] = (middle_grad[...] + dot(upper, sel, 1, 1) + dot(lower, sel, 1, 1)).astype(BF)


def sum_body(parts, own, *refs):
    arrived, outs = refs[: len(refs) - parts], refs[len(refs) - parts :]
    total = own[...].astype(F32)
    if arrived[0].shape[0] < total.shape[0]:
        total = total + jnp.concatenate([ref[...].astype(F32) for ref in arrived], axis=0)
    else:
        for ref in arrived:
            total = total + ref[...].astype(F32)
    size = total.shape[0] // parts
    for index, out in enumerate(outs):
        out[...] = total[index * size : (index + 1) * size, :].astype(out.dtype)


def final_body(width, experts, own, *refs):
    arrived, rest = refs[:-12], refs[-12:]
    w_qkv, gain, *parts, qkv_grad, proj_grad, router_grad, one, two, in_grad, out_grad = rest
    total = own[...]
    for ref in arrived:
        total = total + ref[...].astype(F32)
    qkv = total[:, : 3 * width]
    qkv_grad[...] = qkv
    proj_grad[...] = total[:, 3 * width : 4 * width]
    gain_grad = jnp.sum(qkv * w_qkv[...].astype(F32), axis=1, keepdims=True)
    tail = total[:, 4 * width :]
    share = own.shape[0]
    diagonal = lax.broadcasted_iota(jnp.int32, (share, share), 0) == lane_iota(share, share)

    def turned(column):
        return jnp.sum(jnp.where(diagonal, column, 0.0), axis=0, keepdims=True)

    one[...] = turned(gain_grad) / gain[...].astype(F32)
    two[...] = turned(tail[:, experts + 1 : experts + 2])
    for index in range(experts):
        router_grad[index : index + 1, :] = turned(tail[:, index : index + 1])
    for out, at in ((in_grad, slice(0, width)), (out_grad, slice(width, 2 * width))):
        first, second, third = (part[at, :].astype(F32) for part in parts)
        out[0] = first + second + third


def gather_stages(devices):
    bits = devices.bit_length() - 1
    stages = []
    top = bits - 1
    while top >= 1:
        if top >= 2:
            low, high = 1 << (top - 1), 1 << top
            stages.append([low, high, low | high])
            top -= 2
        else:
            stages.append([1 << top])
            top -= 1
    stages.append([1])
    return stages


def swap(value, devices, mask):
    return lax.ppermute(value, "dp", [(i, i ^ mask) for i in range(devices)])


def reduce_scattered(kept, sent, devices, stages, before):
    total = kept
    arrived = [swap(part, devices, stages[-1][0]) for part in sent]
    for level in range(len(stages) - 1, 0, -1):
        masks = stages[level - 1]
        parts = 1 + len(masks)
        dims = (total.shape[0] // parts, total.shape[1])
        outs = [shape(dims, F32)] + [shape(dims, BF)] * (parts - 1)
        if level == 2:
            arrived, before = lax.optimization_barrier((arrived, before))
        pieces = call(
            functools.partial(sum_body, parts), outs, [total] + arrived, name=f"sum{level}"
        )
        total = pieces[0]
        arrived = [swap(piece, devices, mask) for piece, mask in zip(pieces[1:], masks)]
    return total, arrived, before


def per_device(
    tokens,
    gain_attn,
    w_qkv,
    w_proj,
    gain_moe,
    w_router,
    w_in,
    w_out,
    cotangent,
    image_ids,
    expert_ids,
    slots,
):
    devices = lax.axis_size("dp")
    experts = devices // 4
    rows, width = tokens.shape
    capacity = max(2, 5 * rows // (2 * experts))
    share = width // devices
    span = rows + 2 * HALO
    stages = gather_stages(devices)
    everyone = range(devices)
    half = devices // 2

    ins = [w_qkv, w_proj, w_router.T, gain_attn[None, :], gain_moe[None, :]]
    packed = call(
        functools.partial(pack_body, experts),
        [shape((share, 4 * width + LANES), BF)],
        ins,
        scratch=[pltpu.VMEM(x.shape, x.dtype) for x in ins]
        + [pltpu.SemaphoreType.DMA((len(ins),))],
        name="pack",
        fetch=True,
    )[0]
    ins = [tokens, image_ids.reshape(rows // BLOCK, BLOCK)]
    own, low, high = call(
        functools.partial(front_body, width),
        [
            shape((rows, width + LANES), BF),
            shape((HALO, width + LANES), BF),
            shape((HALO, width + LANES), BF),
        ],
        ins,
        scratch=[pltpu.VMEM(x.shape, x.dtype) for x in ins]
        + [pltpu.SemaphoreType.DMA((len(ins),))],
        name="front",
        fetch=True,
    )
    up = [(i, i + 1) for i in range(devices - 1)]
    down = [(i + 1, i) for i in range(devices - 1)]
    low = lax.ppermute(low, "dp", up)
    high = lax.ppermute(high, "dp", down)
    quarter = call(
        functools.partial(quarter_body, width),
        [shape((2 * width, width), BF)],
        [w_in, w_out],
        scratch=[pltpu.SemaphoreType.DMA((2,))],
        name="quarter",
        fetch=True,
    )[0]
    order = [0]
    near = [packed]
    far = None
    for stage in stages:
        order = [a ^ mask for mask in [0] + stage for a in order]
        arrived = [swap(part, devices, mask) for mask in stage for part in near]
        if stage is stages[0]:
            quarter_far, arrived, low, high = lax.optimization_barrier(
                (quarter, arrived, low, high)
            )
        if stage is stages[-2]:
            quarter_near, arrived = lax.optimization_barrier((quarter, arrived))
        if stage is stages[-1]:
            far = arrived
        else:
            parts = 2 if stage is stages[-2] else 1
            size = near[0].shape[0] * (1 + len(stage)) // parts
            near = call(
                functools.partial(join_body, parts),
                [shape((size, near[0].shape[1]), BF)] * parts,
                [*near, *arrived],
                name="join",
            )
    order = np.stack(
        [
            np.repeat(np.array(order, np.int32), share),
            np.tile(np.arange(share, dtype=np.int32), devices),
        ]
    )

    near_half = [quarter, swap(quarter_near, devices, 2)]
    far_quarter = swap(quarter_far, devices, half)

    masks = [((p >> 1) << 2) | (p & 1) for p in range(experts)]

    def exchange(parts):
        return [parts[0]] + [swap(parts[p], devices, masks[p]) for p in range(1, experts)]

    xhat, rstd, select, idcol, idrow, routes, place_row = call(
        functools.partial(prepare_body, width, experts, capacity),
        [
            shape((span, width), F32),
            shape((span, LANES), F32),
            shape((width, width), BF),
            shape((span, LANES), F32),
            shape((8, span), F32),
            shape((rows, LANES), F32),
            shape((8, rows), F32),
        ],
        [own, low, high, jnp.asarray(order), expert_ids.T, slots.T],
        flops=2 * span * width * width,
        name="prepare",
    )
    outs = call(
        functools.partial(forward_body, width, experts, capacity),
        [shape((capacity, 2 * width), BF)] * experts
        + [
            shape((span, 3 * width), BF),
            shape((rows, width), BF),
            shape((rows, LANES), F32),
            shape((rows, width), F32),
            shape((rows, width), BF),
            shape((rows, LANES), F32),
            shape((span, width), BF),
            shape((width, 3 * width), BF),
            shape((width, width + LANES), BF),
            shape((8, width), F32),
        ],
        [xhat, idcol, idrow, select, own, cotangent, routes, place_row, *near, *far],
        name="forward",
    )
    chunks = outs[:experts]
    qkv, attended, lse, middle, normed_two, probs, normed, weights, weights_tail, gain = outs[
        experts:
    ]

    far_quarter, lse = lax.optimization_barrier((far_quarter, lse))
    far_half = [far_quarter, swap(far_quarter, devices, 2)]
    arrived = exchange(chunks)
    slot_count = experts * capacity
    pair = shape((4 * width, width), BF)
    far_half[1], *arrived[1:-1] = lax.optimization_barrier((far_half[1], *arrived[1:-1]))
    kept_pair, sent_pair = call(
        functools.partial(choose_body, half, 2 * width),
        [pair, pair],
        [*near_half, *far_half],
        name="choose",
    )
    expert_weights = [kept_pair, swap(sent_pair, devices, 1)]
    tile = slot_count // 4
    held = pltpu.VMEM((slot_count, 2 * width), BF)
    outs = call(
        functools.partial(expert_body, width, tile, experts),
        [shape((capacity, 2 * width), BF)] * experts
        + [shape((slot_count, 4 * width), BF)] * 2,
        [*arrived, *expert_weights],
        scratch=[held, held],
        flops=8 * slot_count * width * 4 * width,
        name="expert",
    )
    back, hidden, pre_grad = outs[:experts], outs[experts], outs[experts + 1]
    returned = exchange(back)

    kept_pair, sent_pair = call(
        functools.partial(expert_grad_body, width, experts),
        [pair, pair],
        [*arrived, hidden, pre_grad],
        scratch=[held],
        flops=4 * slot_count * width * 4 * width,
        name="expert_grad",
    )
    other_pair = swap(sent_pair, devices, 1)
    single = shape((2 * width, width), BF)
    home_kept, home_sent, away_kept, away_sent = call(
        functools.partial(split_body, half, 2 * width),
        [single] * 4,
        [kept_pair, other_pair],
        name="split",
    )
    away_came = swap(away_sent, devices, 2)
    home_came = swap(home_sent, devices, 2)
    away = call(
        functools.partial(sum_body, 1), [single], [away_kept, away_came], name="away"
    )[0]

    mixed, middle_grad, attended_grad, tail_grad = call(
        functools.partial(combine_body, width, experts, capacity),
        [
            shape((rows, width), BF),
            shape((rows, width), F32),
            shape((rows, width), BF),
            shape((width, width + LANES), BF),
        ],
        [
            middle,
            normed_two,
            probs,
            cotangent,
            routes,
            attended,
            weights_tail,
            select,
            *returned,
        ],
        scratch=[pltpu.VMEM((slot_count, 2 * width), BF)],
        flops=6 * rows * slot_count * width,
        name="combine",
    )
    attended_grad, away = lax.optimization_barrier((attended_grad, away))
    expert_parts = [home_kept, home_came, swap(away, devices, half)]
    half_rows = width // 2

    dq, rims_low, rims_high, inner, kept, *sent = call(
        functools.partial(backward_body, width),
        [
            shape((rows, width), BF),
            shape((HALO, 2 * width), BF),
            shape((HALO, 2 * width), BF),
            shape((rows, 2 * width), F32),
            shape((half_rows, 4 * width + LANES), F32),
            shape((half_rows // 2, 4 * width + LANES), BF),
            shape((half_rows // 2, 4 * width + LANES), BF),
        ],
        [qkv, lse, attended_grad, idcol, idrow, normed, tail_grad],
        scratch=[pltpu.VMEM((span, 2 * width), F32)],
        name="backward",
    )
    from_high = lax.ppermute(rims_low, "dp", down)
    from_low = lax.ppermute(rims_high, "dp", up)
    total, last, expert_parts = reduce_scattered(kept, sent, devices, stages, expert_parts)
    qkv_grad, proj_grad, router_grad, gain_one_grad, gain_two_grad, in_grad, out_grad = call(
        functools.partial(final_body, width, experts),
        [
            shape((share, 3 * width), F32),
            shape((share, width), F32),
            shape((experts, share), F32),
            shape((1, share), F32),
            shape((1, share), F32),
            shape((1, width, width), F32),
            shape((1, width, width), F32),
        ],
        [total, *last, w_qkv, gain_attn[None, :], *expert_parts],
        name="final",
    )
    grad_tokens = call(
        functools.partial(finish_body, width),
        [shape((rows, width), BF)],
        [dq, inner, from_low, from_high, weights, gain, xhat, rstd, select, middle_grad],
        scratch=[pltpu.VMEM((rows, 2 * width), F32)],
        flops=2 * rows * width * 5 * width,
        name="finish",
    )[0]

    return (
        mixed,
        grad_tokens,
        gain_one_grad.reshape(share),
        qkv_grad,
        proj_grad,
        gain_two_grad.reshape(share),
        router_grad.T,
        in_grad,
        out_grad,
    )


def solution(mesh):
    row, line, cube = P("dp", None), P("dp"), P("dp", None, None)
    return jax.shard_map(
        per_device,
        mesh=mesh,
        in_specs=(row, line, row, row, line, row, cube, cube, row, line, row, row),
        out_specs=(row, row, line, row, row, line, row, cube, cube),
        check_vma=False,
    )
```

time: 863 us -> 191 us (0.22)
  blocking collectives: 356 us -> 0 us
  waiting for transfers between devices: 219 us -> 82.8 us
  matrix products: 81 us -> 0 us
  local copies, waits for them, and re-layouts: 76.1 us -> 7.08 us
  Pallas kernels: 0 us -> 53.1 us
  other arithmetic: 40.7 us -> 0 us
  starting transfers between devices: 78.6 us -> 46.3 us
    all_to_all x4 -> x0, waiting for transfers between devices: 217 us -> none  [the longest x1 80.5 us: per_device(): lax.all_to_all(out_grad, 'dp', split_axis=0, concat_axis=0, tiled=True)]
    all_gather x3 -> x0, blocking collectives: 183 us -> none  [the longest x1 99.8 us: per_device(): lax.all_gather(w_router, 'dp', axis=0, tiled=True)]
    unnamed x3 -> x0, blocking collectives: 173 us -> none
    ppermute x6 -> x42, waiting for transfers between devices: 0.02 us -> 82.8 us  [the longest x38 82.8 us: swap(): return lax.ppermute(value, 'dp', [(i, i ^ mask) for i in range(devices)])]
    dot_general x33 -> x0, matrix products: 81 us -> none  [the longest x1 10.2 us: per_device(): jnp.einsum('scd,fd->scf', grad_arrived, weight_out, preferred_element_typ...]
    pallas_call x0 -> x18, Pallas kernels: none -> 53.1 us  [call(): pl.pallas_call(body, out_shape=tuple(outs), in_specs=[spec] * len(ins), o...]
    unnamed x16 -> x0, starting transfers between devices: 38.4 us -> none
    ppermute x6 -> x42, starting transfers between devices: 11.5 us -> 46.3 us  [the longest x38 38.8 us: swap(): return lax.ppermute(value, 'dp', [(i, i ^ mask) for i in range(devices)])]
  transfers between devices with their start and end apart: 26 -> 42, of which waited for: 5 -> 22; matrix products, arithmetic and copies ran while one was open for 9% -> 0% of each run, Pallas kernels for 0% -> 18%
where the time goes in v1:
time: 191 us; the launch traced here: 190 us
  waiting for transfers between devices  82.8 us (43%)
  Pallas kernels  53.1 us (28%)
  starting transfers between devices  46.3 us (24%)
  local copies, waits for them, and re-layouts  7.08 us (4%)
    ppermute x38, waiting for transfers between devices, swap(): return lax.ppermute(value, 'dp', [(i, i ^ mask) for i in range(devices)])  82.8 us
    pallas_call x18, Pallas kernels, call(): pl.pallas_call(body, out_shape=tuple(outs), in_specs=[spec] * len(ins), o...  53.1 us
    ppermute x38, starting transfers between devices, swap(): return lax.ppermute(value, 'dp', [(i, i ^ mask) for i in range(devices)])  38.8 us
    unnamed x30, local copies, waits for them, and re-layouts  7.08 us
  transfers between devices with their start and end apart: 42, of which 22 were waited for; matrix products, arithmetic and copies ran while one was open for 0% of the time, Pallas kernels for 18%

profile of v1, /device:TPU:0, one launch (start us, length us, event | category | flops | bytes accessed | tf_op | source)
XLA Modules:
  0.0 190.3 jit_solution(13409696129486014528)
XLA Ops:
  0.7 1.0 copy-done.1
  2.7 2.4 %collective-permute-start.3 = (bf16[256,512]{1,0:T(8,128)(2,1)S(1)}, bf16[256,512]{1,0:T(8,128)(2,1)S(1)}, u32[]{:S(2)}, u32[]{:S(2)}) collective-permute-start(bf16[256,512]{1,0:T(8,128)(2,1)S(1)} %get-tuple-element.110), channel_id=1, source_target_pairs={{0,1},{1,2},{2,3},{3,4},{4,5},{5,6},{6,7},{7,8},{8,9},{9,10},{10,1... | collective-permute-start | bytes 786440 | tf_op jit(solution)/shard_map/ppermute | solution.py:682
  5.1 1.3 collective-permute-start.4
  6.4 0.8 copy-done.4
  10.1 8.8 %collective-permute-start.2 = (bf16[12,1664]{1,0:T(8,128)(2,1)S(1)}, bf16[12,1664]{1,0:T(8,128)(2,1)S(1)}, u32[]{:S(2)}, u32[]{:S(2)}) collective-permute-start(bf16[12,1664]{1,0:T(8,128)(2,1)S(1)} %pack.1.refs_0_), channel_id=1, source_target_pairs={{0,24},{1,25},{2,26},{3,27},{4,28},{5,29},{6,30},{7,31},{8,16},{9,... | collective-permute-start | bytes 119816 | tf_op jit(solution)/shard_map/ppermute | solution.py:611
  19.6 1.0 copy-done.2
  20.6 1.0 copy-done.3
  21.7 2.3 %collective-permute-done.1.refs_2_ = bf16[12,1664]{1,0:T(8,128)(2,1)S(1)} collective-permute-done((bf16[12,1664]{1,0:T(8,128)(2,1)S(1)}, bf16[12,1664]{1,0:T(8,128)(2,1)S(1)}, u32[]{:S(2)}, u32[]{:S(2)}) %collective-permute-start.1) | collective-permute-done | bytes 39968 | tf_op jit(solution)/shard_map/ppermute | solution.py:611
  24.0 2.5 %collective-permute-start.10 = (bf16[768,384]{1,0:T(8,128)(2,1)S(1)}, bf16[768,384]{1,0:T(8,128)(2,1)S(1)}, u32[]{:S(2)}, u32[]{:S(2)}) collective-permute-start(bf16[768,384]{1,0:T(8,128)(2,1)S(1)} %quarter.1.near_one), channel_id=1, source_target_pairs={{0,16},{1,17},{2,18},{3,19},{4,20},{5,21},{6,22},{7,23},{8,24},{9,... | collective-permute-start | bytes 1769480 | tf_op jit(solution)/shard_map/ppermute | solution.py:611
  27.3 2.8 %collective-permute-start.5 = (bf16[48,1664]{1,0:T(8,128)(2,1)S(1)}, bf16[48,1664]{1,0:T(8,128)(2,1)S(1)}, u32[]{:S(2)}, u32[]{:S(2)}) collective-permute-start(bf16[48,1664]{1,0:T(8,128)(2,1)S(1)} %join.2.refs_0_), channel_id=1, source_target_pairs={{0,2},{1,3},{2,0},{3,1},{4,6},{5,7},{6,4},{7,5},{8,10},{9,11},{10,... | collective-permute-start | bytes 479240 | tf_op jit(solution)/shard_map/ppermute | solution.py:611
  30.1 2.8 %collective-permute-done.7.refs_3_ = bf16[48,1664]{1,0:T(8,128)(2,1)S(1)} collective-permute-done((bf16[48,1664]{1,0:T(8,128)(2,1)S(1)}, bf16[48,1664]{1,0:T(8,128)(2,1)S(1)}, u32[]{:S(2)}, u32[]{:S(2)}) %collective-permute-start.7) | collective-permute-done | bytes 159776 | tf_op jit(solution)/shard_map/ppermute | solution.py:611
  32.9 0.9 collective-permute-done.6.refs_2_
  34.4 1.7 prepare.1
  36.1 10.5 %forward.1 = (bf16[160,768]{1,0:T(8,128)(2,1)S(1)}, bf16[160,768]{1,0:T(8,128)(2,1)S(1)}, bf16[160,768]{1,0:T(8,128)(2,1)S(1)}, bf16[160,768]{1,0:T(8,128)(2,1)S...) custom-call(f32[1024,384]{1,0:T(8,128)S(1)} %get-tuple-element.114.x, ...), custom_call_target="tpu_custom_call" | custom-call | bytes 1024 | tf_op jit(solution)/shard_map/forward/pallas_call | solution.py:38
  46.6 3.3 %collective-permute-done.10.far_one = bf16[768,384]{1,0:T(8,128)(2,1)S(1)} collective-permute-done((bf16[768,384]{1,0:T(8,128)(2,1)S(1)}, bf16[768,384]{1,0:T(8,128)(2,1)S(1)}, u32[]{:S(2)}, u32[]{:S(2)}) %collective-permute-start.10) | collective-permute-done | bytes 589856 | tf_op jit(solution)/shard_map/ppermute | solution.py:611
  49.9 1.7 collective-permute-start.11
  51.9 1.4 collective-permute-start.13
  53.8 6.9 %collective-permute-done.13.refs_2_ = bf16[160,768]{1,0:T(8,128)(2,1)S(1)} collective-permute-done((bf16[160,768]{1,0:T(8,128)(2,1)S(1)}, bf16[160,768]{1,0:T(8,128)(2,1)S(1)}, u32[]{:S(2)}, u32[]{:S(2)}) %collective-permute-start.13) | collective-permute-done | bytes 245792 | tf_op jit(solution)/shard_map/ppermute | solution.py:611
  60.7 4.5 %collective-permute-done.14.refs_3_ = bf16[160,768]{1,0:T(8,128)(2,1)S(1)} collective-permute-done((bf16[160,768]{1,0:T(8,128)(2,1)S(1)}, bf16[160,768]{1,0:T(8,128)(2,1)S(1)}, u32[]{:S(2)}, u32[]{:S(2)}) %collective-permute-start.14) | collective-permute-done | bytes 245792 | tf_op jit(solution)/shard_map/ppermute | solution.py:611
  65.2 3.3 %collective-permute-done.16.refs_5_ = bf16[160,768]{1,0:T(8,128)(2,1)S(1)} collective-permute-done((bf16[160,768]{1,0:T(8,128)(2,1)S(1)}, bf16[160,768]{1,0:T(8,128)(2,1)S(1)}, u32[]{:S(2)}, u32[]{:S(2)}) %collective-permute-start.16) | collective-permute-done | bytes 245792 | tf_op jit(solution)/shard_map/ppermute | solution.py:611
  68.5 6.1 %collective-permute-done.17.refs_6_ = bf16[160,768]{1,0:T(8,128)(2,1)S(1)} collective-permute-done((bf16[160,768]{1,0:T(8,128)(2,1)S(1)}, bf16[160,768]{1,0:T(8,128)(2,1)S(1)}, u32[]{:S(2)}, u32[]{:S(2)}) %collective-permute-start.17) | collective-permute-done | bytes 245792 | tf_op jit(solution)/shard_map/ppermute | solution.py:611
  74.6 3.1 %collective-permute-done.19.near_two = bf16[768,384]{1,0:T(8,128)(2,1)S(1)} collective-permute-done((bf16[768,384]{1,0:T(8,128)(2,1)S(1)}, bf16[768,384]{1,0:T(8,128)(2,1)S(1)}, u32[]{:S(2)}, u32[]{:S(2)}) %collective-permute-start.19) | collective-permute-done | bytes 589856 | tf_op jit(solution)/shard_map/ppermute | solution.py:611
  78.3 8.6 %collective-permute-done.18.refs_7_ = bf16[160,768]{1,0:T(8,128)(2,1)S(1)} collective-permute-done((bf16[160,768]{1,0:T(8,128)(2,1)S(1)}, bf16[160,768]{1,0:T(8,128)(2,1)S(1)}, u32[]{:S(2)}, u32[]{:S(2)}) %collective-permute-start.18) | collective-permute-done | bytes 245792 | tf_op jit(solution)/shard_map/ppermute | solution.py:611
  86.8 13.4 %expert.1 = (bf16[160,768]{1,0:T(8,128)(2,1)S(1)}, bf16[160,768]{1,0:T(8,128)(2,1)S(1)}, bf16[160,768]{1,0:T(8,128)(2,1)S(1)}, bf16[160,768]{1,0:T(8,128)(2,1)S(...) custom-call(bf16[160,768]{1,0:T(8,128)(2,1)S(1)} %get-tuple-element., ...), custom_call_target="tpu_custom_call" | custom-call | flops 6039797760 | bytes 1024 | tf_op jit(solution)/shard_map/expert/pallas_call | solution.py:38
  100.3 4.3 %expert_grad.1 = (bf16[1536,384]{1,0:T(8,128)(2,1)S(1)}, bf16[1536,384]{1,0:T(8,128)(2,1)S(1)}) custom-call(bf16[160,768]{1,0:T(8,128)(2,1)S(1)} %get-tuple-element.133.refs_0_, bf16[160,768]{1,0:T(8,128)(2,1)S(1)} %collective-permute-done.12.refs_1_, bf16[160,768]{1,0:T(8,128)(2,1)S(1)} %collective-permute-done.13.refs_2_, ...), custom_call_target="tpu_custom_call" | custom-call | flops 3019898880 | bytes 1024 | tf_op jit(solution)/shard_map/expert_grad/pallas_call | solution.py:38
  105.2 1.5 collective-permute-start.22
  108.0 1.8 collective-permute-start.29
  109.8 1.4 collective-permute-start.25
  111.2 2.8 %collective-permute-done.22.refs_2_ = bf16[160,768]{1,0:T(8,128)(2,1)S(1)} collective-permute-done((bf16[160,768]{1,0:T(8,128)(2,1)S(1)}, bf16[160,768]{1,0:T(8,128)(2,1)S(1)}, u32[]{:S(2)}, u32[]{:S(2)}) %collective-permute-start.22) | collective-permute-done | bytes 245792 | tf_op jit(solution)/shard_map/ppermute | solution.py:611
  114.6 3.5 %collective-permute-done.23.refs_3_ = bf16[160,768]{1,0:T(8,128)(2,1)S(1)} collective-permute-done((bf16[160,768]{1,0:T(8,128)(2,1)S(1)}, bf16[160,768]{1,0:T(8,128)(2,1)S(1)}, u32[]{:S(2)}, u32[]{:S(2)}) %collective-permute-start.23) | collective-permute-done | bytes 245792 | tf_op jit(solution)/shard_map/ppermute | solution.py:611
  118.8 1.8 collective-permute-start.34
  120.5 1.6 collective-permute-done.25.refs_5_
  122.1 6.8 %collective-permute-done.26.refs_6_ = bf16[160,768]{1,0:T(8,128)(2,1)S(1)} collective-permute-done((bf16[160,768]{1,0:T(8,128)(2,1)S(1)}, bf16[160,768]{1,0:T(8,128)(2,1)S(1)}, u32[]{:S(2)}, u32[]{:S(2)}) %collective-permute-start.26) | collective-permute-done | bytes 245792 | tf_op jit(solution)/shard_map/ppermute | solution.py:611
  129.0 3.5 %collective-permute-done.27.refs_7_ = bf16[160,768]{1,0:T(8,128)(2,1)S(1)} collective-permute-done((bf16[160,768]{1,0:T(8,128)(2,1)S(1)}, bf16[160,768]{1,0:T(8,128)(2,1)S(1)}, u32[]{:S(2)}, u32[]{:S(2)}) %collective-permute-start.27) | collective-permute-done | bytes 245792 | tf_op jit(solution)/shard_map/ppermute | solution.py:611
  132.5 6.5 %combine.1 = (bf16[512,384]{1,0:T(8,128)(2,1)}, f32[512,384]{1,0:T(8,128)S(1)}, bf16[512,384]{1,0:T(8,128)(2,1)S(1)}, bf16[384,512]{1,0:T(8,128)(2,1)S(1)}) custom-call(f32[512,384]{1,0:T(8,128)S(1)} %get-tuple-element.128.middle, bf16[512,384]{1,0:T(8,128)(2,1)S(1)} %get-tuple-element.129.normed_two, f32[512,128]{1,0:T(8,128)S(1)} %get-tuple-element.130.probs, ...), custom_call_target="tpu_custom_call" | custom-call | flops 1509949440 | bytes 1024 | tf_op jit(solution)/shard_map/combine/pallas_call | solution.py:38
  139.1 1.5 collective-permute-start.35
  140.6 11.0 %backward.1 = (bf16[512,384]{1,0:T(8,128)(2,1)S(1)}, bf16[256,768]{1,0:T(8,128)(2,1)S(1)}, bf16[256,768]{1,0:T(8,128)(2,1)S(1)}, f32[512,768]{1,0:T(8,128)S(1)},...) custom-call(bf16[1024,1152]{1,0:T(8,128)(2,1)S(1)} %get-tuple-element.163.qkv, ...), custom_call_target="tpu_custom_call" | custom-call | bytes 1024 | tf_op jit(solution)/shard_map/backward/pallas_call | solution.py:38
  152.2 2.3 %collective-permute-start.30 = (bf16[256,768]{1,0:T(8,128)(2,1)S(1)}, bf16[256,768]{1,0:T(8,128)(2,1)S(1)}, u32[]{:S(2)}, u32[]{:S(2)}) collective-permute-start(bf16[256,768]{1,0:T(8,128)(2,1)S(1)} %get-tuple-element.177), channel_id=1, source_target_pairs={{0,1},{1,2},{2,3},{3,4},{4,5},{5,6},{6,7},{7,8},{8,9},{9,10},{10,1... | collective-permute-start | bytes 1179656 | tf_op jit(solution)/shard_map/ppermute | solution.py:860
  154.6 1.6 collective-permute-start.31
  156.1 12.6 %collective-permute-done.35.refs_7_ = bf16[768,384]{1,0:T(8,128)(2,1)S(1)} collective-permute-done((bf16[768,384]{1,0:T(8,128)(2,1)S(1)}, bf16[768,384]{1,0:T(8,128)(2,1)S(1)}, u32[]{:S(2)}, u32[]{:S(2)}) %collective-permute-start.35) | collective-permute-done | bytes 589856 | tf_op jit(solution)/shard_map/ppermute | solution.py:611
  168.8 1.1 collective-permute-start.36
  170.5 1.8 collective-permute-start.38
  172.4 3.5 %collective-permute-done.36.refs_0_ = bf16[48,1664]{1,0:T(8,128)(2,1)S(1)} collective-permute-done((bf16[48,1664]{1,0:T(8,128)(2,1)S(1)}, bf16[48,1664]{1,0:T(8,128)(2,1)S(1)}, u32[]{:S(2)}, u32[]{:S(2)}) %collective-permute-start.36) | collective-permute-done | bytes 159776 | tf_op jit(solution)/shard_map/ppermute | solution.py:611
  176.5 2.6 %collective-permute-done.38.refs_2_ = bf16[48,1664]{1,0:T(8,128)(2,1)S(1)} collective-permute-done((bf16[48,1664]{1,0:T(8,128)(2,1)S(1)}, bf16[48,1664]{1,0:T(8,128)(2,1)S(1)}, u32[]{:S(2)}, u32[]{:S(2)}) %collective-permute-start.38) | collective-permute-done | bytes 159776 | tf_op jit(solution)/shard_map/ppermute | solution.py:611
  179.5 3.6 %collective-permute-start.40 = (bf16[12,1664]{1,0:T(8,128)(2,1)S(1)}, bf16[12,1664]{1,0:T(8,128)(2,1)S(1)}, u32[]{:S(2)}, u32[]{:S(2)}) collective-permute-start(bf16[12,1664]{1,0:T(8,128)(2,1)S(1)} %get-tuple-element.197), channel_id=1, source_target_pairs={{0,16},{1,17},{2,18},{3,19},{4,20},{5,21},{6,22},{7,23},{8,24},{9,... | collective-permute-start | bytes 119816 | tf_op jit(solution)/shard_map/ppermute | solution.py:611
  183.7 2.4 %finish.1 = bf16[512,384]{1,0:T(8,128)(2,1)} custom-call(bf16[512,384]{1,0:T(8,128)(2,1)S(1)} %get-tuple-element.175.dq, f32[512,768]{1,0:T(8,128)S(1)} %get-tuple-element.176.inner, bf16[256,768]{1,0:T(8,128)(2,1)S(1)} %collective-permute-done.30.from_low, bf16[256,768]{1,0:T(8,128)(2,1)S(1)} %collective-permute-done.31.from_high, ...), custom_call_target="tpu_custom_call" | custom-call | flops 754974720 | bytes 1024 | tf_op jit(solution)/shard_map/finish/pallas_call | solution.py:38
  186.2 2.8 %collective-permute-done.41.refs_2_ = bf16[12,1664]{1,0:T(8,128)(2,1)S(1)} collective-permute-done((bf16[12,1664]{1,0:T(8,128)(2,1)S(1)}, bf16[12,1664]{1,0:T(8,128)(2,1)S(1)}, u32[]{:S(2)}, u32[]{:S(2)}) %collective-permute-start.41) | collective-permute-done | bytes 39968 | tf_op jit(solution)/shard_map/ppermute | solution.py:611
  189.0 1.3 final.1
  (84 shorter events, 14.0 us)
Async XLA Ops:
  2.3 32.1 %copy-start.12 = (s32[512,2]{0,1:T(2,128)S(1)}, s32[512,2]{0,1:T(2,128)}, u32[]{:S(2)}) copy-start(s32[512,2]{0,1:T(2,128)} %param.23) | copy-start | bytes 12292
  2.3 32.1 %copy-start.13 = (s32[512,2]{0,1:T(2,128)S(1)}, s32[512,2]{0,1:T(2,128)}, u32[]{:S(2)}) copy-start(s32[512,2]{0,1:T(2,128)} %param.24) | copy-start | bytes 12292
  2.3 32.1 %copy-start.14 = (s32[2,384]{1,0:T(2,128)S(1)}, s32[2,384]{1,0:T(2,128)}, u32[]{:S(2)}) copy-start(s32[2,384]{1,0:T(2,128)} %constant.2.clone.order) | copy-start | bytes 9220
  2.7 21.3 %collective-permute-start.3 = (bf16[256,512]{1,0:T(8,128)(2,1)S(1)}, bf16[256,512]{1,0:T(8,128)(2,1)S(1)}, u32[]{:S(2)}, u32[]{:S(2)}) collective-permute-start(bf16[256,512]{1,0:T(8,128)(2,1)S(1)} %get-tuple-element.110), channel_id=1, source_target_pairs={{0,1},{1,2},{2,3},{3,4},{4,5},{5,6},{6,7},{7,8},{8,9},{9,10},{10,1... | collective-permute-start | bytes 786440 | tf_op jit(solution)/shard_map/ppermute | solution.py:682
  5.1 18.9 %collective-permute-start.4 = (bf16[256,512]{1,0:T(8,128)(2,1)S(1)}, bf16[256,512]{1,0:T(8,128)(2,1)S(1)}, u32[]{:S(2)}, u32[]{:S(2)}) collective-permute-start(bf16[256,512]{1,0:T(8,128)(2,1)S(1)} %get-tuple-element.111), channel_id=1, source_target_pairs={{1,0},{2,1},{3,2},{4,3},{5,4},{6,5},{7,6},{8,7},{9,8},{10,9},{11,1... | collective-permute-start | bytes 786440 | tf_op jit(solution)/shard_map/ppermute | solution.py:683
  10.1 11.5 %collective-permute-start.2 = (bf16[12,1664]{1,0:T(8,128)(2,1)S(1)}, bf16[12,1664]{1,0:T(8,128)(2,1)S(1)}, u32[]{:S(2)}, u32[]{:S(2)}) collective-permute-start(bf16[12,1664]{1,0:T(8,128)(2,1)S(1)} %pack.1.refs_0_), channel_id=1, source_target_pairs={{0,24},{1,25},{2,26},{3,27},{4,28},{5,29},{6,30},{7,31},{8,16},{9,... | collective-permute-start | bytes 119816 | tf_op jit(solution)/shard_map/ppermute | solution.py:611
  19.0 5.0 %collective-permute-start.1 = (bf16[12,1664]{1,0:T(8,128)(2,1)S(1)}, bf16[12,1664]{1,0:T(8,128)(2,1)S(1)}, u32[]{:S(2)}, u32[]{:S(2)}) collective-permute-start(bf16[12,1664]{1,0:T(8,128)(2,1)S(1)} %pack.1.refs_0_), channel_id=1, source_target_pairs={{0,16},{1,17},{2,18},{3,19},{4,20},{5,21},{6,22},{7,23},{8,24},{9,... | collective-permute-start | bytes 119816 | tf_op jit(solution)/shard_map/ppermute | solution.py:611
  19.0 5.0 %collective-permute-start = (bf16[12,1664]{1,0:T(8,128)(2,1)S(1)}, bf16[12,1664]{1,0:T(8,128)(2,1)S(1)}, u32[]{:S(2)}, u32[]{:S(2)}) collective-permute-start(bf16[12,1664]{1,0:T(8,128)(2,1)S(1)} %pack.1.refs_0_), channel_id=1, source_target_pairs={{0,8},{1,9},{2,10},{3,11},{4,12},{5,13},{6,14},{7,15},{8,0},{9,1},... | collective-permute-start | bytes 119816 | tf_op jit(solution)/shard_map/ppermute | solution.py:611
  21.7 14.4 %copy-start = (bf16[512,384]{1,0:T(8,128)(2,1)S(1)}, bf16[512,384]{1,0:T(8,128)(2,1)}, u32[]{:S(2)}) copy-start(bf16[512,384]{1,0:T(8,128)(2,1)} %cotangent.3) | copy-start | bytes 1179652
  24.0 25.9 %collective-permute-start.10 = (bf16[768,384]{1,0:T(8,128)(2,1)S(1)}, bf16[768,384]{1,0:T(8,128)(2,1)S(1)}, u32[]{:S(2)}, u32[]{:S(2)}) collective-permute-start(bf16[768,384]{1,0:T(8,128)(2,1)S(1)} %quarter.1.near_one), channel_id=1, source_target_pairs={{0,16},{1,17},{2,18},{3,19},{4,20},{5,21},{6,22},{7,23},{8,24},{9,... | collective-permute-start | bytes 1769480 | tf_op jit(solution)/shard_map/ppermute | solution.py:611
  26.6 6.3 %collective-permute-start.7 = (bf16[48,1664]{1,0:T(8,128)(2,1)S(1)}, bf16[48,1664]{1,0:T(8,128)(2,1)S(1)}, u32[]{:S(2)}, u32[]{:S(2)}) collective-permute-start(bf16[48,1664]{1,0:T(8,128)(2,1)S(1)} %join.2.refs_0_), channel_id=1, source_target_pairs={{0,6},{1,7},{2,4},{3,5},{4,2},{5,3},{6,0},{7,1},{8,14},{9,15},{10,... | collective-permute-start | bytes 479240 | tf_op jit(solution)/shard_map/ppermute | solution.py:611
  26.8 7.0 %collective-permute-start.6 = (bf16[48,1664]{1,0:T(8,128)(2,1)S(1)}, bf16[48,1664]{1,0:T(8,128)(2,1)S(1)}, u32[]{:S(2)}, u32[]{:S(2)}) collective-permute-start(bf16[48,1664]{1,0:T(8,128)(2,1)S(1)} %join.2.refs_0_), channel_id=1, source_target_pairs={{0,4},{1,5},{2,6},{3,7},{4,0},{5,1},{6,2},{7,3},{8,12},{9,13},{10,... | collective-permute-start | bytes 479240 | tf_op jit(solution)/shard_map/ppermute | solution.py:611
  27.3 6.5 %collective-permute-start.5 = (bf16[48,1664]{1,0:T(8,128)(2,1)S(1)}, bf16[48,1664]{1,0:T(8,128)(2,1)S(1)}, u32[]{:S(2)}, u32[]{:S(2)}) collective-permute-start(bf16[48,1664]{1,0:T(8,128)(2,1)S(1)} %join.2.refs_0_), channel_id=1, source_target_pairs={{0,2},{1,3},{2,0},{3,1},{4,6},{5,7},{6,4},{7,5},{8,10},{9,11},{10,... | collective-permute-start | bytes 479240 | tf_op jit(solution)/shard_map/ppermute | solution.py:611
  33.8 2.3 %collective-permute-start.8 = (bf16[96,1664]{1,0:T(8,128)(2,1)S(1)}, bf16[96,1664]{1,0:T(8,128)(2,1)S(1)}, u32[]{:S(2)}, u32[]{:S(2)}) collective-permute-start(bf16[96,1664]{1,0:T(8,128)(2,1)S(1)} %get-tuple-element.126.near_one), channel_id=1, source_target_pairs={{0,1},{1,0},{2,3},{3,2},{4,5},{5,4},{6,7},{7,6},{8,9},{9,8},{10,11... | collective-permute-start | bytes 958472 | tf_op jit(solution)/shard_map/ppermute | solution.py:611
  33.9 2.2 %collective-permute-start.9 = (bf16[96,1664]{1,0:T(8,128)(2,1)S(1)}, bf16[96,1664]{1,0:T(8,128)(2,1)S(1)}, u32[]{:S(2)}, u32[]{:S(2)}) collective-permute-start(bf16[96,1664]{1,0:T(8,128)(2,1)S(1)} %get-tuple-element.127.near_two), channel_id=1, source_target_pairs={{0,1},{1,0},{2,3},{3,2},{4,5},{5,4},{6,7},{7,6},{8,9},{9,8},{10,11... | collective-permute-start | bytes 958472 | tf_op jit(solution)/shard_map/ppermute | solution.py:611
  49.9 24.7 %collective-permute-start.11 = (bf16[768,384]{1,0:T(8,128)(2,1)S(1)}, bf16[768,384]{1,0:T(8,128)(2,1)S(1)}, u32[]{:S(2)}, u32[]{:S(2)}) collective-permute-start(bf16[768,384]{1,0:T(8,128)(2,1)S(1)} %collective-permute-done.10.far_one), channel_id=1, source_target_pairs={{0,2},{1,3},{2,0},{3,1},{4,6},{5,7},{6,4},{7,5},{8,10},{9,11},{10,... | collective-permute-start | bytes 1769480 | tf_op jit(solution)/shard_map/ppermute | solution.py:611
  51.6 26.1 %collective-permute-start.19 = (bf16[768,384]{1,0:T(8,128)(2,1)S(1)}, bf16[768,384]{1,0:T(8,128)(2,1)S(1)}, u32[]{:S(2)}, u32[]{:S(2)}) collective-permute-start(bf16[768,384]{1,0:T(8,128)(2,1)S(1)} %quarter.1.near_one), channel_id=1, source_target_pairs={{0,2},{1,3},{2,0},{3,1},{4,6},{5,7},{6,4},{7,5},{8,10},{9,11},{10,... | collective-permute-start | bytes 1769480 | tf_op jit(solution)/shard_map/ppermute | solution.py:611
  51.9 1.9 collective-permute-start.12
  51.9 8.8 %collective-permute-start.13 = (bf16[160,768]{1,0:T(8,128)(2,1)S(1)}, bf16[160,768]{1,0:T(8,128)(2,1)S(1)}, u32[]{:S(2)}, u32[]{:S(2)}) collective-permute-start(bf16[160,768]{1,0:T(8,128)(2,1)S(1)} %get-tuple-element.138), channel_id=1, source_target_pairs={{0,4},{1,5},{2,6},{3,7},{4,0},{5,1},{6,2},{7,3},{8,12},{9,13},{10,... | collective-permute-start | bytes 737288 | tf_op jit(solution)/shard_map/ppermute | solution.py:611
  53.4 11.8 %collective-permute-start.14 = (bf16[160,768]{1,0:T(8,128)(2,1)S(1)}, bf16[160,768]{1,0:T(8,128)(2,1)S(1)}, u32[]{:S(2)}, u32[]{:S(2)}) collective-permute-start(bf16[160,768]{1,0:T(8,128)(2,1)S(1)} %get-tuple-element.139), channel_id=1, source_target_pairs={{0,5},{1,4},{2,7},{3,6},{4,1},{5,0},{6,3},{7,2},{8,13},{9,12},{10,... | collective-permute-start | bytes 737288 | tf_op jit(solution)/shard_map/ppermute | solution.py:611
  53.8 11.4 %collective-permute-start.15 = (bf16[160,768]{1,0:T(8,128)(2,1)S(1)}, bf16[160,768]{1,0:T(8,128)(2,1)S(1)}, u32[]{:S(2)}, u32[]{:S(2)}) collective-permute-start(bf16[160,768]{1,0:T(8,128)(2,1)S(1)} %get-tuple-element.140), channel_id=1, source_target_pairs={{0,8},{1,9},{2,10},{3,11},{4,12},{5,13},{6,14},{7,15},{8,0},{9,1},... | collective-permute-start | bytes 737288 | tf_op jit(solution)/shard_map/ppermute | solution.py:611
  60.7 7.8 %collective-permute-start.16 = (bf16[160,768]{1,0:T(8,128)(2,1)S(1)}, bf16[160,768]{1,0:T(8,128)(2,1)S(1)}, u32[]{:S(2)}, u32[]{:S(2)}) collective-permute-start(bf16[160,768]{1,0:T(8,128)(2,1)S(1)} %get-tuple-element.141), channel_id=1, source_target_pairs={{0,9},{1,8},{2,11},{3,10},{4,13},{5,12},{6,15},{7,14},{8,1},{9,0},... | collective-permute-start | bytes 737288 | tf_op jit(solution)/shard_map/ppermute | solution.py:611
  65.2 9.4 %collective-permute-start.17 = (bf16[160,768]{1,0:T(8,128)(2,1)S(1)}, bf16[160,768]{1,0:T(8,128)(2,1)S(1)}, u32[]{:S(2)}, u32[]{:S(2)}) collective-permute-start(bf16[160,768]{1,0:T(8,128)(2,1)S(1)} %get-tuple-element.142), channel_id=1, source_target_pairs={{0,12},{1,13},{2,14},{3,15},{4,8},{5,9},{6,10},{7,11},{8,4},{9,5},... | collective-permute-start | bytes 737288 | tf_op jit(solution)/shard_map/ppermute | solution.py:611
  78.1 8.7 %collective-permute-start.20 = (bf16[1536,384]{1,0:T(8,128)(2,1)S(1)}, bf16[1536,384]{1,0:T(8,128)(2,1)S(1)}, u32[]{:S(2)}, u32[]{:S(2)}) collective-permute-start(bf16[1536,384]{1,0:T(8,128)(2,1)S(1)} %get-tuple-element.153), channel_id=1, source_target_pairs={{0,1},{1,0},{2,3},{3,2},{4,5},{5,4},{6,7},{7,6},{8,9},{9,8},{10,11... | collective-permute-start | bytes 3538952 | tf_op jit(solution)/shard_map/ppermute | solution.py:611
  78.2 8.6 %collective-permute-start.18 = (bf16[160,768]{1,0:T(8,128)(2,1)S(1)}, bf16[160,768]{1,0:T(8,128)(2,1)S(1)}, u32[]{:S(2)}, u32[]{:S(2)}) collective-permute-start(bf16[160,768]{1,0:T(8,128)(2,1)S(1)} %get-tuple-element.149), channel_id=1, source_target_pairs={{0,13},{1,12},{2,15},{3,14},{4,9},{5,8},{6,11},{7,10},{8,5},{9,4},... | collective-permute-start | bytes 737288 | tf_op jit(solution)/shard_map/ppermute | solution.py:611
  104.6 2.9 %collective-permute-start.28 = (bf16[1536,384]{1,0:T(8,128)(2,1)S(1)}, bf16[1536,384]{1,0:T(8,128)(2,1)S(1)}, u32[]{:S(2)}, u32[]{:S(2)}) collective-permute-start(bf16[1536,384]{1,0:T(8,128)(2,1)S(1)} %get-tuple-element.169), channel_id=1, source_target_pairs={{0,1},{1,0},{2,3},{3,2},{4,5},{5,4},{6,7},{7,6},{8,9},{9,8},{10,11... | collective-permute-start | bytes 3538952 | tf_op jit(solution)/shard_map/ppermute | solution.py:611
  105.1 4.7 %collective-permute-start.21 = (bf16[160,768]{1,0:T(8,128)(2,1)S(1)}, bf16[160,768]{1,0:T(8,128)(2,1)S(1)}, u32[]{:S(2)}, u32[]{:S(2)}) collective-permute-start(bf16[160,768]{1,0:T(8,128)(2,1)S(1)} %get-tuple-element.155), channel_id=1, source_target_pairs={{0,1},{1,0},{2,3},{3,2},{4,5},{5,4},{6,7},{7,6},{8,9},{9,8},{10,11... | collective-permute-start | bytes 737288 | tf_op jit(solution)/shard_map/ppermute | solution.py:611
  105.2 8.8 %collective-permute-start.22 = (bf16[160,768]{1,0:T(8,128)(2,1)S(1)}, bf16[160,768]{1,0:T(8,128)(2,1)S(1)}, u32[]{:S(2)}, u32[]{:S(2)}) collective-permute-start(bf16[160,768]{1,0:T(8,128)(2,1)S(1)} %get-tuple-element.156), channel_id=1, source_target_pairs={{0,4},{1,5},{2,6},{3,7},{4,0},{5,1},{6,2},{7,3},{8,12},{9,13},{10,... | collective-permute-start | bytes 737288 | tf_op jit(solution)/shard_map/ppermute | solution.py:611
  106.6 11.5 %collective-permute-start.23 = (bf16[160,768]{1,0:T(8,128)(2,1)S(1)}, bf16[160,768]{1,0:T(8,128)(2,1)S(1)}, u32[]{:S(2)}, u32[]{:S(2)}) collective-permute-start(bf16[160,768]{1,0:T(8,128)(2,1)S(1)} %get-tuple-element.157), channel_id=1, source_target_pairs={{0,5},{1,4},{2,7},{3,6},{4,1},{5,0},{6,3},{7,2},{8,13},{9,12},{10,... | collective-permute-start | bytes 737288 | tf_op jit(solution)/shard_map/ppermute | solution.py:611
  108.0 31.0 %collective-permute-start.29 = (bf16[768,384]{1,0:T(8,128)(2,1)S(1)}, bf16[768,384]{1,0:T(8,128)(2,1)S(1)}, u32[]{:S(2)}, u32[]{:S(2)}) collective-permute-start(bf16[768,384]{1,0:T(8,128)(2,1)S(1)} %get-tuple-element.171), channel_id=1, source_target_pairs={{0,2},{1,3},{2,0},{3,1},{4,6},{5,7},{6,4},{7,5},{8,10},{9,11},{10,... | collective-permute-start | bytes 1769480 | tf_op jit(solution)/shard_map/ppermute | solution.py:611
  109.8 9.0 %collective-permute-start.24 = (bf16[160,768]{1,0:T(8,128)(2,1)S(1)}, bf16[160,768]{1,0:T(8,128)(2,1)S(1)}, u32[]{:S(2)}, u32[]{:S(2)}) collective-permute-start(bf16[160,768]{1,0:T(8,128)(2,1)S(1)} %get-tuple-element.158), channel_id=1, source_target_pairs={{0,8},{1,9},{2,10},{3,11},{4,12},{5,13},{6,14},{7,15},{8,0},{9,1},... | collective-permute-start | bytes 737288 | tf_op jit(solution)/shard_map/ppermute | solution.py:611
  109.8 12.3 %collective-permute-start.25 = (bf16[160,768]{1,0:T(8,128)(2,1)S(1)}, bf16[160,768]{1,0:T(8,128)(2,1)S(1)}, u32[]{:S(2)}, u32[]{:S(2)}) collective-permute-start(bf16[160,768]{1,0:T(8,128)(2,1)S(1)} %get-tuple-element.159), channel_id=1, source_target_pairs={{0,9},{1,8},{2,11},{3,10},{4,13},{5,12},{6,15},{7,14},{8,1},{9,0},... | collective-permute-start | bytes 737288 | tf_op jit(solution)/shard_map/ppermute | solution.py:611
  114.0 15.0 %collective-permute-start.26 = (bf16[160,768]{1,0:T(8,128)(2,1)S(1)}, bf16[160,768]{1,0:T(8,128)(2,1)S(1)}, u32[]{:S(2)}, u32[]{:S(2)}) collective-permute-start(bf16[160,768]{1,0:T(8,128)(2,1)S(1)} %get-tuple-element.160), channel_id=1, source_target_pairs={{0,12},{1,13},{2,14},{3,15},{4,8},{5,9},{6,10},{7,11},{8,4},{9,5},... | collective-permute-start | bytes 737288 | tf_op jit(solution)/shard_map/ppermute | solution.py:611
  118.1 14.3 %collective-permute-start.27 = (bf16[160,768]{1,0:T(8,128)(2,1)S(1)}, bf16[160,768]{1,0:T(8,128)(2,1)S(1)}, u32[]{:S(2)}, u32[]{:S(2)}) collective-permute-start(bf16[160,768]{1,0:T(8,128)(2,1)S(1)} %get-tuple-element.161), channel_id=1, source_target_pairs={{0,13},{1,12},{2,15},{3,14},{4,9},{5,8},{6,11},{7,10},{8,5},{9,4},... | collective-permute-start | bytes 737288 | tf_op jit(solution)/shard_map/ppermute | solution.py:611
  118.8 35.8 %collective-permute-start.34 = (bf16[768,384]{1,0:T(8,128)(2,1)S(1)}, bf16[768,384]{1,0:T(8,128)(2,1)S(1)}, u32[]{:S(2)}, u32[]{:S(2)}) collective-permute-start(bf16[768,384]{1,0:T(8,128)(2,1)S(1)} %get-tuple-element.187), channel_id=1, source_target_pairs={{0,2},{1,3},{2,0},{3,1},{4,6},{5,7},{6,4},{7,5},{8,10},{9,11},{10,... | collective-permute-start | bytes 1769480 | tf_op jit(solution)/shard_map/ppermute | solution.py:611
  139.1 29.6 %collective-permute-start.35 = (bf16[768,384]{1,0:T(8,128)(2,1)S(1)}, bf16[768,384]{1,0:T(8,128)(2,1)S(1)}, u32[]{:S(2)}, u32[]{:S(2)}) collective-permute-start(bf16[768,384]{1,0:T(8,128)(2,1)S(1)} %away.1), channel_id=1, source_target_pairs={{0,16},{1,17},{2,18},{3,19},{4,20},{5,21},{6,22},{7,23},{8,24},{9,... | collective-permute-start | bytes 1769480 | tf_op jit(solution)/shard_map/ppermute | solution.py:611
  151.7 4.5 %collective-permute-start.32 = (bf16[96,1664]{1,0:T(8,128)(2,1)S(1)}, bf16[96,1664]{1,0:T(8,128)(2,1)S(1)}, u32[]{:S(2)}, u32[]{:S(2)}) collective-permute-start(bf16[96,1664]{1,0:T(8,128)(2,1)S(1)} %get-tuple-element.184), channel_id=1, source_target_pairs={{0,1},{1,0},{2,3},{3,2},{4,5},{5,4},{6,7},{7,6},{8,9},{9,8},{10,11... | collective-permute-start | bytes 958472 | tf_op jit(solution)/shard_map/ppermute | solution.py:611
  152.1 4.0 %collective-permute-start.33 = (bf16[96,1664]{1,0:T(8,128)(2,1)S(1)}, bf16[96,1664]{1,0:T(8,128)(2,1)S(1)}, u32[]{:S(2)}, u32[]{:S(2)}) collective-permute-start(bf16[96,1664]{1,0:T(8,128)(2,1)S(1)} %get-tuple-element.185), channel_id=1, source_target_pairs={{0,1},{1,0},{2,3},{3,2},{4,5},{5,4},{6,7},{7,6},{8,9},{9,8},{10,11... | collective-permute-start | bytes 958472 | tf_op jit(solution)/shard_map/ppermute | solution.py:611
  152.2 31.5 %collective-permute-start.30 = (bf16[256,768]{1,0:T(8,128)(2,1)S(1)}, bf16[256,768]{1,0:T(8,128)(2,1)S(1)}, u32[]{:S(2)}, u32[]{:S(2)}) collective-permute-start(bf16[256,768]{1,0:T(8,128)(2,1)S(1)} %get-tuple-element.177), channel_id=1, source_target_pairs={{0,1},{1,2},{2,3},{3,4},{4,5},{5,6},{6,7},{7,8},{8,9},{9,10},{10,1... | collective-permute-start | bytes 1179656 | tf_op jit(solution)/shard_map/ppermute | solution.py:860
  154.6 29.1 %collective-permute-start.31 = (bf16[256,768]{1,0:T(8,128)(2,1)S(1)}, bf16[256,768]{1,0:T(8,128)(2,1)S(1)}, u32[]{:S(2)}, u32[]{:S(2)}) collective-permute-start(bf16[256,768]{1,0:T(8,128)(2,1)S(1)} %get-tuple-element.178), channel_id=1, source_target_pairs={{1,0},{2,1},{3,2},{4,3},{5,4},{6,5},{7,6},{8,7},{9,8},{10,9},{11,1... | collective-permute-start | bytes 1179656 | tf_op jit(solution)/shard_map/ppermute | solution.py:859
  168.8 7.0 %collective-permute-start.36 = (bf16[48,1664]{1,0:T(8,128)(2,1)S(1)}, bf16[48,1664]{1,0:T(8,128)(2,1)S(1)}, u32[]{:S(2)}, u32[]{:S(2)}) collective-permute-start(bf16[48,1664]{1,0:T(8,128)(2,1)S(1)} %get-tuple-element.192), channel_id=1, source_target_pairs={{0,2},{1,3},{2,0},{3,1},{4,6},{5,7},{6,4},{7,5},{8,10},{9,11},{10,... | collective-permute-start | bytes 479240 | tf_op jit(solution)/shard_map/ppermute | solution.py:611
  169.9 6.7 %collective-permute-start.37 = (bf16[48,1664]{1,0:T(8,128)(2,1)S(1)}, bf16[48,1664]{1,0:T(8,128)(2,1)S(1)}, u32[]{:S(2)}, u32[]{:S(2)}) collective-permute-start(bf16[48,1664]{1,0:T(8,128)(2,1)S(1)} %get-tuple-element.193), channel_id=1, source_target_pairs={{0,4},{1,5},{2,6},{3,7},{4,0},{5,1},{6,2},{7,3},{8,12},{9,13},{10,... | collective-permute-start | bytes 479240 | tf_op jit(solution)/shard_map/ppermute | solution.py:611
  170.5 8.6 %collective-permute-start.38 = (bf16[48,1664]{1,0:T(8,128)(2,1)S(1)}, bf16[48,1664]{1,0:T(8,128)(2,1)S(1)}, u32[]{:S(2)}, u32[]{:S(2)}) collective-permute-start(bf16[48,1664]{1,0:T(8,128)(2,1)S(1)} %get-tuple-element.194), channel_id=1, source_target_pairs={{0,6},{1,7},{2,4},{3,5},{4,2},{5,3},{6,0},{7,1},{8,14},{9,15},{10,... | collective-permute-start | bytes 479240 | tf_op jit(solution)/shard_map/ppermute | solution.py:611
  179.2 6.9 %collective-permute-start.39 = (bf16[12,1664]{1,0:T(8,128)(2,1)S(1)}, bf16[12,1664]{1,0:T(8,128)(2,1)S(1)}, u32[]{:S(2)}, u32[]{:S(2)}) collective-permute-start(bf16[12,1664]{1,0:T(8,128)(2,1)S(1)} %get-tuple-element.196), channel_id=1, source_target_pairs={{0,8},{1,9},{2,10},{3,11},{4,12},{5,13},{6,14},{7,15},{8,0},{9,1},... | collective-permute-start | bytes 119816 | tf_op jit(solution)/shard_map/ppermute | solution.py:611
  179.5 6.8 %collective-permute-start.40 = (bf16[12,1664]{1,0:T(8,128)(2,1)S(1)}, bf16[12,1664]{1,0:T(8,128)(2,1)S(1)}, u32[]{:S(2)}, u32[]{:S(2)}) collective-permute-start(bf16[12,1664]{1,0:T(8,128)(2,1)S(1)} %get-tuple-element.197), channel_id=1, source_target_pairs={{0,16},{1,17},{2,18},{3,19},{4,20},{5,21},{6,22},{7,23},{8,24},{9,... | collective-permute-start | bytes 119816 | tf_op jit(solution)/shard_map/ppermute | solution.py:611
  183.1 5.9 %collective-permute-start.41 = (bf16[12,1664]{1,0:T(8,128)(2,1)S(1)}, bf16[12,1664]{1,0:T(8,128)(2,1)S(1)}, u32[]{:S(2)}, u32[]{:S(2)}) collective-permute-start(bf16[12,1664]{1,0:T(8,128)(2,1)S(1)} %get-tuple-element.198), channel_id=1, source_target_pairs={{0,24},{1,25},{2,26},{3,27},{4,28},{5,29},{6,30},{7,31},{8,16},{9,... | collective-permute-start | bytes 119816 | tf_op jit(solution)/shard_map/ppermute | solution.py:611
  183.7 5.3 %copy-start.5 = (bf16[12,1152]{1,0:T(8,128)(2,1)S(1)}, bf16[12,1152]{1,0:T(8,128)(2,1)}, u32[]{:S(2)}) copy-start(bf16[12,1152]{1,0:T(8,128)(2,1)} %refs_3_.1) | copy-start | bytes 82948
  183.7 5.3 %copy-start.9 = (bf16[12]{0:T(256)(128)(2,1)S(1)}, bf16[12]{0:T(256)(128)(2,1)}, u32[]{:S(2)}) copy-start(bf16[12]{0:T(256)(128)(2,1)} %param.14) | copy-start | bytes 76
  (9 other events, 7.1 us)

commit v2 on v1

--- a/solution.py
+++ b/solution.py
@@ -34,7 +34,9 @@
 
 def call(body, outs, ins, scratch=(), flops=0, name=None, vmem_mib=12, fetch=False):
     vmem = pl.BlockSpec(memory_space=pltpu.VMEM)
-    spec = pl.BlockSpec(memory_space=pl.ANY) if fetch else vmem
+    spec = pl.BlockSpec(memory_space=pltpu.HBM) if fetch else vmem
+    if fetch:
+        ins = [pltpu.with_memory_space_constraint(x, pltpu.HBM) for x in ins]
     return pl.pallas_call(
         body,
         out_shape=tuple(outs),
@@ -162,7 +164,9 @@
     expert = experts_row[...]
     slot = slots_row[...]
     holder = ((expert & (experts // 2 - 1)) << 1) | (expert >> half_bits)
-    place = jnp.where(slot >= 0, (group ^ holder) * capacity + slot, -1).astype(F32)
+    apart = group ^ holder
+    index = (apart & 1) * (experts // 2) + (apart >> 1)
+    place = jnp.where(slot >= 0, index * capacity + slot, -1).astype(F32)
     lines = jnp.concatenate(
         [place, expert.astype(F32), jnp.zeros((4, rows), F32)], axis=0
     )
@@ -195,10 +199,8 @@
     far_two,
     *outs,
 ):
-    chunks = outs[:experts]
-    qkv, attended, lse, middle, normed_two, probs, normed, weights, weights_tail, gain = outs[
-        experts:
-    ]
+    same_core, other_core, outs = outs[0], outs[1 : 1 + experts // 2], outs[1 + experts // 2 :]
+    qkv, attended, lse, middle, normed_two, probs, normed, weights, weights_tail, gain = outs
     rows = own.shape[0]
     span = xhat.shape[0]
     cols = 3 * width
@@ -223,32 +225,32 @@
 
     def attend(block, carry):
         base = pl.multiple_of(block * BLOCK, BLOCK)
-        marks = idcol[pl.ds(base + HALO, BLOCK), 0:1]
-        same = marks == idrow[0:1, pl.ds(base, WINDOW)]
-        same = jnp.concatenate([same, same], axis=0)
-        totals = jnp.zeros((BLOCK, LANES), F32)
+        window = pl.ds(base, WINDOW)
+        here = pl.ds(base, BLOCK)
+        marks = idrow[0:1, pl.ds(base + HALO, BLOCK)]
+        same = idcol[window, 0:1] == jnp.concatenate([marks, marks], axis=1)
         for pair in range(width // LANES):
             start = pair * LANES
             queries = qkv[pl.ds(base + HALO, BLOCK), start : start + LANES]
             queries = stacked((queries.astype(F32) * SCALE).astype(BF), half)
-            keys = qkv[pl.ds(base, WINDOW), width + start : width + start + LANES]
-            values = qkv[pl.ds(base, WINDOW), 2 * width + start : 2 * width + start + LANES]
-            scores = jnp.where(same, dot(queries, keys, 1, 1), MASKED)
-            peak = jnp.max(scores, axis=1, keepdims=True)
+            keys = qkv[window, width + start : width + start + LANES]
+            values = qkv[window, 2 * width + start : 2 * width + start + LANES]
+            scores = jnp.where(same, dot(keys, queries, 1, 1), MASKED)
+            peak = jnp.max(scores, axis=0, keepdims=True)
             raised = jnp.exp(scores - peak)
-            total = jnp.sum(raised, axis=1, keepdims=True)
-            result = dot(raised.astype(BF), values) / total
-            attended[pl.ds(base, BLOCK), start : start + LANES] = jnp.where(
+            total = jnp.sum(raised, axis=0, keepdims=True)
+            result = dot(raised.astype(BF), values, 0, 0)
+            column = jnp.broadcast_to(1.0 / total, (8, 2 * BLOCK)).T[:, 0:1]
+            result = result * column
+            attended[here, start : start + LANES] = jnp.where(
                 half, result[:BLOCK], result[BLOCK:]
             ).astype(BF)
             logs = peak + jnp.log(total)
-            lanes = lane_iota(BLOCK)
-            totals = jnp.where(lanes == 2 * pair, logs[:BLOCK], totals)
-            totals = jnp.where(lanes == 2 * pair + 1, logs[BLOCK:], totals)
-        lse[pl.ds(base, BLOCK), :] = totals
+            lse[2 * pair : 2 * pair + 1, here] = logs[:, :BLOCK]
+            lse[2 * pair + 1 : 2 * pair + 2, here] = logs[:, BLOCK:]
         return carry
 
-    lax.fori_loop(0, rows // BLOCK, attend, 0)
+    lax.fori_loop(0, rows // BLOCK, attend, 0, unroll=4)
     mid = own[:, :width].astype(F32) + dot(attended[...], weights_tail[:, :width])
     middle[...] = mid
     centered = mid - jnp.mean(mid, axis=1, keepdims=True)
@@ -261,25 +263,33 @@
     share = raised / jnp.sum(raised, axis=1, keepdims=True)
     probs[...] = share
     upstream = cotangent[...].astype(F32)
-    scaled = []
     wide_lanes = lanes.astype(F32)
+    gates = []
     for choice in range(2):
         gate = jnp.sum(
             jnp.where(wide_lanes == routes[:, 2 + choice : 3 + choice], share, 0.0),
             axis=1,
             keepdims=True,
         )
-        scaled.append((gate * upstream).astype(BF))
-    scaled = jnp.concatenate(scaled, axis=0)
-    for index, chunk in enumerate(chunks):
+        gates.append(jnp.broadcast_to(gate, (rows, 8)))
+    gates = jnp.concatenate(gates + [jnp.zeros((rows, LANES - 16), F32)], axis=1).T
+    source = jnp.concatenate([low_two, cotangent[...]], axis=1)
+    for index in range(experts):
+        if index < experts // 2:
+            chunk = same_core.at[index * capacity : (index + 1) * capacity, :]
+        else:
+            chunk = other_core[index - experts // 2]
         slot = (
             lax.broadcasted_iota(jnp.int32, (capacity, rows), 0) + index * capacity
         ).astype(F32)
-        first = (slot == place_row[0:1, :]).astype(F32)
-        second = (slot == place_row[1:2, :]).astype(F32)
-        chunk[:, :width] = dot((first + second).astype(BF), low_two).astype(BF)
-        chunk[:, width:] = dot(
-            jnp.concatenate([first, second], axis=1).astype(BF), scaled
+        first = slot == place_row[0:1, :]
+        second = slot == place_row[1:2, :]
+        weight = jnp.where(first, gates[0:1, :], jnp.where(second, gates[8:9, :], 0.0))
+        taken = jnp.where(first | second, 1.0, 0.0)
+        moved = dot(taken.astype(BF), source)
+        chunk[:, :width] = moved[:, :width].astype(BF)
+        chunk[:, width:] = (
+            moved[:, width:] * jnp.sum(weight, axis=1, keepdims=True)
         ).astype(BF)
 
 
@@ -290,35 +300,38 @@
 
 
 def expert_body(width, tile, count, *refs):
-    pieces, (kept, sent), rest = refs[:count], refs[count : count + 2], refs[count + 2 :]
-    returns, (hidden_out, grad_out, arrived, back) = rest[:count], rest[count:]
+    pieces, kept, sent, rest = (
+        refs[:count],
+        refs[count],
+        refs[count + 1 : count + 5],
+        refs[count + 5 :],
+    )
+    returns, (hidden_out, grad_out, arrived, back, w_in, w_out) = rest[:count], rest[count:]
     joined(pieces, arrived)
-    size = 2 * width
-    weights = [pair.at[at : at + size, :] for pair in (kept, sent) for at in (0, size)]
+    w_ins = [kept.at[:width, :], kept.at[2 * width : 3 * width, :], sent[0], sent[2]]
+    w_outs = [kept.at[width : 2 * width, :], kept.at[3 * width :, :], sent[1], sent[3]]
+    for quarter, (first, second) in enumerate(zip(w_ins, w_outs)):
+        at = slice(quarter * width, (quarter + 1) * width)
+        w_in[:, at] = first[...]
+        w_out[at, :] = second[...]
+    step_width = 2 * width // 3
 
     def step(index, carry):
         at = pl.ds(pl.multiple_of(index * tile, tile), tile)
-        rows = arrived[at, :width]
-        grads = arrived[at, width:]
-        total = jnp.zeros((tile, width), F32)
-        total_grad = jnp.zeros((tile, width), F32)
-        for quarter, weight in enumerate(weights):
-            first, second = weight[:width, :], weight[width:, :]
-            columns = slice(quarter * width, (quarter + 1) * width)
-            pre = dot(rows, first)
+        for start in range(0, 4 * width, step_width):
+            columns = slice(start, start + step_width)
+            pre = dot(arrived[at, :width], w_in[:, columns])
+            hidden_grad = dot(arrived[at, width:], w_out[columns, :], 1, 1)
             square = pre * pre
-            bend = jnp.tanh(GELU_C * pre * (1.0 + GELU_A * square))
-            hidden = (0.5 * pre * (1.0 + bend)).astype(BF)
-            slope = 0.5 * (1.0 + bend) + 0.5 * pre * (1.0 - bend * bend) * (
-                GELU_C * (1.0 + 3.0 * GELU_A * square)
-            )
-            pre_grad = (dot(grads, second, 1, 1) * slope).astype(BF)
-            total = total + dot(hidden, second)
-            total_grad = total_grad + dot(pre_grad, first, 1, 1)
-            hidden_out[at, columns] = hidden
-            grad_out[at, columns] = pre_grad
-        back[at, :width] = total.astype(BF)
-        back[at, width:] = total_grad.astype(BF)
+            bend = jnp.tanh(pre * (GELU_C + (GELU_C * GELU_A) * square))
+            scaled = 0.5 * pre
+            hidden_out[at, columns] = (scaled + scaled * bend).astype(BF)
+            slope = (0.5 + 0.5 * bend) + (
+                scaled * (GELU_C + (3.0 * GELU_C * GELU_A) * square)
+            ) * (1.0 - bend * bend)
+            grad_out[at, columns] = (hidden_grad * slope).astype(BF)
+        back[at, :width] = dot(hidden_out[at, :], w_out[...]).astype(BF)
+        back[at, width:] = dot(grad_out[at, :], w_in[...], 1, 1).astype(BF)
         return carry
 
     lax.fori_loop(0, arrived.shape[0] // tile, step, 0)
@@ -332,10 +345,12 @@
     joined(refs[:count], arrived)
     size = 2 * width
     outs = (kept.at[:size, :], kept.at[size:, :], sent.at[:size, :], sent.at[size:, :])
+    grad_in = dot(arrived[:, :width], pre_grad[...], 0, 0)
     for quarter, out in enumerate(outs):
-        columns = slice(quarter * width, (quarter + 1) * width)
-        out[:width, :] = dot(arrived[:, :width], pre_grad[:, columns], 0, 0).astype(out.dtype)
-        out[width:, :] = dot(hidden[:, columns], arrived[:, width:], 0, 0).astype(out.dtype)
+        out[:width, :] = grad_in[:, quarter * width : (quarter + 1) * width].astype(BF)
+    grad_out = dot(arrived[:, width:], hidden[...], 0, 0)
+    for quarter, out in enumerate(outs):
+        out[width:, :] = grad_out[:, quarter * width : (quarter + 1) * width].T.astype(BF)
 
 
 def at_home(half):
@@ -343,32 +358,63 @@
     return (me >= half) == ((me & 1) == 1)
 
 
-def choose_body(half, size, near_one, near_two, far_one, far_two, kept, sent):
-    home = at_home(half)
-
-    @pl.when(home)
+def halve_body(whole, upper, lower):
+    size = upper.shape[0]
+    upper[...] = whole[:size, :]
+    lower[...] = whole[size:, :]
+
+
+def choose_body(half, size, near_one, near_in, near_out, *refs):
+    far, kept, sent = refs[:4], refs[4], refs[5:]
+    near = (near_one.at[:size, :], near_one.at[size:, :], near_in, near_out)
+
+    def place(mine, theirs):
+        for index, (one, two) in enumerate(zip(mine, theirs)):
+            kept[index * size : (index + 1) * size, :] = one[...]
+            sent[index][...] = two[...]
+
+    @pl.when(at_home(half))
     def _():
-        kept[:size, :], kept[size:, :] = near_one[...], near_two[...]
-        sent[:size, :], sent[size:, :] = far_one[...], far_two[...]
-
-    @pl.when(jnp.logical_not(home))
+        place(near, far)
+
+    @pl.when(jnp.logical_not(at_home(half)))
     def _():
-        kept[:size, :], kept[size:, :] = far_one[...], far_two[...]
-        sent[:size, :], sent[size:, :] = near_one[...], near_two[...]
-
-
-def split_body(half, size, mine, theirs, home_one, home_two, away_one, away_two):
-    home = at_home(half)
-
-    @pl.when(home)
+        place(far, near)
+
+
+def mix_body(capacity, mine, *refs):
+    theirs, outs = refs[: len(refs) // 2], refs[len(refs) // 2 :]
+    for index, (part, out) in enumerate(zip(theirs, outs)):
+        out[:capacity, :] = mine[index * capacity : (index + 1) * capacity, :]
+        out[capacity:, :] = part[...]
+
+
+def unmix_body(capacity, *refs):
+    count = len(refs) // 2
+    pieces, mine, theirs = refs[:count], refs[count], refs[count + 1 :]
+    for index, (piece, out) in enumerate(zip(pieces, theirs)):
+        mine[index * capacity : (index + 1) * capacity, :] = piece[:capacity, :]
+        out[...] = piece[capacity:, :]
+
+
+def split_body(half, size, mine, theirs, weights, normed, *outs):
+    home_one, home_two, home_three, *away, keys_turned = outs
+    width = size // 2
+    keys_turned[...] = dot(weights[:, width : 2 * width], normed[...], 0, 1).astype(BF)
+
+    def place(home, other):
+        home_one[...] = home[:size, :]
+        home_two[...], home_three[...] = home[size : 3 * size // 2, :], home[3 * size // 2 :, :]
+        away[0][...] = other[:size, :]
+        away[1][...], away[2][...] = other[size : 3 * size // 2, :], other[3 * size // 2 :, :]
+
+    @pl.when(at_home(half))
     def _():
-        home_one[...], home_two[...] = mine[:size, :], mine[size:, :]
-        away_one[...], away_two[...] = theirs[:size, :], theirs[size:, :]
-
-    @pl.when(jnp.logical_not(home))
+        place(mine, theirs)
+
+    @pl.when(jnp.logical_not(at_home(half)))
     def _():
-        home_one[...], home_two[...] = theirs[:size, :], theirs[size:, :]
-        away_one[...], away_two[...] = mine[:size, :], mine[size:, :]
+        place(theirs, mine)
 
 
 def combine_body(
@@ -385,15 +431,18 @@
     select,
     *refs,
 ):
-    mixed, middle_grad, attended_grad, tail_grad, held = refs[experts:]
-    joined(refs[:experts], held)
+    mixed, middle_grad, attended_grad, tail_grad, held = refs[-5:]
+    start = 0
+    for ref in refs[:-5]:
+        held[start : start + ref.shape[0], :] = ref[...]
+        start += ref.shape[0]
     rows = middle.shape[0]
     slots = experts * capacity
     gain_two = weights_tail[:, width:].astype(F32).T[experts + 1 : experts + 2, :]
     gain_grad = jnp.zeros((1, width), F32)
     router_rows = []
     branch_rows = []
-    tile = 128
+    tile = rows
     for start in range(0, rows, tile):
         at = slice(start, start + tile)
         lanes = lane_iota(tile).astype(F32)
@@ -458,6 +507,7 @@
 def backward_body(
     width,
     qkv,
+    keys_turned,
     lse,
     attended_grad,
     idcol,
@@ -469,48 +519,45 @@
     rims_high,
     inner,
     kept,
-    sent_one,
-    sent_two,
-    acc,
+    *sents,
 ):
     rows = attended_grad.shape[0]
     half_rows = width // 2
+    *sents, acc = sents
     half = lane_iota(BLOCK) < HEAD_DIM
+    upper = lax.broadcasted_iota(jnp.int32, (LANES, BLOCK), 0) < HEAD_DIM
     acc[...] = jnp.zeros_like(acc)
 
     def attend(block, carry):
         base = pl.multiple_of(block * BLOCK, BLOCK)
-        marks = idcol[pl.ds(base + HALO, BLOCK), 0:1]
-        same = marks == idrow[0:1, pl.ds(base, WINDOW)]
-        same = jnp.concatenate([same, same], axis=0)
-        totals = lse[pl.ds(base, BLOCK), :]
+        window = pl.ds(base, WINDOW)
+        here = pl.ds(base, BLOCK)
+        marks = idrow[0:1, pl.ds(base + HALO, BLOCK)]
+        same = idcol[window, 0:1] == jnp.concatenate([marks, marks], axis=1)
         for pair in range(width // LANES):
             start = pair * LANES
             queries = qkv[pl.ds(base + HALO, BLOCK), start : start + LANES]
             queries = stacked((queries.astype(F32) * SCALE).astype(BF), half)
-            grads = stacked(attended_grad[pl.ds(base, BLOCK), start : start + LANES], half)
-            keys = qkv[pl.ds(base, WINDOW), width + start : width + start + LANES]
-            values = qkv[pl.ds(base, WINDOW), 2 * width + start : 2 * width + start + LANES]
+            grads = stacked(attended_grad[here, start : start + LANES], half)
+            keys = qkv[window, width + start : width + start + LANES]
+            values = qkv[window, 2 * width + start : 2 * width + start + LANES]
             logs = jnp.concatenate(
-                [totals[:, 2 * pair : 2 * pair + 1], totals[:, 2 * pair + 1 : 2 * pair + 2]], axis=0
+                [lse[2 * pair : 2 * pair + 1, here], lse[2 * pair + 1 : 2 * pair + 2, here]], axis=1
             )
-            scores = jnp.where(same, dot(queries, keys, 1, 1), MASKED)
+            scores = jnp.where(same, dot(keys, queries, 1, 1), MASKED)
             weights = jnp.exp(scores - logs)
-            weights_grad = dot(grads, values, 1, 1)
-            product = weights * weights_grad
-            delta = jnp.sum(product, axis=1, keepdims=True)
-            scores_grad = (product - weights * delta).astype(BF)
-            low_weights = weights.astype(BF)
-            window = pl.ds(base, WINDOW)
-            acc[window, start : start + LANES] += dot(scores_grad, queries, 0, 0)
-            acc[window, width + start : width + start + LANES] += dot(low_weights, grads, 0, 0)
-            result = dot(scores_grad, keys)
-            dq[pl.ds(base, BLOCK), start : start + LANES] = (
-                jnp.where(half, result[:BLOCK], result[BLOCK:]) * SCALE
-            ).astype(BF)
+            weights_grad = dot(values, grads, 1, 1)
+            delta = jnp.sum(weights * weights_grad, axis=0, keepdims=True)
+            scores_grad = (weights * (weights_grad - delta)).astype(BF)
+            acc[window, start : start + LANES] += dot(scores_grad, queries)
+            acc[window, width + start : width + start + LANES] += dot(weights.astype(BF), grads)
+            result = dot(keys_turned[start : start + LANES, window], scores_grad) * SCALE
+            dq[here, start : start + LANES] = (
+                jnp.where(upper, result[:, :BLOCK], result[:, BLOCK:]).T.astype(BF)
+            )
         return carry
 
-    lax.fori_loop(0, rows // BLOCK, attend, 0)
+    lax.fori_loop(0, rows // BLOCK, attend, 0, unroll=4)
     rims_low[...] = acc[:HALO, :].astype(BF)
     rims_high[...] = acc[HALO + rows :, :].astype(BF)
     inner[...] = acc[HALO : HALO + rows, :]
@@ -520,9 +567,9 @@
     other_part = dot(normed[...], acc[...].astype(BF), 0, 0)
     kept[:, width : 3 * width] = other_part[:half_rows]
     kept[:, 3 * width :] = tail_grad[:half_rows, :].astype(F32)
-    size = half_rows // 2
-    for start, sent in ((half_rows, sent_one), (half_rows + size, sent_two)):
-        at = slice(start, start + size)
+    size = half_rows // len(sents)
+    for index, sent in enumerate(sents):
+        at = slice(half_rows + index * size, half_rows + (index + 1) * size)
         sent[:, :width] = query_part[at].astype(BF)
         sent[:, width : 3 * width] = other_part[at].astype(BF)
         sent[:, 3 * width :] = tail_grad[at, :]
@@ -566,7 +613,7 @@
 
 
 def final_body(width, experts, own, *refs):
-    arrived, rest = refs[:-12], refs[-12:]
+    arrived, rest = refs[:-13], refs[-13:]
     w_qkv, gain, *parts, qkv_grad, proj_grad, router_grad, one, two, in_grad, out_grad = rest
     total = own[...]
     for ref in arrived:
@@ -586,9 +633,12 @@
     two[...] = turned(tail[:, experts + 1 : experts + 2])
     for index in range(experts):
         router_grad[index : index + 1, :] = turned(tail[:, index : index + 1])
-    for out, at in ((in_grad, slice(0, width)), (out_grad, slice(width, 2 * width))):
-        first, second, third = (part[at, :].astype(F32) for part in parts)
-        out[0] = first + second + third
+    mine, upper, lower, other = parts
+    for out, at, beside in (
+        (in_grad, slice(0, width), upper),
+        (out_grad, slice(width, 2 * width), lower),
+    ):
+        out[0] = mine[at, :].astype(F32) + beside[...].astype(F32) + other[at, :].astype(F32)
 
 
 def gather_stages(devices):
@@ -663,6 +713,19 @@
         name="pack",
         fetch=True,
     )[0]
+    first_arrived = [swap(packed, devices, mask) for mask in stages[0]]
+    first_arrived[0], tokens = lax.optimization_barrier((first_arrived[0], tokens))
+    packed, w_in, w_out = lax.optimization_barrier((packed, w_in, w_out))
+    near_in = swap(w_in[0], devices, 2)
+    near_out = swap(w_out[0], devices, 2)
+    quarter = call(
+        functools.partial(quarter_body, width),
+        [shape((2 * width, width), BF)],
+        [w_in, w_out],
+        scratch=[pltpu.SemaphoreType.DMA((2,))],
+        name="quarter",
+        fetch=True,
+    )[0]
     ins = [tokens, image_ids.reshape(rows // BLOCK, BLOCK)]
     own, low, high = call(
         functools.partial(front_body, width),
@@ -681,26 +744,22 @@
     down = [(i + 1, i) for i in range(devices - 1)]
     low = lax.ppermute(low, "dp", up)
     high = lax.ppermute(high, "dp", down)
-    quarter = call(
-        functools.partial(quarter_body, width),
-        [shape((2 * width, width), BF)],
-        [w_in, w_out],
-        scratch=[pltpu.SemaphoreType.DMA((2,))],
-        name="quarter",
-        fetch=True,
-    )[0]
     order = [0]
     near = [packed]
     far = None
     for stage in stages:
         order = [a ^ mask for mask in [0] + stage for a in order]
-        arrived = [swap(part, devices, mask) for mask in stage for part in near]
         if stage is stages[0]:
-            quarter_far, arrived, low, high = lax.optimization_barrier(
-                (quarter, arrived, low, high)
+            arrived = first_arrived
+        else:
+            arrived = [swap(part, devices, mask) for mask in stage for part in near]
+        if stage is stages[0]:
+            arrived[1], quarter, near_in = lax.optimization_barrier(
+                (arrived[1], quarter, near_in)
             )
+            quarter_far, low, high = lax.optimization_barrier((quarter, low, high))
         if stage is stages[-2]:
-            quarter_near, arrived = lax.optimization_barrier((quarter, arrived))
+            arrived[1], near_out = lax.optimization_barrier((arrived[1], near_out))
         if stage is stages[-1]:
             far = arrived
         else:
@@ -719,13 +778,12 @@
         ]
     )
 
-    near_half = [quarter, swap(quarter_near, devices, 2)]
     far_quarter = swap(quarter_far, devices, half)
 
-    masks = [((p >> 1) << 2) | (p & 1) for p in range(experts)]
-
     def exchange(parts):
-        return [parts[0]] + [swap(parts[p], devices, masks[p]) for p in range(1, experts)]
+        return [parts[0]] + [
+            swap(part, devices, 4 * index) for index, part in enumerate(parts) if index
+        ]
 
     xhat, rstd, select, idcol, idrow, routes, place_row = call(
         functools.partial(prepare_body, width, experts, capacity),
@@ -742,13 +800,16 @@
         flops=2 * span * width * width,
         name="prepare",
     )
+    chips = experts // 2
+    half_slots = chips * capacity
     outs = call(
         functools.partial(forward_body, width, experts, capacity),
-        [shape((capacity, 2 * width), BF)] * experts
+        [shape((half_slots, 2 * width), BF)]
+        + [shape((capacity, 2 * width), BF)] * chips
         + [
             shape((span, 3 * width), BF),
             shape((rows, width), BF),
-            shape((rows, LANES), F32),
+            shape((8, rows), F32),
             shape((rows, width), F32),
             shape((rows, width), BF),
             shape((rows, LANES), F32),
@@ -760,60 +821,84 @@
         [xhat, idcol, idrow, select, own, cotangent, routes, place_row, *near, *far],
         name="forward",
     )
-    chunks = outs[:experts]
-    qkv, attended, lse, middle, normed_two, probs, normed, weights, weights_tail, gain = outs[
-        experts:
-    ]
-
-    far_quarter, lse = lax.optimization_barrier((far_quarter, lse))
-    far_half = [far_quarter, swap(far_quarter, devices, 2)]
-    arrived = exchange(chunks)
+    same_core, other_core, outs = outs[0], outs[1 : 1 + chips], outs[1 + chips :]
+    qkv, attended, lse, middle, normed_two, probs, normed, weights, weights_tail, gain = outs
+
+    both = shape((2 * capacity, 2 * width), BF)
+    pieces = call(
+        functools.partial(mix_body, capacity),
+        [both] * chips,
+        [same_core, *[swap(part, devices, 1) for part in other_core]],
+        name="mix",
+    )
+    far_quarter, piece = lax.optimization_barrier((far_quarter, pieces[0]))
+    arrived = exchange([piece, *pieces[1:]])
+    far_half = call(
+        halve_body, [shape((width, width), BF)] * 2, [far_quarter], name="halve"
+    )
+    far_half = [*far_half] + [swap(part, devices, 2) for part in far_half]
     slot_count = experts * capacity
     pair = shape((4 * width, width), BF)
-    far_half[1], *arrived[1:-1] = lax.optimization_barrier((far_half[1], *arrived[1:-1]))
-    kept_pair, sent_pair = call(
-        functools.partial(choose_body, half, 2 * width),
-        [pair, pair],
-        [*near_half, *far_half],
+    far_half[-1], *arrived[1:] = lax.optimization_barrier((far_half[-1], *arrived[1:]))
+    kept_pair, *sent_parts = call(
+        functools.partial(choose_body, half, width),
+        [pair] + [shape((width, width), BF)] * 4,
+        [quarter, near_in, near_out, *far_half],
         name="choose",
     )
-    expert_weights = [kept_pair, swap(sent_pair, devices, 1)]
+    expert_weights = [kept_pair] + [swap(part, devices, 1) for part in sent_parts]
     tile = slot_count // 4
     held = pltpu.VMEM((slot_count, 2 * width), BF)
     outs = call(
-        functools.partial(expert_body, width, tile, experts),
-        [shape((capacity, 2 * width), BF)] * experts
-        + [shape((slot_count, 4 * width), BF)] * 2,
+        functools.partial(expert_body, width, tile, chips),
+        [both] * chips + [shape((slot_count, 4 * width), BF)] * 2,
         [*arrived, *expert_weights],
-        scratch=[held, held],
+        scratch=[
+            held,
+            held,
+            pltpu.VMEM((width, 4 * width), BF),
+            pltpu.VMEM((4 * width, width), BF),
+        ],
+        vmem_mib=16,
         flops=8 * slot_count * width * 4 * width,
         name="expert",
     )
-    back, hidden, pre_grad = outs[:experts], outs[experts], outs[experts + 1]
+    back, hidden, pre_grad = outs[:chips], outs[chips], outs[chips + 1]
     returned = exchange(back)
-
     kept_pair, sent_pair = call(
-        functools.partial(expert_grad_body, width, experts),
+        functools.partial(expert_grad_body, width, chips),
         [pair, pair],
         [*arrived, hidden, pre_grad],
         scratch=[held],
+        vmem_mib=16,
         flops=4 * slot_count * width * 4 * width,
         name="expert_grad",
     )
     other_pair = swap(sent_pair, devices, 1)
     single = shape((2 * width, width), BF)
-    home_kept, home_sent, away_kept, away_sent = call(
+    square = shape((width, width), BF)
+    home_kept, *home_sent = call(
         functools.partial(split_body, half, 2 * width),
-        [single] * 4,
-        [kept_pair, other_pair],
+        [single, square, square] * 2 + [shape((width, span), BF)],
+        [kept_pair, other_pair, weights, normed],
         name="split",
     )
-    away_came = swap(away_sent, devices, 2)
-    home_came = swap(home_sent, devices, 2)
+    home_sent, (away_kept, *away_sent, keys_turned) = home_sent[:2], home_sent[2:]
+    away_came = [swap(part, devices, 2) for part in away_sent]
+    *home_sent, returned[1] = lax.optimization_barrier((*home_sent, returned[1]))
+    home_came = [swap(part, devices, 2) for part in home_sent]
     away = call(
-        functools.partial(sum_body, 1), [single], [away_kept, away_came], name="away"
+        functools.partial(sum_body, 1), [single], [away_kept, *away_came], name="away"
     )[0]
 
+    returned[-1], away = lax.optimization_barrier((returned[-1], away))
+    mine, *theirs = call(
+        functools.partial(unmix_body, capacity),
+        [shape((half_slots, 2 * width), BF)] + [shape((capacity, 2 * width), BF)] * chips,
+        returned,
+        name="unmix",
+    )
+    theirs = [swap(part, devices, 1) for part in theirs]
     mixed, middle_grad, attended_grad, tail_grad = call(
         functools.partial(combine_body, width, experts, capacity),
         [
@@ -831,14 +916,14 @@
             attended,
             weights_tail,
             select,
-            *returned,
+            mine,
+            *theirs,
         ],
         scratch=[pltpu.VMEM((slot_count, 2 * width), BF)],
         flops=6 * rows * slot_count * width,
         name="combine",
     )
-    attended_grad, away = lax.optimization_barrier((attended_grad, away))
-    expert_parts = [home_kept, home_came, swap(away, devices, half)]
+    expert_parts = [home_kept, *home_came, swap(away, devices, half)]
     half_rows = width // 2
 
     dq, rims_low, rims_high, inner, kept, *sent = call(
@@ -849,10 +934,9 @@
             shape((HALO, 2 * width), BF),
             shape((rows, 2 * width), F32),
             shape((half_rows, 4 * width + LANES), F32),
-            shape((half_rows // 2, 4 * width + LANES), BF),
-            shape((half_rows // 2, 4 * width + LANES), BF),
-        ],
-        [qkv, lse, attended_grad, idcol, idrow, normed, tail_grad],
+        ]
+        + [shape((half_rows // 2, 4 * width + LANES), BF)] * 2,
+        [qkv, keys_turned, lse, attended_grad, idcol, idrow, normed, tail_grad],
         scratch=[pltpu.VMEM((span, 2 * width), F32)],
         name="backward",
     )

time: 191 us -> 177 us (0.927)
  local copies, waits for them, and re-layouts: 7.08 us -> 0.03 us
  Pallas kernels: 53.1 us -> 46.1 us
  starting transfers between devices: 46.3 us -> 51.7 us
  waiting for transfers between devices: 82.8 us -> 78.3 us
    ppermute x38 -> x45, starting transfers between devices: 38.8 us -> 45.9 us  [swap(): return lax.ppermute(value, 'dp', [(i, i ^ mask) for i in range(devices)])]
    unnamed x30 -> x12, local copies, waits for them, and re-layouts: 7.08 us -> 0.03 us
    pallas_call x18 -> x21, Pallas kernels: 53.1 us -> 46.1 us  [call(): pl.pallas_call(body, out_shape=tuple(outs), in_specs=[spec] * len(ins), o...]
    ppermute x38 -> x45, waiting for transfers between devices: 82.8 us -> 77.5 us  [swap(): return lax.ppermute(value, 'dp', [(i, i ^ mask) for i in range(devices)])]
  transfers between devices with their start and end apart: 42 -> 49, of which waited for: 22 -> 27; matrix products, arithmetic and copies ran while one was open for 0% -> 0% of each run, Pallas kernels for 18% -> 16%
where the time goes in v2:
time: 177 us
  waiting for transfers between devices  78.3 us (44%)
  starting transfers between devices  51.7 us (29%)
  Pallas kernels  46.1 us (26%)
    ppermute x45, waiting for transfers between devices, swap(): return lax.ppermute(value, 'dp', [(i, i ^ mask) for i in range(devices)])  77.5 us
    pallas_call x21, Pallas kernels, call(): pl.pallas_call(body, out_shape=tuple(outs), in_specs=[spec] * len(ins), o...  46.1 us
    ppermute x45, starting transfers between devices, swap(): return lax.ppermute(value, 'dp', [(i, i ^ mask) for i in range(devices)])  45.9 us
  transfers between devices with their start and end apart: 49, of which 27 were waited for; matrix products, arithmetic and copies ran while one was open for 0% of the time, Pallas kernels for 16%

profile of v2, /device:TPU:0, one launch (start us, length us, event | category | flops | bytes accessed | tf_op | source)
XLA Modules:
  0.0 177.1 jit_solution(11651634643812951582)
XLA Ops:
  0.7 1.0 pack.1.refs_0_
  1.7 3.0 %collective-permute-start.2 = (bf16[384,384]{1,0:T(8,128)(2,1)}, bf16[384,384]{1,0:T(8,128)(2,1)S(1)}, u32[]{:S(2)}, u32[]{:S(2)}) collective-permute-start(bf16[384,384]{1,0:T(8,128)(2,1)} %bitcast.15), channel_id=1, source_target_pairs={{0,2},{1,3},{2,0},{3,1},{4,6},{5,7},{6,4},{7,5},{8,10},{9,11},{10,... | collective-permute-start | bytes 884744 | tf_op jit(solution)/shard_map/ppermute | solution.py:661
  4.8 2.0 %collective-permute-start = (bf16[12,1664]{1,0:T(8,128)(2,1)S(1)}, bf16[12,1664]{1,0:T(8,128)(2,1)S(1)}, u32[]{:S(2)}, u32[]{:S(2)}) collective-permute-start(bf16[12,1664]{1,0:T(8,128)(2,1)S(1)} %pack.1.refs_0_), channel_id=1, source_target_pairs={{0,8},{1,9},{2,10},{3,11},{4,12},{5,13},{6,14},{7,15},{8,0},{9,1},... | collective-permute-start | bytes 119816 | tf_op jit(solution)/shard_map/ppermute | solution.py:661
  6.8 2.6 %collective-permute-start.1 = (bf16[12,1664]{1,0:T(8,128)(2,1)S(1)}, bf16[12,1664]{1,0:T(8,128)(2,1)S(1)}, u32[]{:S(2)}, u32[]{:S(2)}) collective-permute-start(bf16[12,1664]{1,0:T(8,128)(2,1)S(1)} %pack.1.refs_0_), channel_id=1, source_target_pairs={{0,16},{1,17},{2,18},{3,19},{4,20},{5,21},{6,22},{7,23},{8,24},{9,... | collective-permute-start | bytes 119816 | tf_op jit(solution)/shard_map/ppermute | solution.py:661
  9.4 1.1 quarter.1.near_one
  10.5 1.9 %collective-permute-done.1.refs_2_ = bf16[12,1664]{1,0:T(8,128)(2,1)S(1)} collective-permute-done((bf16[12,1664]{1,0:T(8,128)(2,1)S(1)}, bf16[12,1664]{1,0:T(8,128)(2,1)S(1)}, u32[]{:S(2)}, u32[]{:S(2)}) %collective-permute-start.1) | collective-permute-done | bytes 39968 | tf_op jit(solution)/shard_map/ppermute | solution.py:661
  12.7 2.6 %collective-permute-done.5.refs_3_ = bf16[12,1664]{1,0:T(8,128)(2,1)S(1)} collective-permute-done((bf16[12,1664]{1,0:T(8,128)(2,1)S(1)}, bf16[12,1664]{1,0:T(8,128)(2,1)S(1)}, u32[]{:S(2)}, u32[]{:S(2)}) %collective-permute-start.5) | collective-permute-done | bytes 39968 | tf_op jit(solution)/shard_map/ppermute | solution.py:661
  15.4 1.6 collective-permute-start.7
  17.0 1.4 collective-permute-start.9
  18.9 1.2 front.1
  20.1 1.3 collective-permute-start.3
  21.5 1.3 collective-permute-start.4
  22.8 1.8 %collective-permute-done.9.refs_3_ = bf16[48,1664]{1,0:T(8,128)(2,1)S(1)} collective-permute-done((bf16[48,1664]{1,0:T(8,128)(2,1)S(1)}, bf16[48,1664]{1,0:T(8,128)(2,1)S(1)}, u32[]{:S(2)}, u32[]{:S(2)}) %collective-permute-start.9) | collective-permute-done | bytes 159776 | tf_op jit(solution)/shard_map/ppermute | solution.py:661
  26.6 5.4 %collective-permute-start.12 = (bf16[768,384]{1,0:T(8,128)(2,1)S(1)}, bf16[768,384]{1,0:T(8,128)(2,1)S(1)}, u32[]{:S(2)}, u32[]{:S(2)}) collective-permute-start(bf16[768,384]{1,0:T(8,128)(2,1)S(1)} %quarter.1.near_one), channel_id=1, source_target_pairs={{0,16},{1,17},{2,18},{3,19},{4,20},{5,21},{6,22},{7,23},{8,24},{9,... | collective-permute-start | bytes 1769480 | tf_op jit(solution)/shard_map/ppermute | solution.py:661
  32.0 1.7 prepare.1
  33.7 7.5 %forward.1 = (bf16[640,768]{1,0:T(8,128)(2,1)S(1)}, bf16[160,768]{1,0:T(8,128)(2,1)S(1)}, bf16[160,768]{1,0:T(8,128)(2,1)S(1)}, bf16[160,768]{1,0:T(8,128)(2,1)S...) custom-call(f32[1024,384]{1,0:T(8,128)S(1)} %get-tuple-element.132.x, ...), custom_call_target="tpu_custom_call" | custom-call | bytes 1024 | tf_op jit(solution)/shard_map/forward/pallas_call | solution.py:40
  41.2 1.2 collective-permute-start.13
  44.8 1.5 collective-permute-start.18
  46.3 1.6 collective-permute-start.19
  48.3 9.1 %collective-permute-done.12.whole = bf16[768,384]{1,0:T(8,128)(2,1)S(1)} collective-permute-done((bf16[768,384]{1,0:T(8,128)(2,1)S(1)}, bf16[768,384]{1,0:T(8,128)(2,1)S(1)}, u32[]{:S(2)}, u32[]{:S(2)}) %collective-permute-start.12) | collective-permute-done | bytes 589856 | tf_op jit(solution)/shard_map/ppermute | solution.py:661
  57.5 3.0 %collective-permute-start.17 = (bf16[384,384]{1,0:T(8,128)(2,1)S(1)}, bf16[384,384]{1,0:T(8,128)(2,1)S(1)}, u32[]{:S(2)}, u32[]{:S(2)}) collective-permute-start(bf16[384,384]{1,0:T(8,128)(2,1)S(1)} %get-tuple-element.158.refs_1_), channel_id=1, source_target_pairs={{0,2},{1,3},{2,0},{3,1},{4,6},{5,7},{6,4},{7,5},{8,10},{9,11},{10,... | collective-permute-start | bytes 884744 | tf_op jit(solution)/shard_map/ppermute | solution.py:661
  60.6 7.8 %collective-permute-done.17.refs_3_ = bf16[384,384]{1,0:T(8,128)(2,1)S(1)} collective-permute-done((bf16[384,384]{1,0:T(8,128)(2,1)S(1)}, bf16[384,384]{1,0:T(8,128)(2,1)S(1)}, u32[]{:S(2)}, u32[]{:S(2)}) %collective-permute-start.17) | collective-permute-done | bytes 294944 | tf_op jit(solution)/shard_map/ppermute | solution.py:661
  68.4 1.0 collective-permute-done.19.refs_2_
  69.4 12.8 %collective-permute-done.20.refs_3_ = bf16[320,768]{1,0:T(8,128)(2,1)S(1)} collective-permute-done((bf16[320,768]{1,0:T(8,128)(2,1)S(1)}, bf16[320,768]{1,0:T(8,128)(2,1)S(1)}, u32[]{:S(2)}, u32[]{:S(2)}) %collective-permute-start.20) | collective-permute-done | bytes 491552 | tf_op jit(solution)/shard_map/ppermute | solution.py:661
  85.5 11.0 %expert.1 = (bf16[320,768]{1,0:T(8,128)(2,1)S(1)}, bf16[320,768]{1,0:T(8,128)(2,1)S(1)}, bf16[320,768]{1,0:T(8,128)(2,1)S(1)}, bf16[320,768]{1,0:T(8,128)(2,1)S(...) custom-call(bf16[320,768]{1,0:T(8,128)(2,1)S(1)} %get-tuple-element.156.refs_0_, ...), custom_call_target="tpu_custom_call" | custom-call | flops 6039797760 | bytes 1024 | tf_op jit(solution)/shard_map/expert/pallas_call | solution.py:40
  96.5 3.4 %expert_grad.1 = (bf16[1536,384]{1,0:T(8,128)(2,1)S(1)}, bf16[1536,384]{1,0:T(8,128)(2,1)S(1)}) custom-call(bf16[320,768]{1,0:T(8,128)(2,1)S(1)} %get-tuple-element.156.refs_0_, bf16[320,768]{1,0:T(8,128)(2,1)S(1)} %collective-permute-done.18.refs_1_, bf16[320,768]{1,0:T(8,128)(2,1)S(1)} %collective-permute-done.19.refs_2_, ...), custom_call_target="tpu_custom_call" | custom-call | flops 3019898880 | bytes 1024 | tf_op jit(solution)/shard_map/expert_grad/pallas_call | solution.py:40
  100.1 3.5 %collective-permute-start.28 = (bf16[320,768]{1,0:T(8,128)(2,1)S(1)}, bf16[320,768]{1,0:T(8,128)(2,1)S(1)}, u32[]{:S(2)}, u32[]{:S(2)}) collective-permute-start(bf16[320,768]{1,0:T(8,128)(2,1)S(1)} %get-tuple-element.185), channel_id=1, source_target_pairs={{0,8},{1,9},{2,10},{3,11},{4,12},{5,13},{6,14},{7,15},{8,0},{9,1},... | collective-permute-start | bytes 1474568 | tf_op jit(solution)/shard_map/ppermute | solution.py:661
  103.6 0.8 split.1
  105.2 1.3 collective-permute-start.31
  106.5 17.6 %collective-permute-done.27.refs_1_ = bf16[320,768]{1,0:T(8,128)(2,1)S(1)} collective-permute-done((bf16[320,768]{1,0:T(8,128)(2,1)S(1)}, bf16[320,768]{1,0:T(8,128)(2,1)S(1)}, u32[]{:S(2)}, u32[]{:S(2)}) %collective-permute-start.27) | collective-permute-done | bytes 491552 | tf_op jit(solution)/shard_map/ppermute | solution.py:661
  124.3 1.1 collective-permute-done.28.refs_2_
  127.1 1.0 collective-permute-start.40
  128.1 1.0 collective-permute-start.41
  129.1 5.1 %combine.1 = (bf16[512,384]{1,0:T(8,128)(2,1)}, f32[512,384]{1,0:T(8,128)S(1)}, bf16[512,384]{1,0:T(8,128)(2,1)S(1)}, bf16[384,512]{1,0:T(8,128)(2,1)S(1)}) custom-call(f32[512,384]{1,0:T(8,128)S(1)} %get-tuple-element.144.middle, bf16[512,384]{1,0:T(8,128)(2,1)S(1)} %get-tuple-element.145.normed_two, f32[512,128]{1,0:T(8,128)S(1)} %get-tuple-element.146.probs, ...), custom_call_target="tpu_custom_call" | custom-call | flops 1509949440 | bytes 1024 | tf_op jit(solution)/shard_map/combine/pallas_call | solution.py:40
  134.2 8.5 %backward.1 = (bf16[512,384]{1,0:T(8,128)(2,1)S(1)}, bf16[256,768]{1,0:T(8,128)(2,1)S(1)}, bf16[256,768]{1,0:T(8,128)(2,1)S(1)}, f32[512,768]{1,0:T(8,128)S(1)},...) custom-call(bf16[1024,1152]{1,0:T(8,128)(2,1)S(1)} %get-tuple-element.197.qkv, ...), custom_call_target="tpu_custom_call" | custom-call | bytes 1024 | tf_op jit(solution)/shard_map/backward/pallas_call | solution.py:40
  143.3 2.0 %collective-permute-start.36 = (bf16[256,768]{1,0:T(8,128)(2,1)S(1)}, bf16[256,768]{1,0:T(8,128)(2,1)S(1)}, u32[]{:S(2)}, u32[]{:S(2)}) collective-permute-start(bf16[256,768]{1,0:T(8,128)(2,1)S(1)} %get-tuple-element.204), channel_id=1, source_target_pairs={{0,1},{1,2},{2,3},{3,4},{4,5},{5,6},{6,7},{7,8},{8,9},{9,10},{10,1... | collective-permute-start | bytes 1179656 | tf_op jit(solution)/shard_map/ppermute | solution.py:944
  145.3 1.3 collective-permute-start.37
  146.7 8.0 %collective-permute-done.42.refs_8_ = bf16[768,384]{1,0:T(8,128)(2,1)S(1)} collective-permute-done((bf16[768,384]{1,0:T(8,128)(2,1)S(1)}, bf16[768,384]{1,0:T(8,128)(2,1)S(1)}, u32[]{:S(2)}, u32[]{:S(2)}) %collective-permute-start.42) | collective-permute-done | bytes 589856 | tf_op jit(solution)/shard_map/ppermute | solution.py:661
  154.7 0.8 collective-permute-start.43
  155.5 1.3 collective-permute-start.44
  156.9 1.4 collective-permute-start.45
  158.3 3.5 %collective-permute-done.43.refs_0_ = bf16[48,1664]{1,0:T(8,128)(2,1)S(1)} collective-permute-done((bf16[48,1664]{1,0:T(8,128)(2,1)S(1)}, bf16[48,1664]{1,0:T(8,128)(2,1)S(1)}, u32[]{:S(2)}, u32[]{:S(2)}) %collective-permute-start.43) | collective-permute-done | bytes 159776 | tf_op jit(solution)/shard_map/ppermute | solution.py:661
  162.3 2.4 %collective-permute-done.45.refs_2_ = bf16[48,1664]{1,0:T(8,128)(2,1)S(1)} collective-permute-done((bf16[48,1664]{1,0:T(8,128)(2,1)S(1)}, bf16[48,1664]{1,0:T(8,128)(2,1)S(1)}, u32[]{:S(2)}, u32[]{:S(2)}) %collective-permute-start.45) | collective-permute-done | bytes 159776 | tf_op jit(solution)/shard_map/ppermute | solution.py:661
  164.8 2.5 %collective-permute-start.46 = (bf16[12,1664]{1,0:T(8,128)(2,1)S(1)}, bf16[12,1664]{1,0:T(8,128)(2,1)S(1)}, u32[]{:S(2)}, u32[]{:S(2)}) collective-permute-start(bf16[12,1664]{1,0:T(8,128)(2,1)S(1)} %get-tuple-element.223), channel_id=1, source_target_pairs={{0,8},{1,9},{2,10},{3,11},{4,12},{5,13},{6,14},{7,15},{8,0},{9,1},... | collective-permute-start | bytes 119816 | tf_op jit(solution)/shard_map/ppermute | solution.py:661
  167.3 2.6 %collective-permute-start.47 = (bf16[12,1664]{1,0:T(8,128)(2,1)S(1)}, bf16[12,1664]{1,0:T(8,128)(2,1)S(1)}, u32[]{:S(2)}, u32[]{:S(2)}) collective-permute-start(bf16[12,1664]{1,0:T(8,128)(2,1)S(1)} %get-tuple-element.224), channel_id=1, source_target_pairs={{0,16},{1,17},{2,18},{3,19},{4,20},{5,21},{6,22},{7,23},{8,24},{9,... | collective-permute-start | bytes 119816 | tf_op jit(solution)/shard_map/ppermute | solution.py:661
  170.5 2.4 %finish.1 = bf16[512,384]{1,0:T(8,128)(2,1)} custom-call(bf16[512,384]{1,0:T(8,128)(2,1)S(1)} %get-tuple-element.202.dq, f32[512,768]{1,0:T(8,128)S(1)} %get-tuple-element.203.inner, bf16[256,768]{1,0:T(8,128)(2,1)S(1)} %collective-permute-done.36.from_low, bf16[256,768]{1,0:T(8,128)(2,1)S(1)} %collective-permute-done.37.from_high, ...), custom_call_target="tpu_custom_call" | custom-call | flops 754974720 | bytes 1024 | tf_op jit(solution)/shard_map/finish/pallas_call | solution.py:40
  173.3 2.6 %collective-permute-done.48.refs_2_ = bf16[12,1664]{1,0:T(8,128)(2,1)S(1)} collective-permute-done((bf16[12,1664]{1,0:T(8,128)(2,1)S(1)}, bf16[12,1664]{1,0:T(8,128)(2,1)S(1)}, u32[]{:S(2)}, u32[]{:S(2)}) %collective-permute-start.48) | collective-permute-done | bytes 39968 | tf_op jit(solution)/shard_map/ppermute | solution.py:661
  175.9 1.2 final.1
  (83 shorter events, 14.4 us)
Async XLA Ops:
  1.7 11.1 %collective-permute-start.2 = (bf16[384,384]{1,0:T(8,128)(2,1)}, bf16[384,384]{1,0:T(8,128)(2,1)S(1)}, u32[]{:S(2)}, u32[]{:S(2)}) collective-permute-start(bf16[384,384]{1,0:T(8,128)(2,1)} %bitcast.15), channel_id=1, source_target_pairs={{0,2},{1,3},{2,0},{3,1},{4,6},{5,7},{6,4},{7,5},{8,10},{9,11},{10,... | collective-permute-start | bytes 884744 | tf_op jit(solution)/shard_map/ppermute | solution.py:661
  4.7 16.8 %collective-permute-start.8 = (bf16[384,384]{1,0:T(8,128)(2,1)}, bf16[384,384]{1,0:T(8,128)(2,1)S(1)}, u32[]{:S(2)}, u32[]{:S(2)}) collective-permute-start(bf16[384,384]{1,0:T(8,128)(2,1)} %bitcast.16), channel_id=1, source_target_pairs={{0,2},{1,3},{2,0},{3,1},{4,6},{5,7},{6,4},{7,5},{8,10},{9,11},{10,... | collective-permute-start | bytes 884744 | tf_op jit(solution)/shard_map/ppermute | solution.py:661
  4.8 5.7 %collective-permute-start = (bf16[12,1664]{1,0:T(8,128)(2,1)S(1)}, bf16[12,1664]{1,0:T(8,128)(2,1)S(1)}, u32[]{:S(2)}, u32[]{:S(2)}) collective-permute-start(bf16[12,1664]{1,0:T(8,128)(2,1)S(1)} %pack.1.refs_0_), channel_id=1, source_target_pairs={{0,8},{1,9},{2,10},{3,11},{4,12},{5,13},{6,14},{7,15},{8,0},{9,1},... | collective-permute-start | bytes 119816 | tf_op jit(solution)/shard_map/ppermute | solution.py:661
  6.8 5.6 %collective-permute-start.1 = (bf16[12,1664]{1,0:T(8,128)(2,1)S(1)}, bf16[12,1664]{1,0:T(8,128)(2,1)S(1)}, u32[]{:S(2)}, u32[]{:S(2)}) collective-permute-start(bf16[12,1664]{1,0:T(8,128)(2,1)S(1)} %pack.1.refs_0_), channel_id=1, source_target_pairs={{0,16},{1,17},{2,18},{3,19},{4,20},{5,21},{6,22},{7,23},{8,24},{9,... | collective-permute-start | bytes 119816 | tf_op jit(solution)/shard_map/ppermute | solution.py:661
  9.4 5.9 %collective-permute-start.5 = (bf16[12,1664]{1,0:T(8,128)(2,1)S(1)}, bf16[12,1664]{1,0:T(8,128)(2,1)S(1)}, u32[]{:S(2)}, u32[]{:S(2)}) collective-permute-start(bf16[12,1664]{1,0:T(8,128)(2,1)S(1)} %pack.1.refs_0_), channel_id=1, source_target_pairs={{0,24},{1,25},{2,26},{3,27},{4,28},{5,29},{6,30},{7,31},{8,16},{9,... | collective-permute-start | bytes 119816 | tf_op jit(solution)/shard_map/ppermute | solution.py:661
  15.4 7.4 %collective-permute-start.7 = (bf16[48,1664]{1,0:T(8,128)(2,1)S(1)}, bf16[48,1664]{1,0:T(8,128)(2,1)S(1)}, u32[]{:S(2)}, u32[]{:S(2)}) collective-permute-start(bf16[48,1664]{1,0:T(8,128)(2,1)S(1)} %join.2.refs_0_), channel_id=1, source_target_pairs={{0,4},{1,5},{2,6},{3,7},{4,0},{5,1},{6,2},{7,3},{8,12},{9,13},{10,... | collective-permute-start | bytes 479240 | tf_op jit(solution)/shard_map/ppermute | solution.py:661
  17.0 7.6 %collective-permute-start.9 = (bf16[48,1664]{1,0:T(8,128)(2,1)S(1)}, bf16[48,1664]{1,0:T(8,128)(2,1)S(1)}, u32[]{:S(2)}, u32[]{:S(2)}) collective-permute-start(bf16[48,1664]{1,0:T(8,128)(2,1)S(1)} %join.2.refs_0_), channel_id=1, source_target_pairs={{0,6},{1,7},{2,4},{3,5},{4,2},{5,3},{6,0},{7,1},{8,14},{9,15},{10,... | collective-permute-start | bytes 479240 | tf_op jit(solution)/shard_map/ppermute | solution.py:661
  18.4 6.7 %collective-permute-start.6 = (bf16[48,1664]{1,0:T(8,128)(2,1)S(1)}, bf16[48,1664]{1,0:T(8,128)(2,1)S(1)}, u32[]{:S(2)}, u32[]{:S(2)}) collective-permute-start(bf16[48,1664]{1,0:T(8,128)(2,1)S(1)} %join.2.refs_0_), channel_id=1, source_target_pairs={{0,2},{1,3},{2,0},{3,1},{4,6},{5,7},{6,4},{7,5},{8,10},{9,11},{10,... | collective-permute-start | bytes 479240 | tf_op jit(solution)/shard_map/ppermute | solution.py:661
  20.1 5.7 %collective-permute-start.3 = (bf16[256,512]{1,0:T(8,128)(2,1)S(1)}, bf16[256,512]{1,0:T(8,128)(2,1)S(1)}, u32[]{:S(2)}, u32[]{:S(2)}) collective-permute-start(bf16[256,512]{1,0:T(8,128)(2,1)S(1)} %get-tuple-element.128), channel_id=1, source_target_pairs={{0,1},{1,2},{2,3},{3,4},{4,5},{5,6},{6,7},{7,8},{8,9},{9,10},{10,1... | collective-permute-start | bytes 786440 | tf_op jit(solution)/shard_map/ppermute | solution.py:745
  21.5 5.1 %collective-permute-start.4 = (bf16[256,512]{1,0:T(8,128)(2,1)S(1)}, bf16[256,512]{1,0:T(8,128)(2,1)S(1)}, u32[]{:S(2)}, u32[]{:S(2)}) collective-permute-start(bf16[256,512]{1,0:T(8,128)(2,1)S(1)} %get-tuple-element.129), channel_id=1, source_target_pairs={{1,0},{2,1},{3,2},{4,3},{5,4},{6,5},{7,6},{8,7},{9,8},{10,9},{11,1... | collective-permute-start | bytes 786440 | tf_op jit(solution)/shard_map/ppermute | solution.py:746
  25.1 8.5 %collective-permute-start.10 = (bf16[96,1664]{1,0:T(8,128)(2,1)S(1)}, bf16[96,1664]{1,0:T(8,128)(2,1)S(1)}, u32[]{:S(2)}, u32[]{:S(2)}) collective-permute-start(bf16[96,1664]{1,0:T(8,128)(2,1)S(1)} %get-tuple-element.142.near_one), channel_id=1, source_target_pairs={{0,1},{1,0},{2,3},{3,2},{4,5},{5,4},{6,7},{7,6},{8,9},{9,8},{10,11... | collective-permute-start | bytes 958472 | tf_op jit(solution)/shard_map/ppermute | solution.py:661
  25.8 7.9 %collective-permute-start.11 = (bf16[96,1664]{1,0:T(8,128)(2,1)S(1)}, bf16[96,1664]{1,0:T(8,128)(2,1)S(1)}, u32[]{:S(2)}, u32[]{:S(2)}) collective-permute-start(bf16[96,1664]{1,0:T(8,128)(2,1)S(1)} %get-tuple-element.143.near_two), channel_id=1, source_target_pairs={{0,1},{1,0},{2,3},{3,2},{4,5},{5,4},{6,7},{7,6},{8,9},{9,8},{10,11... | collective-permute-start | bytes 958472 | tf_op jit(solution)/shard_map/ppermute | solution.py:661
  26.6 30.8 %collective-permute-start.12 = (bf16[768,384]{1,0:T(8,128)(2,1)S(1)}, bf16[768,384]{1,0:T(8,128)(2,1)S(1)}, u32[]{:S(2)}, u32[]{:S(2)}) collective-permute-start(bf16[768,384]{1,0:T(8,128)(2,1)S(1)} %quarter.1.near_one), channel_id=1, source_target_pairs={{0,16},{1,17},{2,18},{3,19},{4,20},{5,21},{6,22},{7,23},{8,24},{9,... | collective-permute-start | bytes 1769480 | tf_op jit(solution)/shard_map/ppermute | solution.py:661
  41.2 2.4 %collective-permute-start.13 = (bf16[160,768]{1,0:T(8,128)(2,1)S(1)}, bf16[160,768]{1,0:T(8,128)(2,1)S(1)}, u32[]{:S(2)}, u32[]{:S(2)}) collective-permute-start(bf16[160,768]{1,0:T(8,128)(2,1)S(1)} %get-tuple-element.151), channel_id=1, source_target_pairs={{0,1},{1,0},{2,3},{3,2},{4,5},{5,4},{6,7},{7,6},{8,9},{9,8},{10,11... | collective-permute-start | bytes 737288 | tf_op jit(solution)/shard_map/ppermute | solution.py:661
  42.5 1.8 %collective-permute-start.15 = (bf16[160,768]{1,0:T(8,128)(2,1)S(1)}, bf16[160,768]{1,0:T(8,128)(2,1)S(1)}, u32[]{:S(2)}, u32[]{:S(2)}) collective-permute-start(bf16[160,768]{1,0:T(8,128)(2,1)S(1)} %get-tuple-element.153), channel_id=1, source_target_pairs={{0,1},{1,0},{2,3},{3,2},{4,5},{5,4},{6,7},{7,6},{8,9},{9,8},{10,11... | collective-permute-start | bytes 737288 | tf_op jit(solution)/shard_map/ppermute | solution.py:661
  43.0 1.7 collective-permute-start.16
  44.8 23.6 %collective-permute-start.18 = (bf16[320,768]{1,0:T(8,128)(2,1)S(1)}, bf16[320,768]{1,0:T(8,128)(2,1)S(1)}, u32[]{:S(2)}, u32[]{:S(2)}) collective-permute-start(bf16[320,768]{1,0:T(8,128)(2,1)S(1)} %get-tuple-element.159), channel_id=1, source_target_pairs={{0,4},{1,5},{2,6},{3,7},{4,0},{5,1},{6,2},{7,3},{8,12},{9,13},{10,... | collective-permute-start | bytes 1474568 | tf_op jit(solution)/shard_map/ppermute | solution.py:661
  46.3 23.1 %collective-permute-start.19 = (bf16[320,768]{1,0:T(8,128)(2,1)S(1)}, bf16[320,768]{1,0:T(8,128)(2,1)S(1)}, u32[]{:S(2)}, u32[]{:S(2)}) collective-permute-start(bf16[320,768]{1,0:T(8,128)(2,1)S(1)} %get-tuple-element.160), channel_id=1, source_target_pairs={{0,8},{1,9},{2,10},{3,11},{4,12},{5,13},{6,14},{7,15},{8,0},{9,1},... | collective-permute-start | bytes 1474568 | tf_op jit(solution)/shard_map/ppermute | solution.py:661
  47.9 34.2 %collective-permute-start.20 = (bf16[320,768]{1,0:T(8,128)(2,1)S(1)}, bf16[320,768]{1,0:T(8,128)(2,1)S(1)}, u32[]{:S(2)}, u32[]{:S(2)}) collective-permute-start(bf16[320,768]{1,0:T(8,128)(2,1)S(1)} %get-tuple-element.161), channel_id=1, source_target_pairs={{0,12},{1,13},{2,14},{3,15},{4,8},{5,9},{6,10},{7,11},{8,4},{9,5},... | collective-permute-start | bytes 1474568 | tf_op jit(solution)/shard_map/ppermute | solution.py:661
  57.5 10.9 %collective-permute-start.17 = (bf16[384,384]{1,0:T(8,128)(2,1)S(1)}, bf16[384,384]{1,0:T(8,128)(2,1)S(1)}, u32[]{:S(2)}, u32[]{:S(2)}) collective-permute-start(bf16[384,384]{1,0:T(8,128)(2,1)S(1)} %get-tuple-element.158.refs_1_), channel_id=1, source_target_pairs={{0,2},{1,3},{2,0},{3,1},{4,6},{5,7},{6,4},{7,5},{8,10},{9,11},{10,... | collective-permute-start | bytes 884744 | tf_op jit(solution)/shard_map/ppermute | solution.py:661
  60.5 21.6 %collective-permute-start.21 = (bf16[384,384]{1,0:T(8,128)(2,1)S(1)}, bf16[384,384]{1,0:T(8,128)(2,1)S(1)}, u32[]{:S(2)}, u32[]{:S(2)}) collective-permute-start(bf16[384,384]{1,0:T(8,128)(2,1)S(1)} %get-tuple-element.167.refs_0_), channel_id=1, source_target_pairs={{0,2},{1,3},{2,0},{3,1},{4,6},{5,7},{6,4},{7,5},{8,10},{9,11},{10,... | collective-permute-start | bytes 884744 | tf_op jit(solution)/shard_map/ppermute | solution.py:661
  82.5 1.6 collective-permute-start.22
  82.6 2.0 %collective-permute-start.23 = (bf16[384,384]{1,0:T(8,128)(2,1)S(1)}, bf16[384,384]{1,0:T(8,128)(2,1)S(1)}, u32[]{:S(2)}, u32[]{:S(2)}) collective-permute-start(bf16[384,384]{1,0:T(8,128)(2,1)S(1)} %get-tuple-element.171), channel_id=1, source_target_pairs={{0,1},{1,0},{2,3},{3,2},{4,5},{5,4},{6,7},{7,6},{8,9},{9,8},{10,11... | collective-permute-start | bytes 884744 | tf_op jit(solution)/shard_map/ppermute | solution.py:661
  83.1 1.9 %collective-permute-start.24 = (bf16[384,384]{1,0:T(8,128)(2,1)S(1)}, bf16[384,384]{1,0:T(8,128)(2,1)S(1)}, u32[]{:S(2)}, u32[]{:S(2)}) collective-permute-start(bf16[384,384]{1,0:T(8,128)(2,1)S(1)} %get-tuple-element.172), channel_id=1, source_target_pairs={{0,1},{1,0},{2,3},{3,2},{4,5},{5,4},{6,7},{7,6},{8,9},{9,8},{10,11... | collective-permute-start | bytes 884744 | tf_op jit(solution)/shard_map/ppermute | solution.py:661
  83.2 2.3 %collective-permute-start.25 = (bf16[384,384]{1,0:T(8,128)(2,1)S(1)}, bf16[384,384]{1,0:T(8,128)(2,1)S(1)}, u32[]{:S(2)}, u32[]{:S(2)}) collective-permute-start(bf16[384,384]{1,0:T(8,128)(2,1)S(1)} %get-tuple-element.173), channel_id=1, source_target_pairs={{0,1},{1,0},{2,3},{3,2},{4,5},{5,4},{6,7},{7,6},{8,9},{9,8},{10,11... | collective-permute-start | bytes 884744 | tf_op jit(solution)/shard_map/ppermute | solution.py:661
  99.9 3.7 %collective-permute-start.26 = (bf16[1536,384]{1,0:T(8,128)(2,1)S(1)}, bf16[1536,384]{1,0:T(8,128)(2,1)S(1)}, u32[]{:S(2)}, u32[]{:S(2)}) collective-permute-start(bf16[1536,384]{1,0:T(8,128)(2,1)S(1)} %get-tuple-element.178), channel_id=1, source_target_pairs={{0,1},{1,0},{2,3},{3,2},{4,5},{5,4},{6,7},{7,6},{8,9},{9,8},{10,11... | collective-permute-start | bytes 3538952 | tf_op jit(solution)/shard_map/ppermute | solution.py:661
  100.1 24.0 %collective-permute-start.27 = (bf16[320,768]{1,0:T(8,128)(2,1)S(1)}, bf16[320,768]{1,0:T(8,128)(2,1)S(1)}, u32[]{:S(2)}, u32[]{:S(2)}) collective-permute-start(bf16[320,768]{1,0:T(8,128)(2,1)S(1)} %get-tuple-element.183), channel_id=1, source_target_pairs={{0,4},{1,5},{2,6},{3,7},{4,0},{5,1},{6,2},{7,3},{8,12},{9,13},{10,... | collective-permute-start | bytes 1474568 | tf_op jit(solution)/shard_map/ppermute | solution.py:661
  100.1 24.2 %collective-permute-start.29 = (bf16[320,768]{1,0:T(8,128)(2,1)S(1)}, bf16[320,768]{1,0:T(8,128)(2,1)S(1)}, u32[]{:S(2)}, u32[]{:S(2)}) collective-permute-start(bf16[320,768]{1,0:T(8,128)(2,1)S(1)} %get-tuple-element.186), channel_id=1, source_target_pairs={{0,12},{1,13},{2,14},{3,15},{4,8},{5,9},{6,10},{7,11},{8,4},{9,5},... | collective-permute-start | bytes 1474568 | tf_op jit(solution)/shard_map/ppermute | solution.py:661
  100.1 25.2 %collective-permute-start.28 = (bf16[320,768]{1,0:T(8,128)(2,1)S(1)}, bf16[320,768]{1,0:T(8,128)(2,1)S(1)}, u32[]{:S(2)}, u32[]{:S(2)}) collective-permute-start(bf16[320,768]{1,0:T(8,128)(2,1)S(1)} %get-tuple-element.185), channel_id=1, source_target_pairs={{0,8},{1,9},{2,10},{3,11},{4,12},{5,13},{6,14},{7,15},{8,0},{9,1},... | collective-permute-start | bytes 1474568 | tf_op jit(solution)/shard_map/ppermute | solution.py:661
  104.4 19.7 %collective-permute-start.30 = (bf16[384,384]{1,0:T(8,128)(2,1)S(1)}, bf16[384,384]{1,0:T(8,128)(2,1)S(1)}, u32[]{:S(2)}, u32[]{:S(2)}) collective-permute-start(bf16[384,384]{1,0:T(8,128)(2,1)S(1)} %get-tuple-element.188), channel_id=1, source_target_pairs={{0,2},{1,3},{2,0},{3,1},{4,6},{5,7},{6,4},{7,5},{8,10},{9,11},{10,... | collective-permute-start | bytes 884744 | tf_op jit(solution)/shard_map/ppermute | solution.py:661
  105.2 19.0 %collective-permute-start.31 = (bf16[384,384]{1,0:T(8,128)(2,1)S(1)}, bf16[384,384]{1,0:T(8,128)(2,1)S(1)}, u32[]{:S(2)}, u32[]{:S(2)}) collective-permute-start(bf16[384,384]{1,0:T(8,128)(2,1)S(1)} %get-tuple-element.189), channel_id=1, source_target_pairs={{0,2},{1,3},{2,0},{3,1},{4,6},{5,7},{6,4},{7,5},{8,10},{9,11},{10,... | collective-permute-start | bytes 884744 | tf_op jit(solution)/shard_map/ppermute | solution.py:661
  125.5 1.6 collective-permute-start.32
  125.6 2.5 %collective-permute-start.33 = (bf16[160,768]{1,0:T(8,128)(2,1)S(1)}, bf16[160,768]{1,0:T(8,128)(2,1)S(1)}, u32[]{:S(2)}, u32[]{:S(2)}) collective-permute-start(bf16[160,768]{1,0:T(8,128)(2,1)S(1)} %get-tuple-element.193), channel_id=1, source_target_pairs={{0,1},{1,0},{2,3},{3,2},{4,5},{5,4},{6,7},{7,6},{8,9},{9,8},{10,11... | collective-permute-start | bytes 737288 | tf_op jit(solution)/shard_map/ppermute | solution.py:661
  126.1 3.0 %collective-permute-start.34 = (bf16[160,768]{1,0:T(8,128)(2,1)S(1)}, bf16[160,768]{1,0:T(8,128)(2,1)S(1)}, u32[]{:S(2)}, u32[]{:S(2)}) collective-permute-start(bf16[160,768]{1,0:T(8,128)(2,1)S(1)} %get-tuple-element.194), channel_id=1, source_target_pairs={{0,1},{1,0},{2,3},{3,2},{4,5},{5,4},{6,7},{7,6},{8,9},{9,8},{10,11... | collective-permute-start | bytes 737288 | tf_op jit(solution)/shard_map/ppermute | solution.py:661
  126.1 3.0 %collective-permute-start.35 = (bf16[160,768]{1,0:T(8,128)(2,1)S(1)}, bf16[160,768]{1,0:T(8,128)(2,1)S(1)}, u32[]{:S(2)}, u32[]{:S(2)}) collective-permute-start(bf16[160,768]{1,0:T(8,128)(2,1)S(1)} %get-tuple-element.195), channel_id=1, source_target_pairs={{0,1},{1,0},{2,3},{3,2},{4,5},{5,4},{6,7},{7,6},{8,9},{9,8},{10,11... | collective-permute-start | bytes 737288 | tf_op jit(solution)/shard_map/ppermute | solution.py:661
  126.6 28.0 %collective-permute-start.42 = (bf16[768,384]{1,0:T(8,128)(2,1)S(1)}, bf16[768,384]{1,0:T(8,128)(2,1)S(1)}, u32[]{:S(2)}, u32[]{:S(2)}) collective-permute-start(bf16[768,384]{1,0:T(8,128)(2,1)S(1)} %away.1), channel_id=1, source_target_pairs={{0,16},{1,17},{2,18},{3,19},{4,20},{5,21},{6,22},{7,23},{8,24},{9,... | collective-permute-start | bytes 1769480 | tf_op jit(solution)/shard_map/ppermute | solution.py:661
  127.1 16.3 %collective-permute-start.40 = (bf16[384,384]{1,0:T(8,128)(2,1)S(1)}, bf16[384,384]{1,0:T(8,128)(2,1)S(1)}, u32[]{:S(2)}, u32[]{:S(2)}) collective-permute-start(bf16[384,384]{1,0:T(8,128)(2,1)S(1)} %get-tuple-element.213), channel_id=1, source_target_pairs={{0,2},{1,3},{2,0},{3,1},{4,6},{5,7},{6,4},{7,5},{8,10},{9,11},{10,... | collective-permute-start | bytes 884744 | tf_op jit(solution)/shard_map/ppermute | solution.py:661
  128.1 17.3 %collective-permute-start.41 = (bf16[384,384]{1,0:T(8,128)(2,1)S(1)}, bf16[384,384]{1,0:T(8,128)(2,1)S(1)}, u32[]{:S(2)}, u32[]{:S(2)}) collective-permute-start(bf16[384,384]{1,0:T(8,128)(2,1)S(1)} %get-tuple-element.214), channel_id=1, source_target_pairs={{0,2},{1,3},{2,0},{3,1},{4,6},{5,7},{6,4},{7,5},{8,10},{9,11},{10,... | collective-permute-start | bytes 884744 | tf_op jit(solution)/shard_map/ppermute | solution.py:661
  142.8 3.9 %collective-permute-start.38 = (bf16[96,1664]{1,0:T(8,128)(2,1)S(1)}, bf16[96,1664]{1,0:T(8,128)(2,1)S(1)}, u32[]{:S(2)}, u32[]{:S(2)}) collective-permute-start(bf16[96,1664]{1,0:T(8,128)(2,1)S(1)} %get-tuple-element.210), channel_id=1, source_target_pairs={{0,1},{1,0},{2,3},{3,2},{4,5},{5,4},{6,7},{7,6},{8,9},{9,8},{10,11... | collective-permute-start | bytes 958472 | tf_op jit(solution)/shard_map/ppermute | solution.py:661
  142.8 3.8 %collective-permute-start.39 = (bf16[96,1664]{1,0:T(8,128)(2,1)S(1)}, bf16[96,1664]{1,0:T(8,128)(2,1)S(1)}, u32[]{:S(2)}, u32[]{:S(2)}) collective-permute-start(bf16[96,1664]{1,0:T(8,128)(2,1)S(1)} %get-tuple-element.211), channel_id=1, source_target_pairs={{0,1},{1,0},{2,3},{3,2},{4,5},{5,4},{6,7},{7,6},{8,9},{9,8},{10,11... | collective-permute-start | bytes 958472 | tf_op jit(solution)/shard_map/ppermute | solution.py:661
  143.3 27.1 %collective-permute-start.36 = (bf16[256,768]{1,0:T(8,128)(2,1)S(1)}, bf16[256,768]{1,0:T(8,128)(2,1)S(1)}, u32[]{:S(2)}, u32[]{:S(2)}) collective-permute-start(bf16[256,768]{1,0:T(8,128)(2,1)S(1)} %get-tuple-element.204), channel_id=1, source_target_pairs={{0,1},{1,2},{2,3},{3,4},{4,5},{5,6},{6,7},{7,8},{8,9},{9,10},{10,1... | collective-permute-start | bytes 1179656 | tf_op jit(solution)/shard_map/ppermute | solution.py:944
  145.3 25.1 %collective-permute-start.37 = (bf16[256,768]{1,0:T(8,128)(2,1)S(1)}, bf16[256,768]{1,0:T(8,128)(2,1)S(1)}, u32[]{:S(2)}, u32[]{:S(2)}) collective-permute-start(bf16[256,768]{1,0:T(8,128)(2,1)S(1)} %get-tuple-element.205), channel_id=1, source_target_pairs={{1,0},{2,1},{3,2},{4,3},{5,4},{6,5},{7,6},{8,7},{9,8},{10,9},{11,1... | collective-permute-start | bytes 1179656 | tf_op jit(solution)/shard_map/ppermute | solution.py:943
  154.7 7.0 %collective-permute-start.43 = (bf16[48,1664]{1,0:T(8,128)(2,1)S(1)}, bf16[48,1664]{1,0:T(8,128)(2,1)S(1)}, u32[]{:S(2)}, u32[]{:S(2)}) collective-permute-start(bf16[48,1664]{1,0:T(8,128)(2,1)S(1)} %get-tuple-element.219), channel_id=1, source_target_pairs={{0,2},{1,3},{2,0},{3,1},{4,6},{5,7},{6,4},{7,5},{8,10},{9,11},{10,... | collective-permute-start | bytes 479240 | tf_op jit(solution)/shard_map/ppermute | solution.py:661
  155.5 6.8 %collective-permute-start.44 = (bf16[48,1664]{1,0:T(8,128)(2,1)S(1)}, bf16[48,1664]{1,0:T(8,128)(2,1)S(1)}, u32[]{:S(2)}, u32[]{:S(2)}) collective-permute-start(bf16[48,1664]{1,0:T(8,128)(2,1)S(1)} %get-tuple-element.220), channel_id=1, source_target_pairs={{0,4},{1,5},{2,6},{3,7},{4,0},{5,1},{6,2},{7,3},{8,12},{9,13},{10,... | collective-permute-start | bytes 479240 | tf_op jit(solution)/shard_map/ppermute | solution.py:661
  156.9 7.9 %collective-permute-start.45 = (bf16[48,1664]{1,0:T(8,128)(2,1)S(1)}, bf16[48,1664]{1,0:T(8,128)(2,1)S(1)}, u32[]{:S(2)}, u32[]{:S(2)}) collective-permute-start(bf16[48,1664]{1,0:T(8,128)(2,1)S(1)} %get-tuple-element.221), channel_id=1, source_target_pairs={{0,6},{1,7},{2,4},{3,5},{4,2},{5,3},{6,0},{7,1},{8,14},{9,15},{10,... | collective-permute-start | bytes 479240 | tf_op jit(solution)/shard_map/ppermute | solution.py:661
  164.8 8.1 %collective-permute-start.46 = (bf16[12,1664]{1,0:T(8,128)(2,1)S(1)}, bf16[12,1664]{1,0:T(8,128)(2,1)S(1)}, u32[]{:S(2)}, u32[]{:S(2)}) collective-permute-start(bf16[12,1664]{1,0:T(8,128)(2,1)S(1)} %get-tuple-element.223), channel_id=1, source_target_pairs={{0,8},{1,9},{2,10},{3,11},{4,12},{5,13},{6,14},{7,15},{8,0},{9,1},... | collective-permute-start | bytes 119816 | tf_op jit(solution)/shard_map/ppermute | solution.py:661
  167.3 6.0 %collective-permute-start.47 = (bf16[12,1664]{1,0:T(8,128)(2,1)S(1)}, bf16[12,1664]{1,0:T(8,128)(2,1)S(1)}, u32[]{:S(2)}, u32[]{:S(2)}) collective-permute-start(bf16[12,1664]{1,0:T(8,128)(2,1)S(1)} %get-tuple-element.224), channel_id=1, source_target_pairs={{0,16},{1,17},{2,18},{3,19},{4,20},{5,21},{6,22},{7,23},{8,24},{9,... | collective-permute-start | bytes 119816 | tf_op jit(solution)/shard_map/ppermute | solution.py:661
  169.9 5.9 %collective-permute-start.48 = (bf16[12,1664]{1,0:T(8,128)(2,1)S(1)}, bf16[12,1664]{1,0:T(8,128)(2,1)S(1)}, u32[]{:S(2)}, u32[]{:S(2)}) collective-permute-start(bf16[12,1664]{1,0:T(8,128)(2,1)S(1)} %get-tuple-element.225), channel_id=1, source_target_pairs={{0,24},{1,25},{2,26},{3,27},{4,28},{5,29},{6,30},{7,31},{8,16},{9,... | collective-permute-start | bytes 119816 | tf_op jit(solution)/shard_map/ppermute | solution.py:661
  (7 other events, 135.2 us)
